TPU v7x, 256 devices: a whole 4x4x8 slice. The times are simulated.
256 devices in a mesh: tile: 4 (over y), proj: 16 (over x, z_hi, core), cuts: 4 (over z_lo).
Axes of the slice: x: 4, y: 4, z: 8 (z_hi: 2, z_lo: 4; z = z_hi * 4 + z_lo), core: 2. Of those that a mesh axis runs over, the one named last changes fastest.
Arguments:
- object_field: float32 [64, 2, 384, 2048], P(('proj', 'cuts'), None, None, 'tile'), may hold values from -5 to 5
- probe_field: float32 [2, 256, 256], replicated, may hold values from -6 to 6
- amplitudes: bfloat16 [64, 4, 6, 256, 256], P(('proj', 'cuts'), 'tile'), may hold values from 0 to 16
- pos_rows: int32 [64, 4, 6], P(('proj', 'cuts'), 'tile'), may hold values from 0 to 128
- pos_cols: int32 [64, 4, 6], P(('proj', 'cuts'), 'tile'), may hold values from 0 to 512
- counts: int32 [64, 4], P(('proj', 'cuts'), 'tile'), may hold values from 1 to 6, as said below
- admm_dual: float32 [64, 32, 2048], P(('proj', 'cuts'), None, 'tile'), may hold values from -4 to 4
- volume: float32 [32, 2048, 2048], P('cuts', ('tile', 'proj')), may hold values from -6 to 6
- proj_weights: bfloat16 [16, 2048, 2048], P(None, ('tile', 'proj')), may hold values from -0.125 to 0.125
- ray_weights: float32 [16, 2048], replicated, may hold values from -0.125 to 0.125
- angle_ids: int32 [64], replicated, may hold values from 0 to 15
Outputs:
- new_object: float32 [64, 2, 384, 2048], P(('proj', 'cuts'), None, None, 'tile')
- new_probe: float32 [2, 256, 256], replicated
- new_volume: float32 [32, 2048, 2048], P('cuts', ('tile', 'proj'))
Inputs may be any that keep to these rules, and one draw needn't show every extreme that they name: `counts`: every tile holds at least one live position and at most 6; exactly one tile of one projection holds 6, every other holds at most 3.
All inputs are finite; a program needn't handle non-finite values.
Results may differ from a plain program's by a relative error of at most 0.00095.
The roundings to bfloat16 on the way count: a program that leaves them out, or rounds other values in their place, can miss the bound.
Values may be sent and summed in bfloat16 or wider, within the bound.
A program may use at most 64 MiB of HBM per device.

v0:
```python
import math

import jax
import jax.numpy as jnp
from jax import lax
from jax.experimental import pallas as pl
from jax.experimental.pallas import tpu as pltpu
from jax.sharding import PartitionSpec as P

PB = 256


tomo_step = 1.0


def shifted(value, axis, steps):
    count = lax.axis_size(axis)
    leading, last = (max(0, -steps), min(count, count - steps))
    return lax.ppermute(value, axis, [(source, source + steps) for source in range(leading, last)])


def dft_tables(side):
    indices = jnp.arange(side, dtype=jnp.int32)
    products = indices[:, None] * indices[None, :] % side
    phase_angle = products.astype(jnp.float32) * (2.0 * math.pi / side)
    norm_factor = 1.0 / math.sqrt(side)
    return (
        (jnp.cos(phase_angle) * norm_factor).astype(jnp.bfloat16),
        (-jnp.sin(phase_angle) * norm_factor).astype(jnp.bfloat16),
    )


def matmul(left, right):
    return jnp.dot(left, right, preferred_element_type=jnp.float32)


def complex_matmul(left_real, left_imag, right_real, right_imag):
    out_real = matmul(left_real, right_real) - matmul(left_imag, right_imag)
    out_imag = matmul(left_real, right_imag) + matmul(left_imag, right_real)
    return (out_real, out_imag)


def patch_terms(patch_real, patch_imag, probe_real, probe_imag, amplitude, dft_real, dft_imag):
    wave_real = (probe_real * patch_real - probe_imag * patch_imag).astype(jnp.bfloat16)
    wave_imag = (probe_real * patch_imag + probe_imag * patch_real).astype(jnp.bfloat16)
    half_real, half_imag = complex_matmul(dft_real, dft_imag, wave_real, wave_imag)
    half_real = half_real.astype(jnp.bfloat16)
    half_imag = half_imag.astype(jnp.bfloat16)
    far_real, far_imag = complex_matmul(half_real, half_imag, dft_real, dft_imag)
    modulus = jnp.sqrt(far_real * far_real + far_imag * far_imag + 0.25)
    factor = amplitude.astype(jnp.float32) / modulus - 1.0
    diff_real = (far_real * factor).astype(jnp.bfloat16)
    diff_imag = (far_imag * factor).astype(jnp.bfloat16)
    conj_imag = -dft_imag
    back_half_real, back_half_imag = complex_matmul(dft_real, conj_imag, diff_real, diff_imag)
    back_half_real = back_half_real.astype(jnp.bfloat16)
    back_half_imag = back_half_imag.astype(jnp.bfloat16)
    back_real, back_imag = complex_matmul(back_half_real, back_half_imag, dft_real, conj_imag)
    object_real = probe_real * back_real + probe_imag * back_imag
    object_imag = probe_real * back_imag - probe_imag * back_real
    probe_grad_real = patch_real * back_real + patch_imag * back_imag
    probe_grad_imag = patch_real * back_imag - patch_imag * back_real
    energy = jnp.mean(patch_real * patch_real + patch_imag * patch_imag)
    return (
        jnp.stack([object_real, object_imag]),
        jnp.stack([probe_grad_real, probe_grad_imag]),
        energy,
    )


def axis_bits(axis):
    return lax.axis_size(axis).bit_length() - 1


def bit_steps(axes):
    steps = []
    for axis in axes:
        steps += [(axis, bit) for bit in reversed(range(axis_bits(axis)))]
    return steps


def link_order(steps):
    by_distance = [("proj", 0), ("tile", 0), ("cuts", 0), ("proj", 2), ("tile", 1), ("cuts", 1)]
    ranked = [step for step in by_distance if step in steps]
    return ranked + [step for step in steps if step not in ranked]


def bit_view(values, steps):
    return values.reshape((2,) * len(steps) + (values.shape[0] >> len(steps),) + values.shape[1:])


def ordered_scatter(values, steps, order):
    values = bit_view(values, steps)
    for axis, bit in order:
        place = steps.index((axis, bit))
        mine = (lax.axis_index(axis) >> bit) & 1
        keep = lax.dynamic_slice_in_dim(values, mine, 1, place)
        send = lax.dynamic_slice_in_dim(values, 1 - mine, 1, place)
        values = keep + exchange(send, axis, bit)
    return values.reshape(values.shape[len(steps) :])


def ordered_gather(values, steps, order):
    values = values.reshape((1,) * len(steps) + values.shape)
    for axis, bit in reversed(order):
        place = steps.index((axis, bit))
        mine = (lax.axis_index(axis) >> bit) & 1
        other = exchange(values, axis, bit)
        values = jnp.where(
            mine == 0,
            jnp.concatenate([values, other], axis=place),
            jnp.concatenate([other, values], axis=place),
        )
    return values.reshape((-1,) + values.shape[len(steps) + 1 :])


def exchange(values, axis, bit):
    count = lax.axis_size(axis)
    return lax.ppermute(values, axis, [(source, source ^ (1 << bit)) for source in range(count)])


def halving_scatter(values, steps):
    for axis, bit in steps:
        mine = (lax.axis_index(axis) >> bit) & 1
        half = values.shape[0] // 2
        keep = lax.dynamic_slice_in_dim(values, mine * half, half, 0)
        send = lax.dynamic_slice_in_dim(values, (1 - mine) * half, half, 0)
        values = keep + exchange(send, axis, bit)
    return values


def exchange_sum(values, steps):
    for axis, bit in steps:
        values = values + exchange(values, axis, bit)
    return values


def doubling_gather(values, steps):
    for axis, bit in reversed(steps):
        mine = (lax.axis_index(axis) >> bit) & 1
        other = exchange(values, axis, bit)
        values = jnp.where(
            mine == 0,
            jnp.concatenate([values, other], axis=0),
            jnp.concatenate([other, values], axis=0),
        )
    return values


def stacked_tables(dft_real, dft_imag):
    rows = lambda top, bottom: jnp.concatenate([top, bottom], axis=0)
    cols = lambda left, right: jnp.concatenate([left, right], axis=1)
    return (
        rows(dft_real, dft_imag),
        rows(-dft_imag, dft_real),
        cols(dft_real, dft_imag),
        cols(-dft_imag, dft_real),
        rows(dft_real, -dft_imag),
        rows(dft_imag, dft_real),
        cols(dft_real, -dft_imag),
        cols(dft_imag, dft_real),
    )


def patch_kernel(meta_ref, window_ref, amp_ref, probe_ref, *refs):
    tables = refs[:8]
    grad_ref, probe_sum_ref, energy_ref = refs[8:]
    slot = pl.program_id(0)
    slots = pl.num_programs(0)
    side = probe_ref.shape[1]
    width = window_ref.shape[2]

    @pl.when(slot == 0)
    def _():
        grad_ref[...] = jnp.zeros(grad_ref.shape, jnp.float32)
        probe_sum_ref[...] = jnp.zeros(probe_sum_ref.shape, jnp.float32)
        energy_ref[...] = jnp.zeros(energy_ref.shape, jnp.float32)

    @pl.when(slot < meta_ref[0])
    def _():
        row = meta_ref[1 + slot]
        col = meta_ref[1 + slots + slot]
        band = side + 8
        rows = pl.ds(pl.multiple_of(row // 8 * 8, 8), band)
        row_shift = row % 8
        to_front = (width - col) % width

        def extract(part):
            values = pltpu.roll(window_ref[part, rows, :], (band - row_shift) % band, 0)
            return pltpu.roll(values[:side], to_front, 1)[:, :side]

        patch_real = extract(0)
        patch_imag = extract(1)
        dot = lambda left, right: jnp.dot(left, right, preferred_element_type=jnp.float32)
        left_1a, left_1b, right_2a, right_2b, left_3a, left_3b, right_4a, right_4b = (
            table[...] for table in tables
        )
        probe_real = probe_ref[0]
        probe_imag = probe_ref[1]
        wave_real = (probe_real * patch_real - probe_imag * patch_imag).astype(jnp.bfloat16)
        wave_imag = (probe_real * patch_imag + probe_imag * patch_real).astype(jnp.bfloat16)
        half = (dot(left_1a, wave_real) + dot(left_1b, wave_imag)).astype(jnp.bfloat16)
        far = dot(half[:side], right_2a) + dot(half[side:], right_2b)
        far_real = far[:, :side]
        far_imag = far[:, side:]
        modulus = jnp.sqrt(far_real * far_real + far_imag * far_imag + 0.25)
        factor = amp_ref[0].astype(jnp.float32) / modulus - 1.0
        diff_real = (far_real * factor).astype(jnp.bfloat16)
        diff_imag = (far_imag * factor).astype(jnp.bfloat16)
        back_half = (dot(left_3a, diff_real) + dot(left_3b, diff_imag)).astype(jnp.bfloat16)
        back = dot(back_half[:side], right_4a) + dot(back_half[side:], right_4b)
        back_real = back[:, :side]
        back_imag = back[:, side:]
        filler = jnp.zeros((side, width - side), jnp.float32)
        below = jnp.zeros((8, width), jnp.float32)
        for part, value in enumerate(
            (
                probe_real * back_real + probe_imag * back_imag,
                probe_real * back_imag - probe_imag * back_real,
            )
        ):
            placed = pltpu.roll(jnp.concatenate([value, filler], axis=1), col, 1)
            placed = pltpu.roll(jnp.concatenate([placed, below], axis=0), row_shift, 0)
            grad_ref[part, rows, :] += placed
        probe_sum_ref[0] += patch_real * back_real + patch_imag * back_imag
        probe_sum_ref[1] += patch_real * back_imag - patch_imag * back_real
        energy = jnp.sum(patch_real * patch_real + patch_imag * patch_imag) / (side * side)
        energy_ref[...] += energy


def patch_terms_all(meta, window, amps, probe_field, tables):
    slots, side, _ = amps.shape
    full = lambda shape: pl.BlockSpec(shape, lambda slot, meta_ref: (0,) * len(shape))
    grid_spec = pltpu.PrefetchScalarGridSpec(
        num_scalar_prefetch=1,
        grid=(slots,),
        in_specs=[
            full(window.shape),
            pl.BlockSpec((1, side, side), lambda slot, meta_ref: (slot, 0, 0)),
            full((2, side, side)),
        ]
        + [full(table.shape) for table in tables],
        out_specs=[
            full(window.shape),
            full((2, side, side)),
            full((8, 128)),
        ],
    )
    return pl.pallas_call(
        patch_kernel,
        grid_spec=grid_spec,
        out_shape=[
            jax.ShapeDtypeStruct(window.shape, jnp.float32),
            jax.ShapeDtypeStruct((2, side, side), jnp.float32),
            jax.ShapeDtypeStruct((8, 128), jnp.float32),
        ],
        compiler_params=pltpu.CompilerParams(dimension_semantics=("arbitrary",)),
    )(meta, window, amps, probe_field, *tables)


def tile_edges(values, offset):
    return shifted(values, "tile", offset)


def on_device(
    object_field,
    probe_field,
    amplitudes,
    pos_rows,
    pos_cols,
    counts,
    admm_dual,
    volume,
    proj_weights,
    ray_weights,
    angle_ids,
):
    half_side = PB // 2
    own_object = object_field[0]
    tile_cols = own_object.shape[2]
    from_left = tile_edges(own_object[:, :, tile_cols - half_side :], 1)
    from_right = tile_edges(own_object[:, :, :half_side], -1)
    extended = jnp.concatenate([from_left, own_object, from_right], axis=2)
    dft_real, dft_imag = dft_tables(PB)
    probe_real = probe_field[0]
    probe_imag = probe_field[1]

    spare = -(-extended.shape[2] // 128) * 128 + 128 - extended.shape[2]
    window = jnp.pad(extended, ((0, 0), (0, 8), (0, spare)))
    angle_count = ray_weights.shape[0]
    x_share = volume.shape[1]
    width = volume.shape[2]
    onehot = (angle_ids[:, None] == jnp.arange(angle_count, dtype=jnp.int32)[None, :]).astype(
        jnp.float32
    )
    ray_table = jnp.dot(
        onehot, ray_weights, precision=lax.Precision.HIGHEST, preferred_element_type=jnp.float32
    )
    ray_sums = jnp.einsum("zxy,ay->azx", volume, ray_table, precision=lax.Precision.HIGHEST).astype(
        jnp.bfloat16
    )
    spread = onehot.astype(jnp.bfloat16)[:, :, None, None] * ray_sums[:, None, :, :]
    spread = spread.transpose(1, 3, 0, 2).reshape(
        angle_count * x_share, ray_sums.shape[0] * ray_sums.shape[1]
    )
    weight_flat = proj_weights.reshape(angle_count * x_share, width)
    partial_term = lax.dot_general(
        weight_flat, spread, (((0,), (0,)), ((), ())), preferred_element_type=jnp.float32
    )
    volume_steps = bit_steps(("tile", "proj"))
    volume_order = link_order(volume_steps)
    own_rows = ordered_scatter(partial_term, volume_steps, volume_order)
    own_rows, window = lax.optimization_barrier((own_rows, window))
    meta = jnp.concatenate([counts[0, :1], pos_rows[0, 0], pos_cols[0, 0]])
    grad_sum, probe_sum, energy_rows = patch_terms_all(
        meta,
        window,
        amplitudes[0, 0],
        probe_field,
        stacked_tables(dft_real, dft_imag),
    )
    energy_sum = energy_rows[0, 0]
    grad_sum = grad_sum[:, : extended.shape[1]]
    to_right_edge = tile_edges(grad_sum[:, :, :half_side], -1)
    to_left_edge = tile_edges(grad_sum[:, :, tile_cols + half_side : tile_cols + PB], 1)
    own_cells = grad_sum[:, :, half_side : half_side + tile_cols]
    own_cells = own_cells.at[:, :, :half_side].add(to_left_edge)
    own_cells = own_cells.at[:, :, tile_cols - half_side :].add(to_right_edge)
    probe_order = link_order(bit_steps(("proj", "tile", "cuts")))
    probe_steps, probe_rest = probe_order[:3], probe_order[3:]
    probe_rows = probe_sum.size // 128
    padded_rows = -(-(probe_rows + 1) // 2 ** len(probe_steps)) * 2 ** len(probe_steps)
    probe_flat = jnp.concatenate(
        [
            probe_sum.reshape(probe_rows, 128),
            jnp.broadcast_to(energy_sum, (1, 128)),
            jnp.zeros((padded_rows - probe_rows - 1, 128), jnp.float32),
        ]
    )
    probe_flat = exchange_sum(halving_scatter(probe_flat, probe_steps), probe_rest)
    probe_flat = doubling_gather(probe_flat, probe_steps)
    probe_grad = probe_flat[:probe_rows].reshape(probe_sum.shape)
    energy = probe_flat[probe_rows, 0]
    new_probe = probe_field + probe_grad / (energy + 1e-05)
    probe_peak = jnp.max(probe_real * probe_real + probe_imag * probe_imag)
    new_object = (own_object + own_cells / (probe_peak + 1e-05))[None]
    slab_total = admm_dual.shape[1]
    first_row = (own_object.shape[1] - slab_total) // 2
    slab_values = new_object[:, 1, first_row : first_row + slab_total, :] + admm_dual
    arrived = lax.all_to_all(
        lax.all_to_all(slab_values, "proj", split_axis=2, concat_axis=0, tiled=True),
        "cuts",
        split_axis=1,
        concat_axis=0,
        tiled=True,
    )
    proj_count = lax.axis_size("proj")
    cuts_count = lax.axis_size("cuts")
    slab_dev = arrived.shape[1]
    u_share = arrived.shape[2]
    projections = proj_count * cuts_count
    arrived = arrived.reshape(cuts_count, proj_count, slab_dev, u_share).transpose(1, 0, 2, 3)
    target = (
        arrived.reshape(projections, slab_dev, u_share)
        .transpose(2, 0, 1)
        .reshape(u_share, projections * slab_dev)
    )
    own_residue = (own_rows - target).astype(jnp.bfloat16)
    residue = ordered_gather(own_residue, volume_steps, volume_order)
    backproj = matmul(weight_flat, residue)
    backproj = backproj.reshape(angle_count, x_share, projections, slab_dev)
    back_sums = jnp.einsum("gxaz,ag->azx", backproj, onehot, precision=lax.Precision.HIGHEST)
    gradient = jnp.einsum("azx,ay->zxy", back_sums, ray_table, precision=lax.Precision.HIGHEST)
    new_volume = volume - tomo_step * gradient
    return (new_object, new_probe, new_volume)


def solution(mesh):
    in_specs = (
        P(("proj", "cuts"), None, None, "tile"),
        P(),
        P(("proj", "cuts"), "tile", None, None, None),
        P(("proj", "cuts"), "tile", None),
        P(("proj", "cuts"), "tile", None),
        P(("proj", "cuts"), "tile"),
        P(("proj", "cuts"), None, "tile"),
        P("cuts", ("tile", "proj"), None),
        P(None, ("tile", "proj"), None),
        P(),
        P(),
    )
    out_specs = (P(("proj", "cuts"), None, None, "tile"), P(), P("cuts", ("tile", "proj"), None))
    return jax.shard_map(
        on_device, mesh=mesh, in_specs=in_specs, out_specs=out_specs, check_vma=False
    )
```

profile of v0, /device:TPU:1, one launch (start us, length us, event | category | flops | bytes accessed | tf_op | source)
XLA Modules:
  0.0 282.2 jit_solution(4514354812137442349)
XLA Ops:
  14.6 5.4 %copy.51 = f32[2048,512]{1,0:T(8,128)} copy(f32[2048,512]{0,1:T(8,128)} %convolution_bitcast_fusion) | data formatting | bytes 8388608 | tf_op jit(solution)/shard_map/dot_general | solution.py:307
  26.5 4.1 %collective-permute-done = f32[2,2,2,2,2,1,32,512]{7,6,5,4,3,2,1,0:T(8,128)} collective-permute-done((f32[2,2,2,2,2,1,32,512]{7,6,5,4,3,2,1,0:T(8,128)}, f32[2,2,2,2,2,1,32,512]{7,6,5,4,3,2,1,0:T(8,128)}, u32[]{:S(2)}, u32[]{:S(2)}) %collective-permute-start) | collective-permute-done | bytes 2097184 | tf_op jit(solution)/shard_map/ppermute | solution.py:119
  35.7 24.7 %collective-permute-done.1 = f32[2,1,2,2,2,1,32,512]{7,6,5,4,3,2,1,0:T(8,128)} collective-permute-done((f32[2,1,2,2,2,1,32,512]{7,6,5,4,3,2,1,0:T(8,128)}, f32[2,1,2,2,2,1,32,512]{7,6,5,4,3,2,1,0:T(8,128)}, u32[]{:S(2)}, u32[]{:S(2)}) %collective-permute-start.1) | collective-permute-done | bytes 1048608 | tf_op jit(solution)/shard_map/ppermute | solution.py:119
  67.9 6.7 %collective-permute-done.2 = f32[2,1,2,1,2,1,32,512]{7,6,5,4,3,2,1,0:T(8,128)} collective-permute-done((f32[2,1,2,1,2,1,32,512]{7,6,5,4,3,2,1,0:T(8,128)S(1)}, f32[2,1,2,1,2,1,32,512]{7,6,5,4,3,2,1,0:T(8,128)}, u32[]{:S(2)}, u32[]{:S(2)}) %collective-permute-start.2) | collective-permute-done | bytes 524320 | tf_op jit(solution)/shard_map/ppermute | solution.py:119
  89.8 5.4 %collective-permute-start.5 = (f32[1,1,1,1,1,1,32,512]{7,6,5,4,3,2,1,0:T(8,128)S(1)}, f32[1,1,1,1,1,1,32,512]{7,6,5,4,3,2,1,0:T(8,128)S(1)}, u32[]{:S(2)}, u32[]{:S(2)}) collective-permute-start(f32[1,1,1,1,1,1,32,512]{7,6,5,4,3,2,1,0:T(8,128)S(1)} %constant_dynamic-slice_fusion.3), channel_id=1, source_target_pairs={{0,8},{4,12},{8,0},{12,4},{16,24},{20,28},{24,16},{28,20},{32,40},... | collective-permute-start | bytes 196616 | tf_op jit(solution)/shard_map/ppermute | solution.py:119
  99.2 11.1 %shard_map.130 = (f32[2,392,896]{2,1,0:T(8,128)}, f32[2,256,256]{2,1,0:T(8,128)}, f32[8,128]{1,0:T(8,128)}) custom-call(s32[13]{0:T(128)} %pad_add_fusion.meta_ref, f32[2,392,896]{2,1,0:T(8,128)} %select_maximum_fusion.window_ref, bf16[6,256,256]{2,1,0:T(8,128)(2,1)} %bitcast.120, f32[2,256,256]{2,1,0:T(8,128)} %probe_ref.1, ...), custom_call_target="tpu_custom_call" | custom-call | tf_op jit(solution)/shard_map/pallas_call | solution.py:249
  112.3 13.6 %collective-permute-start.8 = (f32[2,384,128]{2,1,0:T(8,128)}, f32[2,384,128]{2,1,0:T(8,128)}, u32[]{:S(2)}, u32[]{:S(2)}) collective-permute-start(f32[2,384,128]{2,1,0:T(8,128)} %get-tuple-element.38), channel_id=1, source_target_pairs={{0,64},{64,128},{128,192},{1,65},{65,129},{129,193},{2,66},{66,130... | collective-permute-start | bytes 1179656 | tf_op jit(solution)/shard_map/ppermute | solution.py:19
  132.4 4.5 %collective-permute-done.9 = f32[2,384,128]{2,1,0:T(8,128)} collective-permute-done((f32[2,384,128]{2,1,0:T(8,128)S(1)}, f32[2,384,128]{2,1,0:T(8,128)}, u32[]{:S(2)}, u32[]{:S(2)}) %collective-permute-start.9) | collective-permute-done | bytes 393248 | tf_op jit(solution)/shard_map/ppermute | solution.py:19
  144.2 10.6 %all-to-all-start = ((f32[16,1,1024]{2,1,0:T(1,128)}), f32[16,1,1024]{2,1,0:T(1,128)S(1)}, u32[]{:S(2)}, u32[]{:S(2)}) async-start(f32[16,1,1024]{2,1,0:T(1,128)} %reshape.1102), calls=%async_computation | async-start | bytes 131072 | tf_op jit(solution)/shard_map/all_to_all | solution.py:351
  160.9 3.6 %all-to-all-done = f32[16,1,1024]{2,1,0:T(1,128)S(1)} async-done(((f32[16,1,1024]{2,1,0:T(1,128)}), f32[16,1,1024]{2,1,0:T(1,128)S(1)}, u32[]{:S(2)}, u32[]{:S(2)}) %all-to-all-start) | async-done | bytes 65568 | tf_op jit(solution)/shard_map/all_to_all | solution.py:351
  168.4 8.7 %all-to-all-start.1 = ((f32[4,1,4096]{2,1,0:T(1,128)}), f32[4,1,4096]{2,1,0:T(1,128)S(1)}, u32[]{:S(2)}, u32[]{:S(2)}) async-start(f32[4,1,4096]{2,1,0:T(1,128)} %reshape.1104), calls=%async_computation.1 | async-start | bytes 131072 | tf_op jit(solution)/shard_map/all_to_all | solution.py:350
  187.4 4.3 %collective-permute-done.21 = bf16[1,1,1,1,1,1,32,512]{7,6,5,4,3,2,1,0:T(8,128)(2,1)S(1)} collective-permute-done((bf16[1,1,1,1,1,1,32,512]{7,6,5,4,3,2,1,0:T(8,128)(2,1)S(1)}, bf16[1,1,1,1,1,1,32,512]{7,6,5,4,3,2,1,0:T(8,128)(2,1)S(1)}, u32[]{:S(2)}, u32[]{:S(2)}) %collective-permute-start.21) | collective-permute-done | bytes 32800 | tf_op jit(solution)/shard_map/ppermute | solution.py:119
  192.4 4.0 %collective-permute-done.22 = bf16[1,1,1,1,2,1,32,512]{7,6,5,4,3,2,1,0:T(8,128)(2,1)S(1)} collective-permute-done((bf16[1,1,1,1,2,1,32,512]{7,6,5,4,3,2,1,0:T(8,128)(2,1)S(1)}, bf16[1,1,1,1,2,1,32,512]{7,6,5,4,3,2,1,0:T(8,128)(2,1)S(1)}, u32[]{:S(2)}, u32[]{:S(2)}) %collective-permute-start.22) | collective-permute-done | bytes 65568 | tf_op jit(solution)/shard_map/ppermute | solution.py:119
  196.7 5.1 %collective-permute-done.23 = bf16[1,1,2,1,2,1,32,512]{7,6,5,4,3,2,1,0:T(8,128)(2,1)S(1)} collective-permute-done((bf16[1,1,2,1,2,1,32,512]{7,6,5,4,3,2,1,0:T(8,128)(2,1)S(1)}, bf16[1,1,2,1,2,1,32,512]{7,6,5,4,3,2,1,0:T(8,128)(2,1)S(1)}, u32[]{:S(2)}, u32[]{:S(2)}) %collective-permute-start.23) | collective-permute-done | bytes 131104 | tf_op jit(solution)/shard_map/ppermute | solution.py:119
  203.8 3.4 %collective-permute-done.24 = bf16[2,1,2,1,2,1,32,512]{7,6,5,4,3,2,1,0:T(8,128)(2,1)S(1)} collective-permute-done((bf16[2,1,2,1,2,1,32,512]{7,6,5,4,3,2,1,0:T(8,128)(2,1)S(1)}, bf16[2,1,2,1,2,1,32,512]{7,6,5,4,3,2,1,0:T(8,128)(2,1)S(1)}, u32[]{:S(2)}, u32[]{:S(2)}) %collective-permute-start.24) | collective-permute-done | bytes 262176 | tf_op jit(solution)/shard_map/ppermute | solution.py:119
  208.3 4.2 %collective-permute-done.13 = f32[129,128]{1,0:T(8,128)S(1)} collective-permute-done((f32[129,128]{1,0:T(8,128)S(1)}, f32[129,128]{1,0:T(8,128)S(1)}, u32[]{:S(2)}, u32[]{:S(2)}) %collective-permute-start.13) | collective-permute-done | bytes 66080 | tf_op jit(solution)/shard_map/ppermute | solution.py:119
  212.9 5.0 %collective-permute-done.14 = f32[129,128]{1,0:T(8,128)S(1)} collective-permute-done((f32[129,128]{1,0:T(8,128)S(1)}, f32[129,128]{1,0:T(8,128)S(1)}, u32[]{:S(2)}, u32[]{:S(2)}) %collective-permute-start.14) | collective-permute-done | bytes 66080 | tf_op jit(solution)/shard_map/ppermute | solution.py:119
  218.5 4.3 %collective-permute-done.15 = f32[129,128]{1,0:T(8,128)S(1)} collective-permute-done((f32[129,128]{1,0:T(8,128)S(1)}, f32[129,128]{1,0:T(8,128)S(1)}, u32[]{:S(2)}, u32[]{:S(2)}) %collective-permute-start.15) | collective-permute-done | bytes 66080 | tf_op jit(solution)/shard_map/ppermute | solution.py:119
  223.5 4.1 %collective-permute-done.16 = f32[129,128]{1,0:T(8,128)S(1)} collective-permute-done((f32[129,128]{1,0:T(8,128)S(1)}, f32[129,128]{1,0:T(8,128)S(1)}, u32[]{:S(2)}, u32[]{:S(2)}) %collective-permute-start.16) | collective-permute-done | bytes 66080 | tf_op jit(solution)/shard_map/ppermute | solution.py:119
  228.9 5.9 %collective-permute-done.17 = f32[129,128]{1,0:T(8,128)S(1)} collective-permute-done((f32[129,128]{1,0:T(8,128)S(1)}, f32[129,128]{1,0:T(8,128)S(1)}, u32[]{:S(2)}, u32[]{:S(2)}) %collective-permute-start.17) | collective-permute-done | bytes 66080 | tf_op jit(solution)/shard_map/ppermute | solution.py:119
  238.3 11.6 %collective-permute-start.26 = (bf16[2,2,2,2,2,1,32,512]{7,6,5,4,3,2,1,0:T(8,128)(2,1)}, bf16[2,2,2,2,2,1,32,512]{7,6,5,4,3,2,1,0:T(8,128)(2,1)}, u32[]{:S(2)}, u32[]{:S(2)}) collective-permute-start(bf16[2,2,2,2,2,1,32,512]{7,6,5,4,3,2,1,0:T(8,128)(2,1)} %maximum_select_fusion.1), channel_id=1, source_target_pairs={{0,4},{4,0},{8,12},{12,8},{16,20},{20,16},{24,28},{28,24},{32,36},... | collective-permute-start | bytes 3145736 | tf_op jit(solution)/shard_map/ppermute | solution.py:119
  269.8 3.8 %reshape.1098 = f32[16,32,64,8]{1,0,3,2:T(8,128)} reshape(f32[512,512]{0,1:T(8,128)} %convolution_bitcast_fusion.2) | data formatting | bytes 2097152 | tf_op jit(solution)/shard_map/reshape | solution.py:371
  273.6 3.8 %fusion.12 = f32[64,1,32,8]{2,1,3,0:T(1,128)S(1)} fusion(f32[16,32,64,8]{1,0,3,2:T(8,128)} %reshape.1098, pred[64,16,1,1]{1,0,2,3:T(32,128)(4,1)S(1)} %fusion.16), kind=kOutput, calls=%fused_computation.59 | convolution fusion | flops 3145728 | bytes 1115136 | tf_op jit(solution)/shard_map/gxaz,ag->azx/dot_general | solution.py:372
  277.5 4.7 %convolution_subtract_fusion = f32[8,32,2048]{2,1,0:T(8,128)} fusion(f32[8,32,2048]{2,1,0:T(8,128)} %param.22, f32[64,2048,1]{1,0,2:T(8,128)S(1)} %convolution_bitcast_fusion.1, f32[64,1,32,8]{0,2,3,1:T(8,128)S(1)} %copy.66), kind=kOutput, calls=%fused_computation.5 | convolution fusion | flops 403177472 | bytes 4784128 | tf_op jit(solution)/shard_map/azx,ay->zxy/dot_general | solution.py:373
  (146 shorter events, 116.4 us)
Async XLA Ops:
  23.2 7.4 %collective-permute-start = (f32[2,2,2,2,2,1,32,512]{7,6,5,4,3,2,1,0:T(8,128)}, f32[2,2,2,2,2,1,32,512]{7,6,5,4,3,2,1,0:T(8,128)}, u32[]{:S(2)}, u32[]{:S(2)}) collective-permute-start(f32[2,2,2,2,2,1,32,512]{7,6,5,4,3,2,1,0:T(8,128)} %constant_dynamic-slice_fusion.8), channel_id=1, source_target_pairs={{0,4},{4,0},{8,12},{12,8},{16,20},{20,16},{24,28},{28,24},{32,36},... | collective-permute-start | bytes 6291464 | tf_op jit(solution)/shard_map/ppermute | solution.py:119
  35.7 24.7 %collective-permute-start.1 = (f32[2,1,2,2,2,1,32,512]{7,6,5,4,3,2,1,0:T(8,128)}, f32[2,1,2,2,2,1,32,512]{7,6,5,4,3,2,1,0:T(8,128)}, u32[]{:S(2)}, u32[]{:S(2)}) collective-permute-start(f32[2,1,2,2,2,1,32,512]{7,6,5,4,3,2,1,0:T(8,128)} %constant_dynamic-slice_fusion.7), channel_id=1, source_target_pairs={{0,64},{64,0},{128,192},{192,128},{1,65},{65,1},{129,193},{193,129... | collective-permute-start | bytes 3145736 | tf_op jit(solution)/shard_map/ppermute | solution.py:119
  62.2 12.4 %collective-permute-start.2 = (f32[2,1,2,1,2,1,32,512]{7,6,5,4,3,2,1,0:T(8,128)S(1)}, f32[2,1,2,1,2,1,32,512]{7,6,5,4,3,2,1,0:T(8,128)}, u32[]{:S(2)}, u32[]{:S(2)}) collective-permute-start(f32[2,1,2,1,2,1,32,512]{7,6,5,4,3,2,1,0:T(8,128)S(1)} %constant_dynamic-slice_fusion.6), channel_id=1, source_target_pairs={{0,16},{4,20},{8,24},{12,28},{16,0},{20,4},{24,8},{28,12},{32,48},... | collective-permute-start | bytes 1572872 | tf_op jit(solution)/shard_map/ppermute | solution.py:119
  63.3 31.9 %collective-permute-start.6 = (f32[2,384,128]{2,1,0:T(8,128)}, f32[2,384,128]{2,1,0:T(8,128)}, u32[]{:S(2)}, u32[]{:S(2)}) collective-permute-start(f32[2,384,128]{2,1,0:T(8,128)} %get-tuple-element.39), channel_id=1, source_target_pairs={{0,64},{64,128},{128,192},{1,65},{65,129},{129,193},{2,66},{66,130... | collective-permute-start | bytes 1179656 | tf_op jit(solution)/shard_map/ppermute | solution.py:19
  66.6 28.6 %collective-permute-start.7 = (f32[2,384,128]{2,1,0:T(8,128)}, f32[2,384,128]{2,1,0:T(8,128)}, u32[]{:S(2)}, u32[]{:S(2)}) collective-permute-start(f32[2,384,128]{2,1,0:T(8,128)} %get-tuple-element.40), channel_id=1, source_target_pairs={{64,0},{128,64},{192,128},{65,1},{129,65},{193,129},{66,2},{130,66... | collective-permute-start | bytes 1179656 | tf_op jit(solution)/shard_map/ppermute | solution.py:19
  75.9 7.4 %collective-permute-start.3 = (f32[1,1,2,1,2,1,32,512]{7,6,5,4,3,2,1,0:T(8,128)S(1)}, f32[1,1,2,1,2,1,32,512]{7,6,5,4,3,2,1,0:T(8,128)}, u32[]{:S(2)}, u32[]{:S(2)}) collective-permute-start(f32[1,1,2,1,2,1,32,512]{7,6,5,4,3,2,1,0:T(8,128)S(1)} %constant_dynamic-slice_fusion.5), channel_id=1, source_target_pairs={{0,128},{64,192},{128,0},{192,64},{1,129},{65,193},{129,1},{193,65... | collective-permute-start | bytes 786440 | tf_op jit(solution)/shard_map/ppermute | solution.py:119
  84.3 5.4 %collective-permute-start.4 = (f32[1,1,1,1,2,1,32,512]{7,6,5,4,3,2,1,0:T(8,128)S(1)}, f32[1,1,1,1,2,1,32,512]{7,6,5,4,3,2,1,0:T(8,128)S(1)}, u32[]{:S(2)}, u32[]{:S(2)}) collective-permute-start(f32[1,1,1,1,2,1,32,512]{7,6,5,4,3,2,1,0:T(8,128)S(1)} %constant_dynamic-slice_fusion.4), channel_id=1, source_target_pairs={{0,32},{4,36},{8,40},{12,44},{16,48},{20,52},{24,56},{28,60},{32,0... | collective-permute-start | bytes 393224 | tf_op jit(solution)/shard_map/ppermute | solution.py:119
  89.8 8.8 %collective-permute-start.5 = (f32[1,1,1,1,1,1,32,512]{7,6,5,4,3,2,1,0:T(8,128)S(1)}, f32[1,1,1,1,1,1,32,512]{7,6,5,4,3,2,1,0:T(8,128)S(1)}, u32[]{:S(2)}, u32[]{:S(2)}) collective-permute-start(f32[1,1,1,1,1,1,32,512]{7,6,5,4,3,2,1,0:T(8,128)S(1)} %constant_dynamic-slice_fusion.3), channel_id=1, source_target_pairs={{0,8},{4,12},{8,0},{12,4},{16,24},{20,28},{24,16},{28,20},{32,40},... | collective-permute-start | bytes 196616 | tf_op jit(solution)/shard_map/ppermute | solution.py:119
  112.3 19.0 %collective-permute-start.8 = (f32[2,384,128]{2,1,0:T(8,128)}, f32[2,384,128]{2,1,0:T(8,128)}, u32[]{:S(2)}, u32[]{:S(2)}) collective-permute-start(f32[2,384,128]{2,1,0:T(8,128)} %get-tuple-element.38), channel_id=1, source_target_pairs={{0,64},{64,128},{128,192},{1,65},{65,129},{129,193},{2,66},{66,130... | collective-permute-start | bytes 1179656 | tf_op jit(solution)/shard_map/ppermute | solution.py:19
  125.8 11.1 %collective-permute-start.9 = (f32[2,384,128]{2,1,0:T(8,128)S(1)}, f32[2,384,128]{2,1,0:T(8,128)}, u32[]{:S(2)}, u32[]{:S(2)}) collective-permute-start(f32[2,384,128]{2,1,0:T(8,128)S(1)} %get-tuple-element.37), channel_id=1, source_target_pairs={{64,0},{128,64},{192,128},{65,1},{129,65},{193,129},{66,2},{130,66... | collective-permute-start | bytes 1179656 | tf_op jit(solution)/shard_map/ppermute | solution.py:19
  144.2 20.3 %all-to-all-start = ((f32[16,1,1024]{2,1,0:T(1,128)}), f32[16,1,1024]{2,1,0:T(1,128)S(1)}, u32[]{:S(2)}, u32[]{:S(2)}) async-start(f32[16,1,1024]{2,1,0:T(1,128)} %reshape.1102), calls=%async_computation | async-start | bytes 131072 | tf_op jit(solution)/shard_map/all_to_all | solution.py:351
  168.4 13.3 %all-to-all-start.1 = ((f32[4,1,4096]{2,1,0:T(1,128)}), f32[4,1,4096]{2,1,0:T(1,128)S(1)}, u32[]{:S(2)}, u32[]{:S(2)}) async-start(f32[4,1,4096]{2,1,0:T(1,128)} %reshape.1104), calls=%async_computation.1 | async-start | bytes 131072 | tf_op jit(solution)/shard_map/all_to_all | solution.py:350
  178.8 7.5 %collective-permute-start.10 = (f32[516,128]{1,0:T(8,128)}, f32[516,128]{1,0:T(8,128)}, u32[]{:S(2)}, u32[]{:S(2)}) collective-permute-start(f32[516,128]{1,0:T(8,128)} %constant_dynamic-slice_fusion.2), channel_id=1, source_target_pairs={{0,4},{4,0},{8,12},{12,8},{16,20},{20,16},{24,28},{28,24},{32,36},... | collective-permute-start | bytes 792584 | tf_op jit(solution)/shard_map/ppermute | solution.py:119
  184.6 7.1 %collective-permute-start.21 = (bf16[1,1,1,1,1,1,32,512]{7,6,5,4,3,2,1,0:T(8,128)(2,1)S(1)}, bf16[1,1,1,1,1,1,32,512]{7,6,5,4,3,2,1,0:T(8,128)(2,1)S(1)}, u32[]{:S(2)}, u32[]{:S(2)}) collective-permute-start(bf16[1,1,1,1,1,1,32,512]{7,6,5,4,3,2,1,0:T(8,128)(2,1)S(1)} %bitcast.123), channel_id=1, source_target_pairs={{0,8},{4,12},{8,0},{12,4},{16,24},{20,28},{24,16},{28,20},{32,40},... | collective-permute-start | bytes 98312 | tf_op jit(solution)/shard_map/ppermute | solution.py:119
  196.5 5.4 %collective-permute-start.23 = (bf16[1,1,2,1,2,1,32,512]{7,6,5,4,3,2,1,0:T(8,128)(2,1)S(1)}, bf16[1,1,2,1,2,1,32,512]{7,6,5,4,3,2,1,0:T(8,128)(2,1)S(1)}, u32[]{:S(2)}, u32[]{:S(2)}) collective-permute-start(bf16[1,1,2,1,2,1,32,512]{7,6,5,4,3,2,1,0:T(8,128)(2,1)S(1)} %fusion.10), channel_id=1, source_target_pairs={{0,128},{64,192},{128,0},{192,64},{1,129},{65,193},{129,1},{193,65... | collective-permute-start | bytes 393224 | tf_op jit(solution)/shard_map/ppermute | solution.py:119
  196.6 5.4 %collective-permute-start.11 = (f32[258,128]{1,0:T(8,128)S(1)}, f32[258,128]{1,0:T(8,128)S(1)}, u32[]{:S(2)}, u32[]{:S(2)}) collective-permute-start(f32[258,128]{1,0:T(8,128)S(1)} %constant_dynamic-slice_fusion.1), channel_id=1, source_target_pairs={{0,64},{64,0},{128,192},{192,128},{1,65},{65,1},{129,193},{193,129... | collective-permute-start | bytes 396296 | tf_op jit(solution)/shard_map/ppermute | solution.py:119
  201.9 5.3 %collective-permute-start.24 = (bf16[2,1,2,1,2,1,32,512]{7,6,5,4,3,2,1,0:T(8,128)(2,1)S(1)}, bf16[2,1,2,1,2,1,32,512]{7,6,5,4,3,2,1,0:T(8,128)(2,1)S(1)}, u32[]{:S(2)}, u32[]{:S(2)}) collective-permute-start(bf16[2,1,2,1,2,1,32,512]{7,6,5,4,3,2,1,0:T(8,128)(2,1)S(1)} %fusion.6), channel_id=1, source_target_pairs={{0,16},{4,20},{8,24},{12,28},{16,0},{20,4},{24,8},{28,12},{32,48},... | collective-permute-start | bytes 786440 | tf_op jit(solution)/shard_map/ppermute | solution.py:119
  202.1 6.1 %collective-permute-start.12 = (f32[129,128]{1,0:T(8,128)S(1)}, f32[129,128]{1,0:T(8,128)S(1)}, u32[]{:S(2)}, u32[]{:S(2)}) collective-permute-start(f32[129,128]{1,0:T(8,128)S(1)} %constant_dynamic-slice_fusion), channel_id=1, source_target_pairs={{0,1},{1,0},{2,3},{3,2},{4,5},{5,4},{6,7},{7,6},{8,9},{9,8},{10,11... | collective-permute-start | bytes 198152 | tf_op jit(solution)/shard_map/ppermute | solution.py:119
  208.2 27.8 %collective-permute-start.25 = (bf16[2,1,2,2,2,1,32,512]{7,6,5,4,3,2,1,0:T(8,128)(2,1)}, bf16[2,1,2,2,2,1,32,512]{7,6,5,4,3,2,1,0:T(8,128)(2,1)}, u32[]{:S(2)}, u32[]{:S(2)}) collective-permute-start(bf16[2,1,2,2,2,1,32,512]{7,6,5,4,3,2,1,0:T(8,128)(2,1)} %maximum_select_fusion.4), channel_id=1, source_target_pairs={{0,64},{64,0},{128,192},{192,128},{1,65},{65,1},{129,193},{193,129... | collective-permute-start | bytes 1572872 | tf_op jit(solution)/shard_map/ppermute | solution.py:119
  212.5 5.5 %collective-permute-start.14 = (f32[129,128]{1,0:T(8,128)S(1)}, f32[129,128]{1,0:T(8,128)S(1)}, u32[]{:S(2)}, u32[]{:S(2)}) collective-permute-start(f32[129,128]{1,0:T(8,128)S(1)} %add.209), channel_id=1, source_target_pairs={{0,128},{64,192},{128,0},{192,64},{1,129},{65,193},{129,1},{193,65... | collective-permute-start | bytes 198152 | tf_op jit(solution)/shard_map/ppermute | solution.py:119
  227.6 7.2 %collective-permute-start.17 = (f32[129,128]{1,0:T(8,128)S(1)}, f32[129,128]{1,0:T(8,128)S(1)}, u32[]{:S(2)}, u32[]{:S(2)}) collective-permute-start(f32[129,128]{1,0:T(8,128)S(1)} %add.212), channel_id=1, source_target_pairs={{0,8},{4,12},{8,0},{12,4},{16,24},{20,28},{24,16},{28,20},{32,40},... | collective-permute-start | bytes 198152 | tf_op jit(solution)/shard_map/ppermute | solution.py:119
  234.8 15.2 %collective-permute-start.18 = (f32[129,128]{1,0:T(8,128)S(1)}, f32[129,128]{1,0:T(8,128)S(1)}, u32[]{:S(2)}, u32[]{:S(2)}) collective-permute-start(f32[129,128]{1,0:T(8,128)S(1)} %add.213), channel_id=1, source_target_pairs={{0,1},{1,0},{2,3},{3,2},{4,5},{5,4},{6,7},{7,6},{8,9},{9,8},{10,11... | collective-permute-start | bytes 198152 | tf_op jit(solution)/shard_map/ppermute | solution.py:119
  238.3 26.6 %collective-permute-start.26 = (bf16[2,2,2,2,2,1,32,512]{7,6,5,4,3,2,1,0:T(8,128)(2,1)}, bf16[2,2,2,2,2,1,32,512]{7,6,5,4,3,2,1,0:T(8,128)(2,1)}, u32[]{:S(2)}, u32[]{:S(2)}) collective-permute-start(bf16[2,2,2,2,2,1,32,512]{7,6,5,4,3,2,1,0:T(8,128)(2,1)} %maximum_select_fusion.1), channel_id=1, source_target_pairs={{0,4},{4,0},{8,12},{12,8},{16,20},{20,16},{24,28},{28,24},{32,36},... | collective-permute-start | bytes 3145736 | tf_op jit(solution)/shard_map/ppermute | solution.py:119
  250.0 5.3 %collective-permute-start.19 = (f32[258,128]{1,0:T(8,128)S(1)}, f32[258,128]{1,0:T(8,128)S(1)}, u32[]{:S(2)}, u32[]{:S(2)}) collective-permute-start(f32[258,128]{1,0:T(8,128)S(1)} %maximum_select_fusion.7), channel_id=1, source_target_pairs={{0,64},{64,0},{128,192},{192,128},{1,65},{65,1},{129,193},{193,129... | collective-permute-start | bytes 396296 | tf_op jit(solution)/shard_map/ppermute | solution.py:119
  (17 other events, 171.8 us)
where the time goes:
time: 284 us; the launch traced here: 282 us
  waiting for transfers between devices  96.7 us (34%)
  starting transfers between devices  72.4 us (25%)
  local copies, waits for them, and re-layouts  42 us (15%)
  other arithmetic  38.1 us (13%)
  matrix products  18.7 us (7%)
  Pallas kernels  11.1 us (4%)
  between operations  3.11 us (1%)
    ppermute x23, waiting for transfers between devices, exchange(): lax.ppermute(values, axis, [(source, source ^ 1 << bit) for source in ran...  85.3 us
    ppermute x23, starting transfers between devices, exchange(): lax.ppermute(values, axis, [(source, source ^ 1 << bit) for source in ran...  33.7 us
    ppermute x4, starting transfers between devices, shifted(): lax.ppermute(value, axis, [(source, source + steps) for source in range(l...  19.4 us
    pallas_call x1, Pallas kernels, patch_terms_all(): pl.pallas_call(patch_kernel, grid_spec=grid_spec, out_shape=[jax.ShapeDty...  11.1 us
    all_to_all x1, starting transfers between devices, on_device(): lax.all_to_all(slab_values, 'proj', split_axis=2, concat_axis=0, tiled=True)  10.6 us
    all_to_all x1, starting transfers between devices, on_device(): lax.all_to_all(lax.all_to_all(slab_values, 'proj', split_axis=2, concat_a...  8.75 us
    unnamed x30, local copies, waits for them, and re-layouts  7.17 us
    add x5, other arithmetic, ordered_scatter(): values = keep + exchange(send, axis, bit)  6.77 us
  transfers between devices with their start and end apart: 29, of which 20 were waited for; matrix products, arithmetic and copies ran while one was open for 14% of the time, Pallas kernels for 0%

commit v1 on v0

--- a/solution.py
+++ b/solution.py
@@ -85,6 +85,12 @@
     return ranked + [step for step in steps if step not in ranked]
 
 
+def cross_order(steps):
+    by_distance = [("proj", 0), ("cuts", 0), ("proj", 2), ("tile", 0), ("cuts", 1), ("proj", 3), ("tile", 1)]
+    ranked = [step for step in by_distance if step in steps]
+    return ranked + [step for step in steps if step not in ranked]
+
+
 def bit_view(values, steps):
     return values.reshape((2,) * len(steps) + (values.shape[0] >> len(steps),) + values.shape[1:])
 
@@ -126,12 +132,6 @@
         keep = lax.dynamic_slice_in_dim(values, mine * half, half, 0)
         send = lax.dynamic_slice_in_dim(values, (1 - mine) * half, half, 0)
         values = keep + exchange(send, axis, bit)
-    return values
-
-
-def exchange_sum(values, steps):
-    for axis, bit in steps:
-        values = values + exchange(values, axis, bit)
     return values
 
 
@@ -287,30 +287,6 @@
 
     spare = -(-extended.shape[2] // 128) * 128 + 128 - extended.shape[2]
     window = jnp.pad(extended, ((0, 0), (0, 8), (0, spare)))
-    angle_count = ray_weights.shape[0]
-    x_share = volume.shape[1]
-    width = volume.shape[2]
-    onehot = (angle_ids[:, None] == jnp.arange(angle_count, dtype=jnp.int32)[None, :]).astype(
-        jnp.float32
-    )
-    ray_table = jnp.dot(
-        onehot, ray_weights, precision=lax.Precision.HIGHEST, preferred_element_type=jnp.float32
-    )
-    ray_sums = jnp.einsum("zxy,ay->azx", volume, ray_table, precision=lax.Precision.HIGHEST).astype(
-        jnp.bfloat16
-    )
-    spread = onehot.astype(jnp.bfloat16)[:, :, None, None] * ray_sums[:, None, :, :]
-    spread = spread.transpose(1, 3, 0, 2).reshape(
-        angle_count * x_share, ray_sums.shape[0] * ray_sums.shape[1]
-    )
-    weight_flat = proj_weights.reshape(angle_count * x_share, width)
-    partial_term = lax.dot_general(
-        weight_flat, spread, (((0,), (0,)), ((), ())), preferred_element_type=jnp.float32
-    )
-    volume_steps = bit_steps(("tile", "proj"))
-    volume_order = link_order(volume_steps)
-    own_rows = ordered_scatter(partial_term, volume_steps, volume_order)
-    own_rows, window = lax.optimization_barrier((own_rows, window))
     meta = jnp.concatenate([counts[0, :1], pos_rows[0, 0], pos_cols[0, 0]])
     grad_sum, probe_sum, energy_rows = patch_terms_all(
         meta,
@@ -326,10 +302,11 @@
     own_cells = grad_sum[:, :, half_side : half_side + tile_cols]
     own_cells = own_cells.at[:, :, :half_side].add(to_left_edge)
     own_cells = own_cells.at[:, :, tile_cols - half_side :].add(to_right_edge)
-    probe_order = link_order(bit_steps(("proj", "tile", "cuts")))
-    probe_steps, probe_rest = probe_order[:3], probe_order[3:]
+    probe_bits = bit_steps(("proj", "tile", "cuts"))
+    probe_orders = (link_order(probe_bits), cross_order(probe_bits))
     probe_rows = probe_sum.size // 128
-    padded_rows = -(-(probe_rows + 1) // 2 ** len(probe_steps)) * 2 ** len(probe_steps)
+    block_rows = 2 ** (len(probe_bits) + 1)
+    padded_rows = -(-(probe_rows + 1) // block_rows) * block_rows
     probe_flat = jnp.concatenate(
         [
             probe_sum.reshape(probe_rows, 128),
@@ -337,8 +314,13 @@
             jnp.zeros((padded_rows - probe_rows - 1, 128), jnp.float32),
         ]
     )
-    probe_flat = exchange_sum(halving_scatter(probe_flat, probe_steps), probe_rest)
-    probe_flat = doubling_gather(probe_flat, probe_steps)
+    half_rows = padded_rows // 2
+    probe_flat = jnp.concatenate(
+        [
+            doubling_gather(halving_scatter(probe_flat[start : start + half_rows], order), order)
+            for start, order in zip((0, half_rows), probe_orders)
+        ]
+    )
     probe_grad = probe_flat[:probe_rows].reshape(probe_sum.shape)
     energy = probe_flat[probe_rows, 0]
     new_probe = probe_field + probe_grad / (energy + 1e-05)
@@ -365,8 +347,42 @@
         .transpose(2, 0, 1)
         .reshape(u_share, projections * slab_dev)
     )
+    angle_count = ray_weights.shape[0]
+    x_share = volume.shape[1]
+    width = volume.shape[2]
+    onehot = (angle_ids[:, None] == jnp.arange(angle_count, dtype=jnp.int32)[None, :]).astype(
+        jnp.float32
+    )
+    ray_table = jnp.dot(
+        onehot, ray_weights, precision=lax.Precision.HIGHEST, preferred_element_type=jnp.float32
+    )
+    ray_sums = jnp.einsum("zxy,ay->azx", volume, ray_table, precision=lax.Precision.HIGHEST).astype(
+        jnp.bfloat16
+    )
+    spread = onehot.astype(jnp.bfloat16)[:, :, None, None] * ray_sums[:, None, :, :]
+    spread = spread.transpose(1, 3, 0, 2).reshape(angle_count * x_share, projections * slab_dev)
+    weight_flat = proj_weights.reshape(angle_count * x_share, width)
+    partial_term = lax.dot_general(
+        weight_flat, spread, (((0,), (0,)), ((), ())), preferred_element_type=jnp.float32
+    )
+    volume_steps = bit_steps(("tile", "proj"))
+    volume_orders = (link_order(volume_steps), cross_order(volume_steps))
+    half_cols = partial_term.shape[1] // 2
+    own_rows = jnp.concatenate(
+        [
+            ordered_scatter(partial_term[:, start : start + half_cols], volume_steps, order)
+            for start, order in zip((0, half_cols), volume_orders)
+        ],
+        axis=1,
+    )
     own_residue = (own_rows - target).astype(jnp.bfloat16)
-    residue = ordered_gather(own_residue, volume_steps, volume_order)
+    residue = jnp.concatenate(
+        [
+            ordered_gather(own_residue[:, start : start + half_cols], volume_steps, order)
+            for start, order in zip((0, half_cols), volume_orders)
+        ],
+        axis=1,
+    )
     backproj = matmul(weight_flat, residue)
     backproj = backproj.reshape(angle_count, x_share, projections, slab_dev)
     back_sums = jnp.einsum("gxaz,ag->azx", backproj, onehot, precision=lax.Precision.HIGHEST)

time: 284 us -> 339 us (1.19); the launches traced: 282 us -> 332 us
  starting transfers between devices: 72.4 us -> 158 us
  waiting for transfers between devices: 96.7 us -> 62 us
    ppermute x23 -> x56, starting transfers between devices: 33.7 us -> 121 us  [exchange(): lax.ppermute(values, axis, [(source, source ^ 1 << bit) for source in ran...]
    ppermute x23 -> x56, waiting for transfers between devices: 85.3 us -> 58.2 us  [exchange(): lax.ppermute(values, axis, [(source, source ^ 1 << bit) for source in ran...]
    all_to_all x1, starting transfers between devices: 10.6 us -> 22.7 us  [on_device(): lax.all_to_all(slab_values, 'proj', split_axis=2, concat_axis=0, tiled=True)]
    slice x0 -> x5, local copies, waits for them, and re-layouts: none -> 9.28 us  [the longest x3 8.11 us: on_device(): partial_term[:, start:start + half_cols]]
    ppermute x4, starting transfers between devices: 19.4 us -> 11.2 us  [shifted(): lax.ppermute(value, axis, [(source, source + steps) for source in range(l...]
    dot_general x1 -> x0, local copies, waits for them, and re-layouts: 5.38 us -> none  [on_device(): lax.dot_general(weight_flat, spread, (((0,), (0,)), ((), ())), preferred_...]
    all_to_all x1, starting transfers between devices: 8.75 us -> 3.65 us  [on_device(): lax.all_to_all(lax.all_to_all(slab_values, 'proj', split_axis=2, concat_a...]
    all_to_all x1, waiting for transfers between devices: 3.64 us -> 0.01 us  [on_device(): lax.all_to_all(slab_values, 'proj', split_axis=2, concat_axis=0, tiled=True)]
  transfers between devices with their start and end apart: 29 -> 62, of which waited for: 20 -> 34; matrix products, arithmetic and copies ran while one was open for 14% -> 18% of each run, Pallas kernels for 0% -> 3%
where the time goes in v1:
time: 339 us; the launch traced here: 332 us
  starting transfers between devices  158 us (47%)
  waiting for transfers between devices  62 us (18%)
  local copies, waits for them, and re-layouts  44.5 us (13%)
  other arithmetic  36 us (11%)
  matrix products  16.7 us (5%)
  Pallas kernels  11 us (3%)
  between operations  3.66 us (1%)
    ppermute x56, starting transfers between devices, exchange(): lax.ppermute(values, axis, [(source, source ^ 1 << bit) for source in ran...  121 us
    ppermute x56, waiting for transfers between devices, exchange(): lax.ppermute(values, axis, [(source, source ^ 1 << bit) for source in ran...  58.2 us
    all_to_all x1, starting transfers between devices, on_device(): lax.all_to_all(slab_values, 'proj', split_axis=2, concat_axis=0, tiled=True)  22.7 us
    ppermute x4, starting transfers between devices, shifted(): lax.ppermute(value, axis, [(source, source + steps) for source in range(l...  11.2 us
    pallas_call x1, Pallas kernels, patch_terms_all(): pl.pallas_call(patch_kernel, grid_spec=grid_spec, out_shape=[jax.ShapeDty...  11 us
    slice x3, local copies, waits for them, and re-layouts, on_device(): partial_term[:, start:start + half_cols]  8.11 us
  transfers between devices with their start and end apart: 62, of which 34 were waited for; matrix products, arithmetic and copies ran while one was open for 18% of the time, Pallas kernels for 3%

profile of v1, /device:TPU:1, one launch (start us, length us, event | category | flops | bytes accessed | tf_op | source)
XLA Modules:
  0.0 332.1 jit_solution(4476587387957386124)
XLA Ops:
  2.9 3.4 %fusion.7 = bf16[32,64,8]{1,0,2:T(8,128)(2,1)S(1)} fusion(f32[64,2048,1]{1,0,2:T(8,128)S(1)} %convolution_bitcast_fusion.1, f32[8,32,2048]{2,1,0:T(8,128)} %param.22), kind=kOutput, calls=%fused_computation.14 | convolution fusion | flops 402669568 | bytes 2654208 | tf_op jit(solution)/shard_map/zxy,ay->azx/dot_general | solution.py:359
  8.0 3.4 %mul.333 = bf16[512,512]{0,1:T(8,128)(2,1)S(1)} reshape(bf16[16,32,64,8]{1,0,3,2:T(8,128)(2,1)} %broadcast_multiply_fusion) | data formatting | bytes 1048576 | tf_op jit(solution)/shard_map/mul | solution.py:362
  20.2 3.2 collective-permute-start.36
  40.2 3.8 %collective-permute-done.1 = f32[2,384,128]{2,1,0:T(8,128)} collective-permute-done((f32[2,384,128]{2,1,0:T(8,128)}, f32[2,384,128]{2,1,0:T(8,128)}, u32[]{:S(2)}, u32[]{:S(2)}) %collective-permute-start.1) | collective-permute-done | bytes 393248 | tf_op jit(solution)/shard_map/ppermute | solution.py:19
  46.9 11.0 %shard_map.130 = (f32[2,392,896]{2,1,0:T(8,128)}, f32[2,256,256]{2,1,0:T(8,128)}, f32[8,128]{1,0:T(8,128)}) custom-call(s32[13]{0:T(128)} %pad_add_fusion.meta_ref, f32[2,392,896]{2,1,0:T(8,128)} %select_maximum_fusion.window_ref, bf16[6,256,256]{2,1,0:T(8,128)(2,1)} %bitcast.147, f32[2,256,256]{2,1,0:T(8,128)} %probe_ref.1, ...), custom_call_target="tpu_custom_call" | custom-call | tf_op jit(solution)/shard_map/pallas_call | solution.py:249
  59.7 5.5 %collective-permute-start.4 = (f32[384,128]{1,0:T(8,128)}, f32[384,128]{1,0:T(8,128)}, u32[]{:S(2)}, u32[]{:S(2)}) collective-permute-start(f32[384,128]{1,0:T(8,128)} %constant_dynamic-slice_fusion.35), channel_id=1, source_target_pairs={{0,4},{4,0},{8,12},{12,8},{16,20},{20,16},{24,28},{28,24},{32,36},... | collective-permute-start | bytes 589832 | tf_op jit(solution)/shard_map/ppermute | solution.py:125
  69.9 6.3 %collective-permute-start.2 = (f32[2,384,128]{2,1,0:T(8,128)}, f32[2,384,128]{2,1,0:T(8,128)}, u32[]{:S(2)}, u32[]{:S(2)}) collective-permute-start(f32[2,384,128]{2,1,0:T(8,128)} %get-tuple-element.36), channel_id=1, source_target_pairs={{0,64},{64,128},{128,192},{1,65},{65,129},{129,193},{2,66},{66,130... | collective-permute-start | bytes 1179656 | tf_op jit(solution)/shard_map/ppermute | solution.py:19
  79.9 3.1 concatenate.860
  107.2 3.7 %collective-permute-done.8 = f32[24,128]{1,0:T(8,128)S(1)} collective-permute-done((f32[24,128]{1,0:T(8,128)S(1)}, f32[24,128]{1,0:T(8,128)S(1)}, u32[]{:S(2)}, u32[]{:S(2)}) %collective-permute-start.8) | collective-permute-done | bytes 12320 | tf_op jit(solution)/shard_map/ppermute | solution.py:125
  130.1 11.8 %collective-permute-start.11 = (f32[3,128]{1,0:T(4,128)S(1)}, f32[3,128]{1,0:T(4,128)S(1)}, u32[]{:S(2)}, u32[]{:S(2)}) collective-permute-start(f32[3,128]{1,0:T(4,128)S(1)} %constant_dynamic-slice_fusion.24), channel_id=1, source_target_pairs={{0,8},{4,12},{8,0},{12,4},{16,24},{20,28},{24,16},{28,20},{32,40},... | collective-permute-start | bytes 4616 | tf_op jit(solution)/shard_map/ppermute | solution.py:125
  142.9 5.4 %collective-permute-start.27 = (f32[3,128]{1,0:T(4,128)S(1)}, f32[3,128]{1,0:T(4,128)S(1)}, u32[]{:S(2)}, u32[]{:S(2)}) collective-permute-start(f32[3,128]{1,0:T(4,128)S(1)} %constant_dynamic-slice_fusion.12), channel_id=1, source_target_pairs={{0,8},{4,12},{8,0},{12,4},{16,24},{20,28},{24,16},{28,20},{32,40},... | collective-permute-start | bytes 4616 | tf_op jit(solution)/shard_map/ppermute | solution.py:125
  149.2 5.4 %collective-permute-start.12 = (f32[3,128]{1,0:T(4,128)S(1)}, f32[3,128]{1,0:T(4,128)S(1)}, u32[]{:S(2)}, u32[]{:S(2)}) collective-permute-start(f32[3,128]{1,0:T(4,128)S(1)} %fusion.43), channel_id=1, source_target_pairs={{0,8},{4,12},{8,0},{12,4},{16,24},{20,28},{24,16},{28,20},{32,40},... | collective-permute-start | bytes 4616 | tf_op jit(solution)/shard_map/ppermute | solution.py:125
  161.5 22.7 %all-to-all-start = ((f32[16,1,1024]{2,1,0:T(1,128)}), f32[16,1,1024]{2,1,0:T(1,128)S(1)}, u32[]{:S(2)}, u32[]{:S(2)}) async-start(f32[16,1,1024]{2,1,0:T(1,128)} %reshape.2050), calls=%async_computation | async-start | bytes 131072 | tf_op jit(solution)/shard_map/all_to_all | solution.py:333
  217.3 3.6 %all-to-all-start.1 = ((f32[4,1,4096]{2,1,0:T(1,128)}), f32[4,1,4096]{2,1,0:T(1,128)S(1)}, u32[]{:S(2)}, u32[]{:S(2)}) async-start(f32[4,1,4096]{2,1,0:T(1,128)} %reshape.2052), calls=%async_computation.1 | async-start | bytes 131072 | tf_op jit(solution)/shard_map/all_to_all | solution.py:332
  221.9 7.2 %collective-permute-start.19 = (f32[384,128]{1,0:T(8,128)S(1)}, f32[384,128]{1,0:T(8,128)}, u32[]{:S(2)}, u32[]{:S(2)}) collective-permute-start(f32[384,128]{1,0:T(8,128)S(1)} %maximum_select_fusion.10), channel_id=1, source_target_pairs={{0,4},{4,0},{8,12},{12,8},{16,20},{20,16},{24,28},{28,24},{32,36},... | collective-permute-start | bytes 589832 | tf_op jit(solution)/shard_map/ppermute | solution.py:125
  243.3 3.1 collective-permute-start.40
  248.4 5.4 %collective-permute-start.41 = (f32[1,1,1,1,1,1,32,256]{7,6,5,4,3,2,1,0:T(8,128)S(1)}, f32[1,1,1,1,1,1,32,256]{7,6,5,4,3,2,1,0:T(8,128)S(1)}, u32[]{:S(2)}, u32[]{:S(2)}) collective-permute-start(f32[1,1,1,1,1,1,32,256]{7,6,5,4,3,2,1,0:T(8,128)S(1)} %constant_dynamic-slice_fusion.6), channel_id=1, source_target_pairs={{0,8},{4,12},{8,0},{12,4},{16,24},{20,28},{24,16},{28,20},{32,40},... | collective-permute-start | bytes 98312 | tf_op jit(solution)/shard_map/ppermute | solution.py:125
  256.5 4.5 %collective-permute-done.47 = f32[1,1,1,1,1,1,32,256]{7,6,5,4,3,2,1,0:T(8,128)S(1)} collective-permute-done((f32[1,1,1,1,1,1,32,256]{7,6,5,4,3,2,1,0:T(8,128)S(1)}, f32[1,1,1,1,1,1,32,256]{7,6,5,4,3,2,1,0:T(8,128)S(1)}, u32[]{:S(2)}, u32[]{:S(2)}) %collective-permute-start.47) | collective-permute-done | bytes 32800 | tf_op jit(solution)/shard_map/ppermute | solution.py:125
  264.4 8.6 %collective-permute-start.35 = (f32[384,128]{1,0:T(8,128)S(1)}, f32[384,128]{1,0:T(8,128)}, u32[]{:S(2)}, u32[]{:S(2)}) collective-permute-start(f32[384,128]{1,0:T(8,128)S(1)} %maximum_select_fusion.11), channel_id=1, source_target_pairs={{0,4},{4,0},{8,12},{12,8},{16,20},{20,16},{24,28},{28,24},{32,36},... | collective-permute-start | bytes 589832 | tf_op jit(solution)/shard_map/ppermute | solution.py:125
  293.4 3.5 %collective-permute-done.52 = bf16[2,1,2,2,2,1,32,256]{7,6,5,4,3,2,1,0:T(8,128)(2,1)S(1)} collective-permute-done((bf16[2,1,2,2,2,1,32,256]{7,6,5,4,3,2,1,0:T(8,128)(2,1)S(1)}, bf16[2,1,2,2,2,1,32,256]{7,6,5,4,3,2,1,0:T(8,128)(2,1)S(1)}, u32[]{:S(2)}, u32[]{:S(2)}) %collective-permute-start.52) | collective-permute-done | bytes 262176 | tf_op jit(solution)/shard_map/ppermute | solution.py:125
  297.7 4.1 %collective-permute-start.53 = (bf16[2,2,2,2,2,1,32,256]{7,6,5,4,3,2,1,0:T(8,128)(2,1)}, bf16[2,2,2,2,2,1,32,256]{7,6,5,4,3,2,1,0:T(8,128)(2,1)}, u32[]{:S(2)}, u32[]{:S(2)}) collective-permute-start(bf16[2,2,2,2,2,1,32,256]{7,6,5,4,3,2,1,0:T(8,128)(2,1)} %maximum_select_fusion.2), channel_id=1, source_target_pairs={{0,4},{4,0},{8,12},{12,8},{16,20},{20,16},{24,28},{28,24},{32,36},... | collective-permute-start | bytes 1572872 | tf_op jit(solution)/shard_map/ppermute | solution.py:125
  319.5 3.8 %reshape.2046 = f32[16,32,64,8]{1,0,3,2:T(8,128)} reshape(f32[512,512]{0,1:T(8,128)} %fusion.4) | data formatting | bytes 2097152 | tf_op jit(solution)/shard_map/reshape | solution.py:387
  323.2 3.8 %fusion.19 = f32[64,1,32,8]{2,1,3,0:T(1,128)S(1)} fusion(f32[16,32,64,8]{1,0,3,2:T(8,128)} %reshape.2046, pred[64,16,1,1]{1,0,2,3:T(32,128)(4,1)S(1)} %fusion.27), kind=kOutput, calls=%fused_computation.74 | convolution fusion | flops 3145728 | bytes 1115136 | tf_op jit(solution)/shard_map/gxaz,ag->azx/dot_general | solution.py:388
  327.1 4.7 %convolution_subtract_fusion = f32[8,32,2048]{2,1,0:T(8,128)} fusion(f32[8,32,2048]{2,1,0:T(8,128)} %param.22, f32[64,2048,1]{1,0,2:T(8,128)S(1)} %convolution_bitcast_fusion.1, f32[64,1,32,8]{0,2,3,1:T(8,128)S(1)} %copy.105), kind=kOutput, calls=%fused_computation.5 | convolution fusion | flops 403177472 | bytes 4784128 | tf_op jit(solution)/shard_map/azx,ay->zxy/dot_general | solution.py:389
  (285 shorter events, 187.7 us)
Async XLA Ops:
  20.2 189.0 %collective-permute-start.36 = (f32[2,2,2,2,2,1,32,256]{7,6,5,4,3,2,1,0:T(8,128)}, f32[2,2,2,2,2,1,32,256]{7,6,5,4,3,2,1,0:T(8,128)}, u32[]{:S(2)}, u32[]{:S(2)}) collective-permute-start(f32[2,2,2,2,2,1,32,256]{7,6,5,4,3,2,1,0:T(8,128)} %constant_dynamic-slice_fusion.11), channel_id=1, source_target_pairs={{0,4},{4,0},{8,12},{12,8},{16,20},{20,16},{24,28},{28,24},{32,36},... | collective-permute-start | bytes 3145736 | tf_op jit(solution)/shard_map/ppermute | solution.py:125
  28.8 184.2 %collective-permute-start.42 = (f32[2,2,2,2,2,1,32,256]{7,6,5,4,3,2,1,0:T(8,128)}, f32[2,2,2,2,2,1,32,256]{7,6,5,4,3,2,1,0:T(8,128)}, u32[]{:S(2)}, u32[]{:S(2)}) collective-permute-start(f32[2,2,2,2,2,1,32,256]{7,6,5,4,3,2,1,0:T(8,128)} %constant_dynamic-slice_fusion.5), channel_id=1, source_target_pairs={{0,4},{4,0},{8,12},{12,8},{16,20},{20,16},{24,28},{28,24},{32,36},... | collective-permute-start | bytes 3145736 | tf_op jit(solution)/shard_map/ppermute | solution.py:125
  29.8 10.5 %collective-permute-start = (f32[2,384,128]{2,1,0:T(8,128)}, f32[2,384,128]{2,1,0:T(8,128)}, u32[]{:S(2)}, u32[]{:S(2)}) collective-permute-start(f32[2,384,128]{2,1,0:T(8,128)} %get-tuple-element.37), channel_id=1, source_target_pairs={{0,64},{64,128},{128,192},{1,65},{65,129},{129,193},{2,66},{66,130... | collective-permute-start | bytes 1179656 | tf_op jit(solution)/shard_map/ppermute | solution.py:19
  32.0 12.1 %collective-permute-start.1 = (f32[2,384,128]{2,1,0:T(8,128)}, f32[2,384,128]{2,1,0:T(8,128)}, u32[]{:S(2)}, u32[]{:S(2)}) collective-permute-start(f32[2,384,128]{2,1,0:T(8,128)} %get-tuple-element.38), channel_id=1, source_target_pairs={{64,0},{128,64},{192,128},{65,1},{129,65},{193,129},{66,2},{130,66... | collective-permute-start | bytes 1179656 | tf_op jit(solution)/shard_map/ppermute | solution.py:19
  59.7 24.5 %collective-permute-start.4 = (f32[384,128]{1,0:T(8,128)}, f32[384,128]{1,0:T(8,128)}, u32[]{:S(2)}, u32[]{:S(2)}) collective-permute-start(f32[384,128]{1,0:T(8,128)} %constant_dynamic-slice_fusion.35), channel_id=1, source_target_pairs={{0,4},{4,0},{8,12},{12,8},{16,20},{20,16},{24,28},{28,24},{32,36},... | collective-permute-start | bytes 589832 | tf_op jit(solution)/shard_map/ppermute | solution.py:125
  69.9 84.7 %collective-permute-start.2 = (f32[2,384,128]{2,1,0:T(8,128)}, f32[2,384,128]{2,1,0:T(8,128)}, u32[]{:S(2)}, u32[]{:S(2)}) collective-permute-start(f32[2,384,128]{2,1,0:T(8,128)} %get-tuple-element.36), channel_id=1, source_target_pairs={{0,64},{64,128},{128,192},{1,65},{65,129},{129,193},{2,66},{66,130... | collective-permute-start | bytes 1179656 | tf_op jit(solution)/shard_map/ppermute | solution.py:19
  76.2 79.7 %collective-permute-start.3 = (f32[2,384,128]{2,1,0:T(8,128)}, f32[2,384,128]{2,1,0:T(8,128)}, u32[]{:S(2)}, u32[]{:S(2)}) collective-permute-start(f32[2,384,128]{2,1,0:T(8,128)} %get-tuple-element.35), channel_id=1, source_target_pairs={{64,0},{128,64},{192,128},{65,1},{129,65},{193,129},{66,2},{130,66... | collective-permute-start | bytes 1179656 | tf_op jit(solution)/shard_map/ppermute | solution.py:19
  130.1 12.8 %collective-permute-start.11 = (f32[3,128]{1,0:T(4,128)S(1)}, f32[3,128]{1,0:T(4,128)S(1)}, u32[]{:S(2)}, u32[]{:S(2)}) collective-permute-start(f32[3,128]{1,0:T(4,128)S(1)} %constant_dynamic-slice_fusion.24), channel_id=1, source_target_pairs={{0,8},{4,12},{8,0},{12,4},{16,24},{20,28},{24,16},{28,20},{32,40},... | collective-permute-start | bytes 4616 | tf_op jit(solution)/shard_map/ppermute | solution.py:125
  149.2 35.0 %collective-permute-start.12 = (f32[3,128]{1,0:T(4,128)S(1)}, f32[3,128]{1,0:T(4,128)S(1)}, u32[]{:S(2)}, u32[]{:S(2)}) collective-permute-start(f32[3,128]{1,0:T(4,128)S(1)} %fusion.43), channel_id=1, source_target_pairs={{0,8},{4,12},{8,0},{12,4},{16,24},{20,28},{24,16},{28,20},{32,40},... | collective-permute-start | bytes 4616 | tf_op jit(solution)/shard_map/ppermute | solution.py:125
  154.6 32.6 %collective-permute-start.28 = (f32[3,128]{1,0:T(4,128)S(1)}, f32[3,128]{1,0:T(4,128)S(1)}, u32[]{:S(2)}, u32[]{:S(2)}) collective-permute-start(f32[3,128]{1,0:T(4,128)S(1)} %fusion.44), channel_id=1, source_target_pairs={{0,8},{4,12},{8,0},{12,4},{16,24},{20,28},{24,16},{28,20},{32,40},... | collective-permute-start | bytes 4616 | tf_op jit(solution)/shard_map/ppermute | solution.py:125
  161.5 46.2 %all-to-all-start = ((f32[16,1,1024]{2,1,0:T(1,128)}), f32[16,1,1024]{2,1,0:T(1,128)S(1)}, u32[]{:S(2)}, u32[]{:S(2)}) async-start(f32[16,1,1024]{2,1,0:T(1,128)} %reshape.2050), calls=%async_computation | async-start | bytes 131072 | tf_op jit(solution)/shard_map/all_to_all | solution.py:333
  204.7 16.2 %collective-permute-start.18 = (f32[192,128]{1,0:T(8,128)S(1)}, f32[192,128]{1,0:T(8,128)}, u32[]{:S(2)}, u32[]{:S(2)}) collective-permute-start(f32[192,128]{1,0:T(8,128)S(1)} %maximum_select_fusion.16), channel_id=1, source_target_pairs={{0,64},{64,0},{128,192},{192,128},{1,65},{65,1},{129,193},{193,129... | collective-permute-start | bytes 294920 | tf_op jit(solution)/shard_map/ppermute | solution.py:125
  206.5 57.0 %collective-permute-start.34 = (f32[192,128]{1,0:T(8,128)S(1)}, f32[192,128]{1,0:T(8,128)}, u32[]{:S(2)}, u32[]{:S(2)}) collective-permute-start(f32[192,128]{1,0:T(8,128)S(1)} %maximum_select_fusion.17), channel_id=1, source_target_pairs={{0,1},{1,0},{2,3},{3,2},{4,5},{5,4},{6,7},{7,6},{8,9},{9,8},{10,11... | collective-permute-start | bytes 294920 | tf_op jit(solution)/shard_map/ppermute | solution.py:125
  212.0 18.3 %collective-permute-start.37 = (f32[2,1,2,2,2,1,32,256]{7,6,5,4,3,2,1,0:T(8,128)}, f32[2,1,2,2,2,1,32,256]{7,6,5,4,3,2,1,0:T(8,128)}, u32[]{:S(2)}, u32[]{:S(2)}) collective-permute-start(f32[2,1,2,2,2,1,32,256]{7,6,5,4,3,2,1,0:T(8,128)} %constant_dynamic-slice_fusion.10), channel_id=1, source_target_pairs={{0,64},{64,0},{128,192},{192,128},{1,65},{65,1},{129,193},{193,129... | collective-permute-start | bytes 1572872 | tf_op jit(solution)/shard_map/ppermute | solution.py:125
  216.2 16.9 %collective-permute-start.43 = (f32[2,2,2,1,2,1,32,256]{7,6,5,4,3,2,1,0:T(8,128)}, f32[2,2,2,1,2,1,32,256]{7,6,5,4,3,2,1,0:T(8,128)}, u32[]{:S(2)}, u32[]{:S(2)}) collective-permute-start(f32[2,2,2,1,2,1,32,256]{7,6,5,4,3,2,1,0:T(8,128)} %constant_dynamic-slice_fusion.4), channel_id=1, source_target_pairs={{0,16},{4,20},{8,24},{12,28},{16,0},{20,4},{24,8},{28,12},{32,48},... | collective-permute-start | bytes 1572872 | tf_op jit(solution)/shard_map/ppermute | solution.py:125
  217.3 11.8 %all-to-all-start.1 = ((f32[4,1,4096]{2,1,0:T(1,128)}), f32[4,1,4096]{2,1,0:T(1,128)S(1)}, u32[]{:S(2)}, u32[]{:S(2)}) async-start(f32[4,1,4096]{2,1,0:T(1,128)} %reshape.2052), calls=%async_computation.1 | async-start | bytes 131072 | tf_op jit(solution)/shard_map/all_to_all | solution.py:332
  221.9 86.0 %collective-permute-start.19 = (f32[384,128]{1,0:T(8,128)S(1)}, f32[384,128]{1,0:T(8,128)}, u32[]{:S(2)}, u32[]{:S(2)}) collective-permute-start(f32[384,128]{1,0:T(8,128)S(1)} %maximum_select_fusion.10), channel_id=1, source_target_pairs={{0,4},{4,0},{8,12},{12,8},{16,20},{20,16},{24,28},{28,24},{32,36},... | collective-permute-start | bytes 589832 | tf_op jit(solution)/shard_map/ppermute | solution.py:125
  246.5 7.3 %collective-permute-start.46 = (f32[1,1,1,1,2,1,32,256]{7,6,5,4,3,2,1,0:T(8,128)S(1)}, f32[1,1,1,1,2,1,32,256]{7,6,5,4,3,2,1,0:T(8,128)S(1)}, u32[]{:S(2)}, u32[]{:S(2)}) collective-permute-start(f32[1,1,1,1,2,1,32,256]{7,6,5,4,3,2,1,0:T(8,128)S(1)} %constant_dynamic-slice_fusion.1), channel_id=1, source_target_pairs={{0,128},{64,192},{128,0},{192,64},{1,129},{65,193},{129,1},{193,65... | collective-permute-start | bytes 196616 | tf_op jit(solution)/shard_map/ppermute | solution.py:125
  248.4 8.1 %collective-permute-start.41 = (f32[1,1,1,1,1,1,32,256]{7,6,5,4,3,2,1,0:T(8,128)S(1)}, f32[1,1,1,1,1,1,32,256]{7,6,5,4,3,2,1,0:T(8,128)S(1)}, u32[]{:S(2)}, u32[]{:S(2)}) collective-permute-start(f32[1,1,1,1,1,1,32,256]{7,6,5,4,3,2,1,0:T(8,128)S(1)} %constant_dynamic-slice_fusion.6), channel_id=1, source_target_pairs={{0,8},{4,12},{8,0},{12,4},{16,24},{20,28},{24,16},{28,20},{32,40},... | collective-permute-start | bytes 98312 | tf_op jit(solution)/shard_map/ppermute | solution.py:125
  261.1 14.7 %collective-permute-start.48 = (bf16[1,1,1,1,1,1,32,256]{7,6,5,4,3,2,1,0:T(8,128)(2,1)S(1)}, bf16[1,1,1,1,1,1,32,256]{7,6,5,4,3,2,1,0:T(8,128)(2,1)S(1)}, u32[]{:S(2)}, u32[]{:S(2)}) collective-permute-start(bf16[1,1,1,1,1,1,32,256]{7,6,5,4,3,2,1,0:T(8,128)(2,1)S(1)} %get-tuple-element.63), channel_id=1, source_target_pairs={{0,8},{4,12},{8,0},{12,4},{16,24},{20,28},{24,16},{28,20},{32,40},... | collective-permute-start | bytes 49160 | tf_op jit(solution)/shard_map/ppermute | solution.py:125
  264.4 41.3 %collective-permute-start.35 = (f32[384,128]{1,0:T(8,128)S(1)}, f32[384,128]{1,0:T(8,128)}, u32[]{:S(2)}, u32[]{:S(2)}) collective-permute-start(f32[384,128]{1,0:T(8,128)S(1)} %maximum_select_fusion.11), channel_id=1, source_target_pairs={{0,4},{4,0},{8,12},{12,8},{16,20},{20,16},{24,28},{28,24},{32,36},... | collective-permute-start | bytes 589832 | tf_op jit(solution)/shard_map/ppermute | solution.py:125
  293.0 8.8 %collective-permute-start.58 = (bf16[2,2,2,1,2,1,32,256]{7,6,5,4,3,2,1,0:T(8,128)(2,1)S(1)}, bf16[2,2,2,1,2,1,32,256]{7,6,5,4,3,2,1,0:T(8,128)(2,1)S(1)}, u32[]{:S(2)}, u32[]{:S(2)}) collective-permute-start(bf16[2,2,2,1,2,1,32,256]{7,6,5,4,3,2,1,0:T(8,128)(2,1)S(1)} %maximum_select_fusion.9), channel_id=1, source_target_pairs={{0,16},{4,20},{8,24},{12,28},{16,0},{20,4},{24,8},{28,12},{32,48},... | collective-permute-start | bytes 786440 | tf_op jit(solution)/shard_map/ppermute | solution.py:125
  297.7 16.0 %collective-permute-start.53 = (bf16[2,2,2,2,2,1,32,256]{7,6,5,4,3,2,1,0:T(8,128)(2,1)}, bf16[2,2,2,2,2,1,32,256]{7,6,5,4,3,2,1,0:T(8,128)(2,1)}, u32[]{:S(2)}, u32[]{:S(2)}) collective-permute-start(bf16[2,2,2,2,2,1,32,256]{7,6,5,4,3,2,1,0:T(8,128)(2,1)} %maximum_select_fusion.2), channel_id=1, source_target_pairs={{0,4},{4,0},{8,12},{12,8},{16,20},{20,16},{24,28},{28,24},{32,36},... | collective-permute-start | bytes 1572872 | tf_op jit(solution)/shard_map/ppermute | solution.py:125
  302.8 12.7 %collective-permute-start.59 = (bf16[2,2,2,2,2,1,32,256]{7,6,5,4,3,2,1,0:T(8,128)(2,1)}, bf16[2,2,2,2,2,1,32,256]{7,6,5,4,3,2,1,0:T(8,128)(2,1)}, u32[]{:S(2)}, u32[]{:S(2)}) collective-permute-start(bf16[2,2,2,2,2,1,32,256]{7,6,5,4,3,2,1,0:T(8,128)(2,1)} %maximum_select_fusion.3), channel_id=1, source_target_pairs={{0,4},{4,0},{8,12},{12,8},{16,20},{20,16},{24,28},{28,24},{32,36},... | collective-permute-start | bytes 1572872 | tf_op jit(solution)/shard_map/ppermute | solution.py:125
  (56 other events, 427.5 us)

commit v2 on v1

--- a/solution.py
+++ b/solution.py
@@ -85,12 +85,6 @@
     return ranked + [step for step in steps if step not in ranked]
 
 
-def cross_order(steps):
-    by_distance = [("proj", 0), ("cuts", 0), ("proj", 2), ("tile", 0), ("cuts", 1), ("proj", 3), ("tile", 1)]
-    ranked = [step for step in by_distance if step in steps]
-    return ranked + [step for step in steps if step not in ranked]
-
-
 def bit_view(values, steps):
     return values.reshape((2,) * len(steps) + (values.shape[0] >> len(steps),) + values.shape[1:])
 
@@ -125,6 +119,32 @@
     return lax.ppermute(values, axis, [(source, source ^ (1 << bit)) for source in range(count)])
 
 
+def halving_step(values, axis, bit):
+    mine = (lax.axis_index(axis) >> bit) & 1
+    half = values.shape[0] // 2
+    keep = lax.dynamic_slice_in_dim(values, mine * half, half, 0)
+    send = lax.dynamic_slice_in_dim(values, (1 - mine) * half, half, 0)
+    return keep + exchange(send, axis, bit)
+
+
+def doubling_step(values, axis, bit, place=0):
+    mine = (lax.axis_index(axis) >> bit) & 1
+    other = exchange(values, axis, bit)
+    return jnp.where(
+        mine == 0,
+        jnp.concatenate([values, other], axis=place),
+        jnp.concatenate([other, values], axis=place),
+    )
+
+
+def probe_ops(first, rest):
+    return (
+        [lambda values, step=step: halving_step(values, *step) for step in first]
+        + [lambda values, step=step: values + exchange(values, *step) for step in rest]
+        + [lambda values, step=step: doubling_step(values, *step) for step in reversed(first)]
+    )
+
+
 def halving_scatter(values, steps):
     for axis, bit in steps:
         mine = (lax.axis_index(axis) >> bit) & 1
@@ -132,6 +152,12 @@
         keep = lax.dynamic_slice_in_dim(values, mine * half, half, 0)
         send = lax.dynamic_slice_in_dim(values, (1 - mine) * half, half, 0)
         values = keep + exchange(send, axis, bit)
+    return values
+
+
+def exchange_sum(values, steps):
+    for axis, bit in steps:
+        values = values + exchange(values, axis, bit)
     return values
 
 
@@ -302,11 +328,10 @@
     own_cells = grad_sum[:, :, half_side : half_side + tile_cols]
     own_cells = own_cells.at[:, :, :half_side].add(to_left_edge)
     own_cells = own_cells.at[:, :, tile_cols - half_side :].add(to_right_edge)
-    probe_bits = bit_steps(("proj", "tile", "cuts"))
-    probe_orders = (link_order(probe_bits), cross_order(probe_bits))
+    probe_order = link_order(bit_steps(("proj", "tile", "cuts")))
+    probe_steps, probe_rest = probe_order[:3], probe_order[3:]
     probe_rows = probe_sum.size // 128
-    block_rows = 2 ** (len(probe_bits) + 1)
-    padded_rows = -(-(probe_rows + 1) // block_rows) * block_rows
+    padded_rows = -(-(probe_rows + 1) // 2 ** len(probe_steps)) * 2 ** len(probe_steps)
     probe_flat = jnp.concatenate(
         [
             probe_sum.reshape(probe_rows, 128),
@@ -314,16 +339,7 @@
             jnp.zeros((padded_rows - probe_rows - 1, 128), jnp.float32),
         ]
     )
-    half_rows = padded_rows // 2
-    probe_flat = jnp.concatenate(
-        [
-            doubling_gather(halving_scatter(probe_flat[start : start + half_rows], order), order)
-            for start, order in zip((0, half_rows), probe_orders)
-        ]
-    )
-    probe_grad = probe_flat[:probe_rows].reshape(probe_sum.shape)
-    energy = probe_flat[probe_rows, 0]
-    new_probe = probe_field + probe_grad / (energy + 1e-05)
+    probe_chain = probe_ops(probe_steps, probe_rest)
     probe_peak = jnp.max(probe_real * probe_real + probe_imag * probe_imag)
     new_object = (own_object + own_cells / (probe_peak + 1e-05))[None]
     slab_total = admm_dual.shape[1]
@@ -366,23 +382,25 @@
         weight_flat, spread, (((0,), (0,)), ((), ())), preferred_element_type=jnp.float32
     )
     volume_steps = bit_steps(("tile", "proj"))
-    volume_orders = (link_order(volume_steps), cross_order(volume_steps))
-    half_cols = partial_term.shape[1] // 2
-    own_rows = jnp.concatenate(
-        [
-            ordered_scatter(partial_term[:, start : start + half_cols], volume_steps, order)
-            for start, order in zip((0, half_cols), volume_orders)
-        ],
-        axis=1,
-    )
+    volume_order = link_order(volume_steps)
+    own_rows = ordered_scatter(partial_term, volume_steps, volume_order)
     own_residue = (own_rows - target).astype(jnp.bfloat16)
-    residue = jnp.concatenate(
-        [
-            ordered_gather(own_residue[:, start : start + half_cols], volume_steps, order)
-            for start, order in zip((0, half_cols), volume_orders)
-        ],
-        axis=1,
-    )
+    gather_chain = [
+        lambda values, step=step: doubling_step(values, *step, place=volume_steps.index(step))
+        for step in reversed(volume_order)
+    ]
+    lead = len(probe_chain) - len(gather_chain)
+    for operation in probe_chain[:lead]:
+        probe_flat = operation(probe_flat)
+    residue = own_residue.reshape((1,) * len(volume_steps) + own_residue.shape)
+    for probe_op, gather_op in zip(probe_chain[lead:], gather_chain):
+        probe_flat, residue = lax.optimization_barrier((probe_flat, residue))
+        probe_flat = probe_op(probe_flat)
+        residue = gather_op(residue)
+    residue = residue.reshape((-1,) + residue.shape[len(volume_steps) + 1 :])
+    probe_grad = probe_flat[:probe_rows].reshape(probe_sum.shape)
+    energy = probe_flat[probe_rows, 0]
+    new_probe = probe_field + probe_grad / (energy + 1e-05)
     backproj = matmul(weight_flat, residue)
     backproj = backproj.reshape(angle_count, x_share, projections, slab_dev)
     back_sums = jnp.einsum("gxaz,ag->azx", backproj, onehot, precision=lax.Precision.HIGHEST)

time: 339 us -> 268 us (0.79); the launches traced: 332 us -> 266 us
  starting transfers between devices: 158 us -> 76.8 us
  other arithmetic: 36 us -> 45.6 us
  Pallas kernels: 11 us -> 14.8 us
    ppermute x56 -> x23, starting transfers between devices: 121 us -> 47.5 us  [exchange(): lax.ppermute(values, axis, [(source, source ^ 1 << bit) for source in ran...]
    ppermute x56 -> x23, waiting for transfers between devices: 58.2 us -> 31.6 us  [exchange(): lax.ppermute(values, axis, [(source, source ^ 1 << bit) for source in ran...]
    ppermute x4, waiting for transfers between devices: 3.79 us -> 24.2 us  [shifted(): lax.ppermute(value, axis, [(source, source + steps) for source in range(l...]
    all_to_all x1, starting transfers between devices: 22.7 us -> 13.2 us  [on_device(): lax.all_to_all(slab_values, 'proj', split_axis=2, concat_axis=0, tiled=True)]
    slice x5 -> x0, local copies, waits for them, and re-layouts: 9.28 us -> none  [the longest x3 8.11 us: on_device(): partial_term[:, start:start + half_cols]]
    all_to_all x1, waiting for transfers between devices: 0.01 us -> 6.81 us  [on_device(): lax.all_to_all(slab_values, 'proj', split_axis=2, concat_axis=0, tiled=True)]
    dot_general x0 -> x1, local copies, waits for them, and re-layouts: none -> 5.38 us  [on_device(): lax.dot_general(weight_flat, spread, (((0,), (0,)), ((), ())), preferred_...]
    add x16 -> x8, other arithmetic: 1.07 us -> 5.66 us  [the longest x5 3.11 us: probe_ops(): values + exchange(values, *step)]
  transfers between devices with their start and end apart: 62 -> 29, of which waited for: 34 -> 15; matrix products, arithmetic and copies ran while one was open for 18% -> 22% of each run, Pallas kernels for 3% -> 6%
where the time goes in v2:
time: 268 us; the launch traced here: 266 us
  starting transfers between devices  76.8 us (29%)
  waiting for transfers between devices  62.5 us (23%)
  other arithmetic  45.6 us (17%)
  local copies, waits for them, and re-layouts  44.3 us (17%)
  matrix products  18.7 us (7%)
  Pallas kernels  14.8 us (6%)
  between operations  3 us (1%)
    ppermute x23, starting transfers between devices, exchange(): lax.ppermute(values, axis, [(source, source ^ 1 << bit) for source in ran...  47.5 us
    ppermute x23, waiting for transfers between devices, exchange(): lax.ppermute(values, axis, [(source, source ^ 1 << bit) for source in ran...  31.6 us
    ppermute x4, waiting for transfers between devices, shifted(): lax.ppermute(value, axis, [(source, source + steps) for source in range(l...  24.2 us
    pallas_call x1, Pallas kernels, patch_terms_all(): pl.pallas_call(patch_kernel, grid_spec=grid_spec, out_shape=[jax.ShapeDty...  14.8 us
    all_to_all x1, starting transfers between devices, on_device(): lax.all_to_all(slab_values, 'proj', split_axis=2, concat_axis=0, tiled=True)  13.2 us
    select_n x9, other arithmetic, doubling_step(): jnp.where(mine == 0, jnp.concatenate([values, other], axis=place), jnp.co...  12.3 us
    unnamed x36, local copies, waits for them, and re-layouts  8.32 us
    ppermute x4, starting transfers between devices, shifted(): lax.ppermute(value, axis, [(source, source + steps) for source in range(l...  8.27 us
  transfers between devices with their start and end apart: 29, of which 15 were waited for; matrix products, arithmetic and copies ran while one was open for 22% of the time, Pallas kernels for 6%

profile of v2, /device:TPU:1, one launch (start us, length us, event | category | flops | bytes accessed | tf_op | source)
XLA Modules:
  0.0 265.8 jit_solution(10111041882935811880)
XLA Ops:
  2.9 3.4 %fusion = bf16[32,64,8]{1,0,2:T(8,128)(2,1)S(1)} fusion(f32[64,2048,1]{1,0,2:T(8,128)S(1)} %convolution_bitcast_fusion.1, f32[8,32,2048]{2,1,0:T(8,128)} %param.22), kind=kOutput, calls=%fused_computation.12 | convolution fusion | flops 402669568 | bytes 2654208 | tf_op jit(solution)/shard_map/zxy,ay->azx/dot_general | solution.py:375
  8.0 3.4 %mul.241 = bf16[512,512]{0,1:T(8,128)(2,1)S(1)} reshape(bf16[16,32,64,8]{1,0,3,2:T(8,128)(2,1)} %broadcast_multiply_fusion) | data formatting | bytes 1048576 | tf_op jit(solution)/shard_map/mul | solution.py:378
  11.4 3.3 %convolution_bitcast_fusion = f32[2048,512]{0,1:T(8,128)} fusion(bf16[512,512]{0,1:T(8,128)(2,1)S(1)} %mul.241, bf16[512,2048]{1,0:T(8,128)(2,1)S(1)} %bitcast.63), kind=kOutput, calls=%fused_computation | convolution fusion | flops 1073741824 | bytes 6815744 | tf_op jit(solution)/shard_map/dot_general | solution.py:381
  14.6 5.4 %copy.24 = f32[2048,512]{1,0:T(8,128)} copy(f32[2048,512]{0,1:T(8,128)} %convolution_bitcast_fusion) | data formatting | bytes 8388608 | tf_op jit(solution)/shard_map/dot_general | solution.py:381
  20.0 3.3 %constant_dynamic-slice_fusion.5 = f32[2,2,2,2,2,1,32,512]{7,6,5,4,3,2,1,0:T(8,128)} fusion(f32[2,2,2,2,2,2,32,512]{7,6,5,4,3,2,1,0:T(8,128)} %bitcast.65, s32[]{:T(128)S(6)} %select_n.224), kind=kLoop, calls=%fused_computation.70 | loop fusion | bytes 4194308 | tf_op jit(solution)/shard_map/dynamic_slice | solution.py:98
  23.3 3.2 %collective-permute-start.9 = (f32[2,2,2,2,2,1,32,512]{7,6,5,4,3,2,1,0:T(8,128)}, f32[2,2,2,2,2,1,32,512]{7,6,5,4,3,2,1,0:T(8,128)}, u32[]{:S(2)}, u32[]{:S(2)}) collective-permute-start(f32[2,2,2,2,2,1,32,512]{7,6,5,4,3,2,1,0:T(8,128)} %constant_dynamic-slice_fusion.5), channel_id=1, source_target_pairs={{0,4},{4,0},{8,12},{12,8},{16,20},{20,16},{24,28},{28,24},{32,36},... | collective-permute-start | bytes 6291464 | tf_op jit(solution)/shard_map/ppermute | solution.py:119
  37.8 3.8 %collective-permute-done.1 = f32[2,384,128]{2,1,0:T(8,128)} collective-permute-done((f32[2,384,128]{2,1,0:T(8,128)}, f32[2,384,128]{2,1,0:T(8,128)}, u32[]{:S(2)}, u32[]{:S(2)}) %collective-permute-start.1) | collective-permute-done | bytes 393248 | tf_op jit(solution)/shard_map/ppermute | solution.py:19
  44.5 14.8 %shard_map.130 = (f32[2,392,896]{2,1,0:T(8,128)}, f32[2,256,256]{2,1,0:T(8,128)}, f32[8,128]{1,0:T(8,128)}) custom-call(s32[13]{0:T(128)} %pad_add_fusion.meta_ref, f32[2,392,896]{2,1,0:T(8,128)} %select_maximum_fusion.window_ref, bf16[6,256,256]{2,1,0:T(8,128)(2,1)} %bitcast.74, f32[2,256,256]{2,1,0:T(8,128)} %probe_ref.1, ...), custom_call_target="tpu_custom_call" | custom-call | tf_op jit(solution)/shard_map/pallas_call | solution.py:275
  73.7 3.9 %collective-permute-start.2 = (f32[2,384,128]{2,1,0:T(8,128)}, f32[2,384,128]{2,1,0:T(8,128)}, u32[]{:S(2)}, u32[]{:S(2)}) collective-permute-start(f32[2,384,128]{2,1,0:T(8,128)} %get-tuple-element.58), channel_id=1, source_target_pairs={{0,64},{64,128},{128,192},{1,65},{65,129},{129,193},{2,66},{66,130... | collective-permute-start | bytes 1179656 | tf_op jit(solution)/shard_map/ppermute | solution.py:19
  85.2 17.3 %collective-permute-done.2 = f32[2,384,128]{2,1,0:T(8,128)} collective-permute-done((f32[2,384,128]{2,1,0:T(8,128)}, f32[2,384,128]{2,1,0:T(8,128)}, u32[]{:S(2)}, u32[]{:S(2)}) %collective-permute-start.2) | collective-permute-done | bytes 393248 | tf_op jit(solution)/shard_map/ppermute | solution.py:19
  106.7 4.4 %collective-permute-start.11 = (f32[2,1,2,1,2,1,32,512]{7,6,5,4,3,2,1,0:T(8,128)S(1)}, f32[2,1,2,1,2,1,32,512]{7,6,5,4,3,2,1,0:T(8,128)S(1)}, u32[]{:S(2)}, u32[]{:S(2)}) collective-permute-start(f32[2,1,2,1,2,1,32,512]{7,6,5,4,3,2,1,0:T(8,128)S(1)} %constant_dynamic-slice_fusion.3), channel_id=1, source_target_pairs={{0,16},{4,20},{8,24},{12,28},{16,0},{20,4},{24,8},{28,12},{32,48},... | collective-permute-start | bytes 1572872 | tf_op jit(solution)/shard_map/ppermute | solution.py:119
  114.2 8.0 %collective-permute-done.11 = f32[2,1,2,1,2,1,32,512]{7,6,5,4,3,2,1,0:T(8,128)S(1)} collective-permute-done((f32[2,1,2,1,2,1,32,512]{7,6,5,4,3,2,1,0:T(8,128)S(1)}, f32[2,1,2,1,2,1,32,512]{7,6,5,4,3,2,1,0:T(8,128)S(1)}, u32[]{:S(2)}, u32[]{:S(2)}) %collective-permute-start.11) | collective-permute-done | bytes 524320 | tf_op jit(solution)/shard_map/ppermute | solution.py:119
  132.5 13.2 %all-to-all-start = ((f32[16,1,1024]{2,1,0:T(1,128)}), f32[16,1,1024]{2,1,0:T(1,128)S(1)}, u32[]{:S(2)}, u32[]{:S(2)}) async-start(f32[16,1,1024]{2,1,0:T(1,128)} %reshape.417), calls=%async_computation | async-start | bytes 131072 | tf_op jit(solution)/shard_map/all_to_all | solution.py:349
  148.6 6.8 %all-to-all-done = f32[16,1,1024]{2,1,0:T(1,128)S(1)} async-done(((f32[16,1,1024]{2,1,0:T(1,128)}), f32[16,1,1024]{2,1,0:T(1,128)S(1)}, u32[]{:S(2)}, u32[]{:S(2)}) %all-to-all-start) | async-done | bytes 65568 | tf_op jit(solution)/shard_map/all_to_all | solution.py:349
  162.0 7.9 %all-to-all-start.1 = ((f32[4,1,4096]{2,1,0:T(1,128)}), f32[4,1,4096]{2,1,0:T(1,128)S(1)}, u32[]{:S(2)}, u32[]{:S(2)}) async-start(f32[4,1,4096]{2,1,0:T(1,128)} %reshape.419), calls=%async_computation.1 | async-start | bytes 131072 | tf_op jit(solution)/shard_map/all_to_all | solution.py:348
  170.8 3.3 %collective-permute-start.8 = (f32[129,128]{1,0:T(8,128)S(1)}, f32[129,128]{1,0:T(8,128)S(1)}, u32[]{:S(2)}, u32[]{:S(2)}) collective-permute-start(f32[129,128]{1,0:T(8,128)S(1)} %add.191), channel_id=1, source_target_pairs={{0,128},{64,192},{128,0},{192,64},{1,129},{65,193},{129,1},{193,65... | collective-permute-start | bytes 198152 | tf_op jit(solution)/shard_map/ppermute | solution.py:119
  184.0 3.0 %collective-permute-start.16 = (bf16[1,1,1,1,1,1,32,512]{7,6,5,4,3,2,1,0:T(8,128)(2,1)S(1)}, bf16[1,1,1,1,1,1,32,512]{7,6,5,4,3,2,1,0:T(8,128)(2,1)S(1)}, u32[]{:S(2)}, u32[]{:S(2)}) collective-permute-start(bf16[1,1,1,1,1,1,32,512]{7,6,5,4,3,2,1,0:T(8,128)(2,1)S(1)} %subtract_convert_fusion), channel_id=1, source_target_pairs={{0,8},{4,12},{8,0},{12,4},{16,24},{20,28},{24,16},{28,20},{32,40},... | collective-permute-start | bytes 98312 | tf_op jit(solution)/shard_map/ppermute | solution.py:119
  199.6 3.5 %collective-permute-start.19 = (f32[129,128]{1,0:T(8,128)S(1)}, f32[129,128]{1,0:T(8,128)S(1)}, u32[]{:S(2)}, u32[]{:S(2)}) collective-permute-start(f32[129,128]{1,0:T(8,128)S(1)} %add.213), channel_id=1, source_target_pairs={{0,8},{4,12},{8,0},{12,4},{16,24},{20,28},{24,16},{28,20},{32,40},... | collective-permute-start | bytes 198152 | tf_op jit(solution)/shard_map/ppermute | solution.py:119
  203.1 3.6 %collective-permute-done.19 = f32[129,128]{1,0:T(8,128)S(1)} collective-permute-done((f32[129,128]{1,0:T(8,128)S(1)}, f32[129,128]{1,0:T(8,128)S(1)}, u32[]{:S(2)}, u32[]{:S(2)}) %collective-permute-start.19) | collective-permute-done | bytes 66080 | tf_op jit(solution)/shard_map/ppermute | solution.py:119
  217.7 8.3 %collective-permute-done.23 = f32[258,128]{1,0:T(8,128)} collective-permute-done((f32[258,128]{1,0:T(8,128)S(1)}, f32[258,128]{1,0:T(8,128)}, u32[]{:S(2)}, u32[]{:S(2)}) %collective-permute-start.23) | collective-permute-done | bytes 132128 | tf_op jit(solution)/shard_map/ppermute | solution.py:119
  229.8 9.1 %collective-permute-start.26 = (bf16[2,2,2,2,2,1,32,512]{7,6,5,4,3,2,1,0:T(8,128)(2,1)}, bf16[2,2,2,2,2,1,32,512]{7,6,5,4,3,2,1,0:T(8,128)(2,1)}, u32[]{:S(2)}, u32[]{:S(2)}) collective-permute-start(bf16[2,2,2,2,2,1,32,512]{7,6,5,4,3,2,1,0:T(8,128)(2,1)} %maximum_select_fusion.1), channel_id=1, source_target_pairs={{0,4},{4,0},{8,12},{12,8},{16,20},{20,16},{24,28},{28,24},{32,36},... | collective-permute-start | bytes 3145736 | tf_op jit(solution)/shard_map/ppermute | solution.py:119
  253.4 3.8 %reshape.413 = f32[16,32,64,8]{1,0,3,2:T(8,128)} reshape(f32[512,512]{0,1:T(8,128)} %convolution_bitcast_fusion.2) | data formatting | bytes 2097152 | tf_op jit(solution)/shard_map/reshape | solution.py:405
  257.2 3.8 %fusion.9 = f32[64,1,32,8]{2,1,3,0:T(1,128)S(1)} fusion(f32[16,32,64,8]{1,0,3,2:T(8,128)} %reshape.413, pred[64,16,1,1]{1,0,2,3:T(32,128)(4,1)S(1)} %fusion.13), kind=kOutput, calls=%fused_computation.52 | convolution fusion | flops 3145728 | bytes 1115136 | tf_op jit(solution)/shard_map/gxaz,ag->azx/dot_general | solution.py:406
  261.1 4.7 %convolution_subtract_fusion = f32[8,32,2048]{2,1,0:T(8,128)} fusion(f32[8,32,2048]{2,1,0:T(8,128)} %param.22, f32[64,2048,1]{1,0,2:T(8,128)S(1)} %convolution_bitcast_fusion.1, f32[64,1,32,8]{0,2,3,1:T(8,128)S(1)} %copy.30), kind=kOutput, calls=%fused_computation.5 | convolution fusion | flops 403177472 | bytes 4784128 | tf_op jit(solution)/shard_map/azx,ay->zxy/dot_general | solution.py:407
  (147 shorter events, 117.6 us)
Async XLA Ops:
  23.3 43.1 %collective-permute-start.9 = (f32[2,2,2,2,2,1,32,512]{7,6,5,4,3,2,1,0:T(8,128)}, f32[2,2,2,2,2,1,32,512]{7,6,5,4,3,2,1,0:T(8,128)}, u32[]{:S(2)}, u32[]{:S(2)}) collective-permute-start(f32[2,2,2,2,2,1,32,512]{7,6,5,4,3,2,1,0:T(8,128)} %constant_dynamic-slice_fusion.5), channel_id=1, source_target_pairs={{0,4},{4,0},{8,12},{12,8},{16,20},{20,16},{24,28},{28,24},{32,36},... | collective-permute-start | bytes 6291464 | tf_op jit(solution)/shard_map/ppermute | solution.py:119
  27.5 10.3 %collective-permute-start = (f32[2,384,128]{2,1,0:T(8,128)}, f32[2,384,128]{2,1,0:T(8,128)S(1)}, u32[]{:S(2)}, u32[]{:S(2)}) collective-permute-start(f32[2,384,128]{2,1,0:T(8,128)} %get-tuple-element.59), channel_id=1, source_target_pairs={{0,64},{64,128},{128,192},{1,65},{65,129},{129,193},{2,66},{66,130... | collective-permute-start | bytes 1179656 | tf_op jit(solution)/shard_map/ppermute | solution.py:19
  29.0 12.6 %collective-permute-start.1 = (f32[2,384,128]{2,1,0:T(8,128)}, f32[2,384,128]{2,1,0:T(8,128)}, u32[]{:S(2)}, u32[]{:S(2)}) collective-permute-start(f32[2,384,128]{2,1,0:T(8,128)} %get-tuple-element.60), channel_id=1, source_target_pairs={{64,0},{128,64},{192,128},{65,1},{129,65},{193,129},{66,2},{130,66... | collective-permute-start | bytes 1179656 | tf_op jit(solution)/shard_map/ppermute | solution.py:19
  65.4 16.6 %collective-permute-start.4 = (f32[516,128]{1,0:T(8,128)}, f32[516,128]{1,0:T(8,128)}, u32[]{:S(2)}, u32[]{:S(2)}) collective-permute-start(f32[516,128]{1,0:T(8,128)} %constant_dynamic-slice_fusion.8), channel_id=1, source_target_pairs={{0,4},{4,0},{8,12},{12,8},{16,20},{20,16},{24,28},{28,24},{32,36},... | collective-permute-start | bytes 792584 | tf_op jit(solution)/shard_map/ppermute | solution.py:119
  71.6 33.5 %collective-permute-start.10 = (f32[2,1,2,2,2,1,32,512]{7,6,5,4,3,2,1,0:T(8,128)}, f32[2,1,2,2,2,1,32,512]{7,6,5,4,3,2,1,0:T(8,128)}, u32[]{:S(2)}, u32[]{:S(2)}) collective-permute-start(f32[2,1,2,2,2,1,32,512]{7,6,5,4,3,2,1,0:T(8,128)} %constant_dynamic-slice_fusion.4), channel_id=1, source_target_pairs={{0,64},{64,0},{128,192},{192,128},{1,65},{65,1},{129,193},{193,129... | collective-permute-start | bytes 3145736 | tf_op jit(solution)/shard_map/ppermute | solution.py:119
  73.7 28.8 %collective-permute-start.2 = (f32[2,384,128]{2,1,0:T(8,128)}, f32[2,384,128]{2,1,0:T(8,128)}, u32[]{:S(2)}, u32[]{:S(2)}) collective-permute-start(f32[2,384,128]{2,1,0:T(8,128)} %get-tuple-element.58), channel_id=1, source_target_pairs={{0,64},{64,128},{128,192},{1,65},{65,129},{129,193},{2,66},{66,130... | collective-permute-start | bytes 1179656 | tf_op jit(solution)/shard_map/ppermute | solution.py:19
  80.5 24.4 %collective-permute-start.3 = (f32[2,384,128]{2,1,0:T(8,128)S(1)}, f32[2,384,128]{2,1,0:T(8,128)S(1)}, u32[]{:S(2)}, u32[]{:S(2)}) collective-permute-start(f32[2,384,128]{2,1,0:T(8,128)S(1)} %get-tuple-element.57), channel_id=1, source_target_pairs={{64,0},{128,64},{192,128},{65,1},{129,65},{193,129},{66,2},{130,66... | collective-permute-start | bytes 1179656 | tf_op jit(solution)/shard_map/ppermute | solution.py:19
  83.0 28.5 %collective-permute-start.5 = (f32[258,128]{1,0:T(8,128)S(1)}, f32[258,128]{1,0:T(8,128)S(1)}, u32[]{:S(2)}, u32[]{:S(2)}) collective-permute-start(f32[258,128]{1,0:T(8,128)S(1)} %constant_dynamic-slice_fusion.7), channel_id=1, source_target_pairs={{0,64},{64,0},{128,192},{192,128},{1,65},{65,1},{129,193},{193,129... | collective-permute-start | bytes 396296 | tf_op jit(solution)/shard_map/ppermute | solution.py:119
  106.7 15.5 %collective-permute-start.11 = (f32[2,1,2,1,2,1,32,512]{7,6,5,4,3,2,1,0:T(8,128)S(1)}, f32[2,1,2,1,2,1,32,512]{7,6,5,4,3,2,1,0:T(8,128)S(1)}, u32[]{:S(2)}, u32[]{:S(2)}) collective-permute-start(f32[2,1,2,1,2,1,32,512]{7,6,5,4,3,2,1,0:T(8,128)S(1)} %constant_dynamic-slice_fusion.3), channel_id=1, source_target_pairs={{0,16},{4,20},{8,24},{12,28},{16,0},{20,4},{24,8},{28,12},{32,48},... | collective-permute-start | bytes 1572872 | tf_op jit(solution)/shard_map/ppermute | solution.py:119
  112.2 33.4 %collective-permute-start.6 = (f32[129,128]{1,0:T(8,128)}, f32[129,128]{1,0:T(8,128)}, u32[]{:S(2)}, u32[]{:S(2)}) collective-permute-start(f32[129,128]{1,0:T(8,128)} %constant_dynamic-slice_fusion.6), channel_id=1, source_target_pairs={{0,1},{1,0},{2,3},{3,2},{4,5},{5,4},{6,7},{7,6},{8,9},{9,8},{10,11... | collective-permute-start | bytes 198152 | tf_op jit(solution)/shard_map/ppermute | solution.py:119
  123.8 33.7 %collective-permute-start.12 = (f32[1,1,2,1,2,1,32,512]{7,6,5,4,3,2,1,0:T(8,128)}, f32[1,1,2,1,2,1,32,512]{7,6,5,4,3,2,1,0:T(8,128)}, u32[]{:S(2)}, u32[]{:S(2)}) collective-permute-start(f32[1,1,2,1,2,1,32,512]{7,6,5,4,3,2,1,0:T(8,128)} %constant_dynamic-slice_fusion.2), channel_id=1, source_target_pairs={{0,128},{64,192},{128,0},{192,64},{1,129},{65,193},{129,1},{193,65... | collective-permute-start | bytes 786440 | tf_op jit(solution)/shard_map/ppermute | solution.py:119
  132.5 22.9 %all-to-all-start = ((f32[16,1,1024]{2,1,0:T(1,128)}), f32[16,1,1024]{2,1,0:T(1,128)S(1)}, u32[]{:S(2)}, u32[]{:S(2)}) async-start(f32[16,1,1024]{2,1,0:T(1,128)} %reshape.417), calls=%async_computation | async-start | bytes 131072 | tf_op jit(solution)/shard_map/all_to_all | solution.py:349
  147.2 22.7 %collective-permute-start.7 = (f32[129,128]{1,0:T(8,128)}, f32[129,128]{1,0:T(8,128)}, u32[]{:S(2)}, u32[]{:S(2)}) collective-permute-start(f32[129,128]{1,0:T(8,128)} %dynamic-slice_add_fusion.7), channel_id=1, source_target_pairs={{0,16},{4,20},{8,24},{12,28},{16,0},{20,4},{24,8},{28,12},{32,48},... | collective-permute-start | bytes 198152 | tf_op jit(solution)/shard_map/ppermute | solution.py:119
  159.3 14.8 %collective-permute-start.13 = (f32[1,1,1,1,2,1,32,512]{7,6,5,4,3,2,1,0:T(8,128)S(1)}, f32[1,1,1,1,2,1,32,512]{7,6,5,4,3,2,1,0:T(8,128)}, u32[]{:S(2)}, u32[]{:S(2)}) collective-permute-start(f32[1,1,1,1,2,1,32,512]{7,6,5,4,3,2,1,0:T(8,128)S(1)} %constant_dynamic-slice_fusion.1), channel_id=1, source_target_pairs={{0,32},{4,36},{8,40},{12,44},{16,48},{20,52},{24,56},{28,60},{32,0... | collective-permute-start | bytes 393224 | tf_op jit(solution)/shard_map/ppermute | solution.py:119
  162.0 14.8 %all-to-all-start.1 = ((f32[4,1,4096]{2,1,0:T(1,128)}), f32[4,1,4096]{2,1,0:T(1,128)S(1)}, u32[]{:S(2)}, u32[]{:S(2)}) async-start(f32[4,1,4096]{2,1,0:T(1,128)} %reshape.419), calls=%async_computation.1 | async-start | bytes 131072 | tf_op jit(solution)/shard_map/all_to_all | solution.py:348
  170.8 5.3 %collective-permute-start.8 = (f32[129,128]{1,0:T(8,128)S(1)}, f32[129,128]{1,0:T(8,128)S(1)}, u32[]{:S(2)}, u32[]{:S(2)}) collective-permute-start(f32[129,128]{1,0:T(8,128)S(1)} %add.191), channel_id=1, source_target_pairs={{0,128},{64,192},{128,0},{192,64},{1,129},{65,193},{129,1},{193,65... | collective-permute-start | bytes 198152 | tf_op jit(solution)/shard_map/ppermute | solution.py:119
  175.8 7.4 %collective-permute-start.14 = (f32[1,1,1,1,1,1,32,512]{7,6,5,4,3,2,1,0:T(8,128)}, f32[1,1,1,1,1,1,32,512]{7,6,5,4,3,2,1,0:T(8,128)}, u32[]{:S(2)}, u32[]{:S(2)}) collective-permute-start(f32[1,1,1,1,1,1,32,512]{7,6,5,4,3,2,1,0:T(8,128)} %constant_dynamic-slice_fusion), channel_id=1, source_target_pairs={{0,8},{4,12},{8,0},{12,4},{16,24},{20,28},{24,16},{28,20},{32,40},... | collective-permute-start | bytes 196616 | tf_op jit(solution)/shard_map/ppermute | solution.py:119
  184.0 6.8 %collective-permute-start.16 = (bf16[1,1,1,1,1,1,32,512]{7,6,5,4,3,2,1,0:T(8,128)(2,1)S(1)}, bf16[1,1,1,1,1,1,32,512]{7,6,5,4,3,2,1,0:T(8,128)(2,1)S(1)}, u32[]{:S(2)}, u32[]{:S(2)}) collective-permute-start(bf16[1,1,1,1,1,1,32,512]{7,6,5,4,3,2,1,0:T(8,128)(2,1)S(1)} %subtract_convert_fusion), channel_id=1, source_target_pairs={{0,8},{4,12},{8,0},{12,4},{16,24},{20,28},{24,16},{28,20},{32,40},... | collective-permute-start | bytes 98312 | tf_op jit(solution)/shard_map/ppermute | solution.py:119
  199.1 8.3 %collective-permute-start.20 = (bf16[1,1,2,1,2,1,32,512]{7,6,5,4,3,2,1,0:T(8,128)(2,1)S(1)}, bf16[1,1,2,1,2,1,32,512]{7,6,5,4,3,2,1,0:T(8,128)(2,1)}, u32[]{:S(2)}, u32[]{:S(2)}) collective-permute-start(bf16[1,1,2,1,2,1,32,512]{7,6,5,4,3,2,1,0:T(8,128)(2,1)S(1)} %maximum_select_fusion.7), channel_id=1, source_target_pairs={{0,128},{64,192},{128,0},{192,64},{1,129},{65,193},{129,1},{193,65... | collective-permute-start | bytes 393224 | tf_op jit(solution)/shard_map/ppermute | solution.py:119
  199.6 7.1 %collective-permute-start.19 = (f32[129,128]{1,0:T(8,128)S(1)}, f32[129,128]{1,0:T(8,128)S(1)}, u32[]{:S(2)}, u32[]{:S(2)}) collective-permute-start(f32[129,128]{1,0:T(8,128)S(1)} %add.213), channel_id=1, source_target_pairs={{0,8},{4,12},{8,0},{12,4},{16,24},{20,28},{24,16},{28,20},{32,40},... | collective-permute-start | bytes 198152 | tf_op jit(solution)/shard_map/ppermute | solution.py:119
  208.4 5.8 %collective-permute-start.22 = (bf16[2,1,2,1,2,1,32,512]{7,6,5,4,3,2,1,0:T(8,128)(2,1)S(1)}, bf16[2,1,2,1,2,1,32,512]{7,6,5,4,3,2,1,0:T(8,128)(2,1)}, u32[]{:S(2)}, u32[]{:S(2)}) collective-permute-start(bf16[2,1,2,1,2,1,32,512]{7,6,5,4,3,2,1,0:T(8,128)(2,1)S(1)} %maximum_select_fusion.5), channel_id=1, source_target_pairs={{0,16},{4,20},{8,24},{12,28},{16,0},{20,4},{24,8},{28,12},{32,48},... | collective-permute-start | bytes 786440 | tf_op jit(solution)/shard_map/ppermute | solution.py:119
  216.1 11.0 %collective-permute-start.24 = (bf16[2,1,2,2,2,1,32,512]{7,6,5,4,3,2,1,0:T(8,128)(2,1)}, bf16[2,1,2,2,2,1,32,512]{7,6,5,4,3,2,1,0:T(8,128)(2,1)}, u32[]{:S(2)}, u32[]{:S(2)}) collective-permute-start(bf16[2,1,2,2,2,1,32,512]{7,6,5,4,3,2,1,0:T(8,128)(2,1)} %maximum_select_fusion.3), channel_id=1, source_target_pairs={{0,64},{64,0},{128,192},{192,128},{1,65},{65,1},{129,193},{193,129... | collective-permute-start | bytes 1572872 | tf_op jit(solution)/shard_map/ppermute | solution.py:119
  217.7 8.3 %collective-permute-start.23 = (f32[258,128]{1,0:T(8,128)S(1)}, f32[258,128]{1,0:T(8,128)}, u32[]{:S(2)}, u32[]{:S(2)}) collective-permute-start(f32[258,128]{1,0:T(8,128)S(1)} %maximum_select_fusion.6), channel_id=1, source_target_pairs={{0,64},{64,0},{128,192},{192,128},{1,65},{65,1},{129,193},{193,129... | collective-permute-start | bytes 396296 | tf_op jit(solution)/shard_map/ppermute | solution.py:119
  229.8 18.7 %collective-permute-start.26 = (bf16[2,2,2,2,2,1,32,512]{7,6,5,4,3,2,1,0:T(8,128)(2,1)}, bf16[2,2,2,2,2,1,32,512]{7,6,5,4,3,2,1,0:T(8,128)(2,1)}, u32[]{:S(2)}, u32[]{:S(2)}) collective-permute-start(bf16[2,2,2,2,2,1,32,512]{7,6,5,4,3,2,1,0:T(8,128)(2,1)} %maximum_select_fusion.1), channel_id=1, source_target_pairs={{0,4},{4,0},{8,12},{12,8},{16,20},{20,16},{24,28},{28,24},{32,36},... | collective-permute-start | bytes 3145736 | tf_op jit(solution)/shard_map/ppermute | solution.py:119
  (20 other events, 173.0 us)

commit v3 on v2

--- a/solution.py
+++ b/solution.py
@@ -119,32 +119,6 @@
     return lax.ppermute(values, axis, [(source, source ^ (1 << bit)) for source in range(count)])
 
 
-def halving_step(values, axis, bit):
-    mine = (lax.axis_index(axis) >> bit) & 1
-    half = values.shape[0] // 2
-    keep = lax.dynamic_slice_in_dim(values, mine * half, half, 0)
-    send = lax.dynamic_slice_in_dim(values, (1 - mine) * half, half, 0)
-    return keep + exchange(send, axis, bit)
-
-
-def doubling_step(values, axis, bit, place=0):
-    mine = (lax.axis_index(axis) >> bit) & 1
-    other = exchange(values, axis, bit)
-    return jnp.where(
-        mine == 0,
-        jnp.concatenate([values, other], axis=place),
-        jnp.concatenate([other, values], axis=place),
-    )
-
-
-def probe_ops(first, rest):
-    return (
-        [lambda values, step=step: halving_step(values, *step) for step in first]
-        + [lambda values, step=step: values + exchange(values, *step) for step in rest]
-        + [lambda values, step=step: doubling_step(values, *step) for step in reversed(first)]
-    )
-
-
 def halving_scatter(values, steps):
     for axis, bit in steps:
         mine = (lax.axis_index(axis) >> bit) & 1
@@ -194,7 +168,6 @@
     slot = pl.program_id(0)
     slots = pl.num_programs(0)
     side = probe_ref.shape[1]
-    width = window_ref.shape[2]
 
     @pl.when(slot == 0)
     def _():
@@ -209,10 +182,13 @@
         band = side + 8
         rows = pl.ds(pl.multiple_of(row // 8 * 8, 8), band)
         row_shift = row % 8
-        to_front = (width - col) % width
+        span = side + 128
+        cols = pl.ds(pl.multiple_of(col // 128 * 128, 128), span)
+        col_shift = col % 128
+        to_front = (span - col_shift) % span
 
         def extract(part):
-            values = pltpu.roll(window_ref[part, rows, :], (band - row_shift) % band, 0)
+            values = pltpu.roll(window_ref[part, rows, cols], (band - row_shift) % band, 0)
             return pltpu.roll(values[:side], to_front, 1)[:, :side]
 
         patch_real = extract(0)
@@ -237,17 +213,17 @@
         back = dot(back_half[:side], right_4a) + dot(back_half[side:], right_4b)
         back_real = back[:, :side]
         back_imag = back[:, side:]
-        filler = jnp.zeros((side, width - side), jnp.float32)
-        below = jnp.zeros((8, width), jnp.float32)
+        filler = jnp.zeros((side, span - side), jnp.float32)
+        below = jnp.zeros((8, span), jnp.float32)
         for part, value in enumerate(
             (
                 probe_real * back_real + probe_imag * back_imag,
                 probe_real * back_imag - probe_imag * back_real,
             )
         ):
-            placed = pltpu.roll(jnp.concatenate([value, filler], axis=1), col, 1)
+            placed = pltpu.roll(jnp.concatenate([value, filler], axis=1), col_shift, 1)
             placed = pltpu.roll(jnp.concatenate([placed, below], axis=0), row_shift, 0)
-            grad_ref[part, rows, :] += placed
+            grad_ref[part, rows, cols] += placed
         probe_sum_ref[0] += patch_real * back_real + patch_imag * back_imag
         probe_sum_ref[1] += patch_real * back_imag - patch_imag * back_real
         energy = jnp.sum(patch_real * patch_real + patch_imag * patch_imag) / (side * side)
@@ -339,7 +315,11 @@
             jnp.zeros((padded_rows - probe_rows - 1, 128), jnp.float32),
         ]
     )
-    probe_chain = probe_ops(probe_steps, probe_rest)
+    probe_flat = exchange_sum(halving_scatter(probe_flat, probe_steps), probe_rest)
+    probe_flat = doubling_gather(probe_flat, probe_steps)
+    probe_grad = probe_flat[:probe_rows].reshape(probe_sum.shape)
+    energy = probe_flat[probe_rows, 0]
+    new_probe = probe_field + probe_grad / (energy + 1e-05)
     probe_peak = jnp.max(probe_real * probe_real + probe_imag * probe_imag)
     new_object = (own_object + own_cells / (probe_peak + 1e-05))[None]
     slab_total = admm_dual.shape[1]
@@ -385,22 +365,7 @@
     volume_order = link_order(volume_steps)
     own_rows = ordered_scatter(partial_term, volume_steps, volume_order)
     own_residue = (own_rows - target).astype(jnp.bfloat16)
-    gather_chain = [
-        lambda values, step=step: doubling_step(values, *step, place=volume_steps.index(step))
-        for step in reversed(volume_order)
-    ]
-    lead = len(probe_chain) - len(gather_chain)
-    for operation in probe_chain[:lead]:
-        probe_flat = operation(probe_flat)
-    residue = own_residue.reshape((1,) * len(volume_steps) + own_residue.shape)
-    for probe_op, gather_op in zip(probe_chain[lead:], gather_chain):
-        probe_flat, residue = lax.optimization_barrier((probe_flat, residue))
-        probe_flat = probe_op(probe_flat)
-        residue = gather_op(residue)
-    residue = residue.reshape((-1,) + residue.shape[len(volume_steps) + 1 :])
-    probe_grad = probe_flat[:probe_rows].reshape(probe_sum.shape)
-    energy = probe_flat[probe_rows, 0]
-    new_probe = probe_field + probe_grad / (energy + 1e-05)
+    residue = ordered_gather(own_residue, volume_steps, volume_order)
     backproj = matmul(weight_flat, residue)
     backproj = backproj.reshape(angle_count, x_share, projections, slab_dev)
     back_sums = jnp.einsum("gxaz,ag->azx", backproj, onehot, precision=lax.Precision.HIGHEST)

time: 268 us -> 242 us (0.903)
  waiting for transfers between devices: 62.5 us -> 52.3 us
  other arithmetic: 45.6 us -> 35.9 us
    ppermute x4, waiting for transfers between devices: 24.2 us -> 6.21 us  [shifted(): lax.ppermute(value, axis, [(source, source + steps) for source in range(l...]
    ppermute x23, waiting for transfers between devices: 31.6 us -> 42.5 us  [exchange(): lax.ppermute(values, axis, [(source, source ^ 1 << bit) for source in ran...]
    select_n x9, other arithmetic: 12.3 us -> 6.99 us  [the longest x6 5.84 us: ordered_gather(): jnp.where(mine == 0, jnp.concatenate([values, other], axis=place), jnp.co...]
    all_to_all x1, starting transfers between devices: 7.88 us -> 3.28 us  [on_device(): lax.all_to_all(lax.all_to_all(slab_values, 'proj', split_axis=2, concat_a...]
    add x8, other arithmetic: 5.66 us -> 1.16 us  [the longest x3 1.11 us: halving_scatter(): values = keep + exchange(send, axis, bit)]
    all_to_all x1, waiting for transfers between devices: 6.81 us -> 3.6 us  [on_device(): lax.all_to_all(slab_values, 'proj', split_axis=2, concat_axis=0, tiled=True)]
    unnamed x36 -> x34, local copies, waits for them, and re-layouts: 8.32 us -> 6.94 us
  transfers between devices with their start and end apart: 29 -> 29, of which waited for: 15 -> 17; matrix products, arithmetic and copies ran while one was open for 22% -> 23% of each run, Pallas kernels for 6% -> 5%
where the time goes in v3:
time: 242 us; the launch traced here: 240 us
  starting transfers between devices  74.8 us (31%)
  waiting for transfers between devices  52.3 us (22%)
  local copies, waits for them, and re-layouts  43.2 us (18%)
  other arithmetic  35.9 us (15%)
  matrix products  18.7 us (8%)
  Pallas kernels  12.3 us (5%)
  between operations  3.02 us (1%)
    ppermute x23, starting transfers between devices, exchange(): lax.ppermute(values, axis, [(source, source ^ 1 << bit) for source in ran...  48 us
    ppermute x23, waiting for transfers between devices, exchange(): lax.ppermute(values, axis, [(source, source ^ 1 << bit) for source in ran...  42.5 us
    all_to_all x1, starting transfers between devices, on_device(): lax.all_to_all(slab_values, 'proj', split_axis=2, concat_axis=0, tiled=True)  13.6 us
    pallas_call x1, Pallas kernels, patch_terms_all(): pl.pallas_call(patch_kernel, grid_spec=grid_spec, out_shape=[jax.ShapeDty...  12.3 us
    ppermute x4, starting transfers between devices, shifted(): lax.ppermute(value, axis, [(source, source + steps) for source in range(l...  9.95 us
    unnamed x34, local copies, waits for them, and re-layouts  6.94 us
    add x5, other arithmetic, ordered_scatter(): values = keep + exchange(send, axis, bit)  6.39 us
    ppermute x4, waiting for transfers between devices, shifted(): lax.ppermute(value, axis, [(source, source + steps) for source in range(l...  6.21 us
  transfers between devices with their start and end apart: 29, of which 17 were waited for; matrix products, arithmetic and copies ran while one was open for 23% of the time, Pallas kernels for 5%

profile of v3, /device:TPU:1, one launch (start us, length us, event | category | flops | bytes accessed | tf_op | source)
XLA Modules:
  0.0 240.2 jit_solution(11119251253240415700)
XLA Ops:
  2.9 3.4 %fusion = bf16[32,64,8]{1,0,2:T(8,128)(2,1)S(1)} fusion(f32[64,2048,1]{1,0,2:T(8,128)S(1)} %convolution_bitcast_fusion.1, f32[8,32,2048]{2,1,0:T(8,128)} %param.22), kind=kOutput, calls=%fused_computation.12 | convolution fusion | flops 402669568 | bytes 2654208 | tf_op jit(solution)/shard_map/zxy,ay->azx/dot_general | solution.py:355
  8.0 3.4 %mul.241 = bf16[512,512]{0,1:T(8,128)(2,1)S(1)} reshape(bf16[16,32,64,8]{1,0,3,2:T(8,128)(2,1)} %broadcast_multiply_fusion) | data formatting | bytes 1048576 | tf_op jit(solution)/shard_map/mul | solution.py:358
  11.4 3.3 %convolution_bitcast_fusion = f32[2048,512]{0,1:T(8,128)} fusion(bf16[512,512]{0,1:T(8,128)(2,1)S(1)} %mul.241, bf16[512,2048]{1,0:T(8,128)(2,1)S(1)} %bitcast.104), kind=kOutput, calls=%fused_computation | convolution fusion | flops 1073741824 | bytes 6815744 | tf_op jit(solution)/shard_map/dot_general | solution.py:361
  14.7 5.4 %copy.59 = f32[2048,512]{1,0:T(8,128)} copy(f32[2048,512]{0,1:T(8,128)} %convolution_bitcast_fusion) | data formatting | bytes 8388608 | tf_op jit(solution)/shard_map/dot_general | solution.py:361
  20.0 3.3 %constant_dynamic-slice_fusion.5 = f32[2,2,2,2,2,1,32,512]{7,6,5,4,3,2,1,0:T(8,128)} fusion(f32[2,2,2,2,2,2,32,512]{7,6,5,4,3,2,1,0:T(8,128)} %bitcast.106, s32[]{:T(128)S(6)} %select_n.344), kind=kLoop, calls=%fused_computation.79 | loop fusion | bytes 4194308 | tf_op jit(solution)/shard_map/dynamic_slice | solution.py:98
  23.3 3.2 %collective-permute-start.15 = (f32[2,2,2,2,2,1,32,512]{7,6,5,4,3,2,1,0:T(8,128)}, f32[2,2,2,2,2,1,32,512]{7,6,5,4,3,2,1,0:T(8,128)}, u32[]{:S(2)}, u32[]{:S(2)}) collective-permute-start(f32[2,2,2,2,2,1,32,512]{7,6,5,4,3,2,1,0:T(8,128)} %constant_dynamic-slice_fusion.5), channel_id=1, source_target_pairs={{0,4},{4,0},{8,12},{12,8},{16,20},{20,16},{24,28},{28,24},{32,36},... | collective-permute-start | bytes 6291464 | tf_op jit(solution)/shard_map/ppermute | solution.py:119
  43.6 12.3 %shard_map.130 = (f32[2,392,896]{2,1,0:T(8,128)}, f32[2,256,256]{2,1,0:T(8,128)}, f32[8,128]{1,0:T(8,128)}) custom-call(s32[13]{0:T(128)} %pad_add_fusion.meta_ref, f32[2,392,896]{2,1,0:T(8,128)} %select_maximum_fusion.window_ref, bf16[6,256,256]{2,1,0:T(8,128)(2,1)} %bitcast.118, f32[2,256,256]{2,1,0:T(8,128)} %probe_ref.1, ...), custom_call_target="tpu_custom_call" | custom-call | tf_op jit(solution)/shard_map/pallas_call | solution.py:251
  57.8 5.9 %collective-permute-start.2 = (f32[2,384,128]{2,1,0:T(8,128)}, f32[2,384,128]{2,1,0:T(8,128)}, u32[]{:S(2)}, u32[]{:S(2)}) collective-permute-start(f32[2,384,128]{2,1,0:T(8,128)} %get-tuple-element.34), channel_id=1, source_target_pairs={{0,64},{64,128},{128,192},{1,65},{65,129},{129,193},{2,66},{66,130... | collective-permute-start | bytes 1179656 | tf_op jit(solution)/shard_map/ppermute | solution.py:19
  68.0 4.5 %collective-permute-done.2 = f32[2,384,128]{2,1,0:T(8,128)} collective-permute-done((f32[2,384,128]{2,1,0:T(8,128)}, f32[2,384,128]{2,1,0:T(8,128)}, u32[]{:S(2)}, u32[]{:S(2)}) %collective-permute-start.2) | collective-permute-done | bytes 393248 | tf_op jit(solution)/shard_map/ppermute | solution.py:19
  78.9 8.5 %collective-permute-done.17 = f32[2,1,2,1,2,1,32,512]{7,6,5,4,3,2,1,0:T(8,128)S(1)} collective-permute-done((f32[2,1,2,1,2,1,32,512]{7,6,5,4,3,2,1,0:T(8,128)S(1)}, f32[2,1,2,1,2,1,32,512]{7,6,5,4,3,2,1,0:T(8,128)S(1)}, u32[]{:S(2)}, u32[]{:S(2)}) %collective-permute-start.17) | collective-permute-done | bytes 524320 | tf_op jit(solution)/shard_map/ppermute | solution.py:119
  96.1 13.6 %all-to-all-start = ((f32[16,1,1024]{2,1,0:T(1,128)}), f32[16,1,1024]{2,1,0:T(1,128)S(1)}, u32[]{:S(2)}, u32[]{:S(2)}) async-start(f32[16,1,1024]{2,1,0:T(1,128)} %reshape.1080), calls=%async_computation | async-start | bytes 131072 | tf_op jit(solution)/shard_map/all_to_all | solution.py:329
  115.8 3.6 %all-to-all-done = f32[16,1,1024]{2,1,0:T(1,128)S(1)} async-done(((f32[16,1,1024]{2,1,0:T(1,128)}), f32[16,1,1024]{2,1,0:T(1,128)S(1)}, u32[]{:S(2)}, u32[]{:S(2)}) %all-to-all-start) | async-done | bytes 65568 | tf_op jit(solution)/shard_map/all_to_all | solution.py:329
  125.9 3.3 %all-to-all-start.1 = ((f32[4,1,4096]{2,1,0:T(1,128)}), f32[4,1,4096]{2,1,0:T(1,128)S(1)}, u32[]{:S(2)}, u32[]{:S(2)}) async-start(f32[4,1,4096]{2,1,0:T(1,128)} %reshape.1082), calls=%async_computation.1 | async-start | bytes 131072 | tf_op jit(solution)/shard_map/all_to_all | solution.py:328
  131.1 3.2 %collective-permute-start.20 = (f32[1,1,1,1,1,1,32,512]{7,6,5,4,3,2,1,0:T(8,128)}, f32[1,1,1,1,1,1,32,512]{7,6,5,4,3,2,1,0:T(8,128)}, u32[]{:S(2)}, u32[]{:S(2)}) collective-permute-start(f32[1,1,1,1,1,1,32,512]{7,6,5,4,3,2,1,0:T(8,128)} %constant_dynamic-slice_fusion), channel_id=1, source_target_pairs={{0,8},{4,12},{8,0},{12,4},{16,24},{20,28},{24,16},{28,20},{32,40},... | collective-permute-start | bytes 196616 | tf_op jit(solution)/shard_map/ppermute | solution.py:119
  142.0 2.9 %collective-permute-start.21 = (bf16[1,1,1,1,1,1,32,512]{7,6,5,4,3,2,1,0:T(8,128)(2,1)S(1)}, bf16[1,1,1,1,1,1,32,512]{7,6,5,4,3,2,1,0:T(8,128)(2,1)S(1)}, u32[]{:S(2)}, u32[]{:S(2)}) collective-permute-start(bf16[1,1,1,1,1,1,32,512]{7,6,5,4,3,2,1,0:T(8,128)(2,1)S(1)} %subtract_convert_fusion), channel_id=1, source_target_pairs={{0,8},{4,12},{8,0},{12,4},{16,24},{20,28},{24,16},{28,20},{32,40},... | collective-permute-start | bytes 98312 | tf_op jit(solution)/shard_map/ppermute | solution.py:119
  167.1 2.8 %collective-permute-done.7 = f32[129,128]{1,0:T(8,128)S(1)} collective-permute-done((f32[129,128]{1,0:T(8,128)S(1)}, f32[129,128]{1,0:T(8,128)S(1)}, u32[]{:S(2)}, u32[]{:S(2)}) %collective-permute-start.7) | collective-permute-done | bytes 66080 | tf_op jit(solution)/shard_map/ppermute | solution.py:119
  171.9 4.5 %collective-permute-done.8 = f32[129,128]{1,0:T(8,128)S(1)} collective-permute-done((f32[129,128]{1,0:T(8,128)S(1)}, f32[129,128]{1,0:T(8,128)S(1)}, u32[]{:S(2)}, u32[]{:S(2)}) %collective-permute-start.8) | collective-permute-done | bytes 66080 | tf_op jit(solution)/shard_map/ppermute | solution.py:119
  176.4 3.5 %collective-permute-start.9 = (f32[129,128]{1,0:T(8,128)S(1)}, f32[129,128]{1,0:T(8,128)S(1)}, u32[]{:S(2)}, u32[]{:S(2)}) collective-permute-start(f32[129,128]{1,0:T(8,128)S(1)} %add.192), channel_id=1, source_target_pairs={{0,2},{1,3},{2,0},{3,1},{4,6},{5,7},{6,4},{7,5},{8,10},{9,11},{10,... | collective-permute-start | bytes 198152 | tf_op jit(solution)/shard_map/ppermute | solution.py:119
  189.0 4.9 %collective-permute-done.11 = f32[129,128]{1,0:T(8,128)S(1)} collective-permute-done((f32[129,128]{1,0:T(8,128)S(1)}, f32[129,128]{1,0:T(8,128)S(1)}, u32[]{:S(2)}, u32[]{:S(2)}) %collective-permute-start.11) | collective-permute-done | bytes 66080 | tf_op jit(solution)/shard_map/ppermute | solution.py:119
  198.4 10.0 %collective-permute-start.26 = (bf16[2,2,2,2,2,1,32,512]{7,6,5,4,3,2,1,0:T(8,128)(2,1)}, bf16[2,2,2,2,2,1,32,512]{7,6,5,4,3,2,1,0:T(8,128)(2,1)}, u32[]{:S(2)}, u32[]{:S(2)}) collective-permute-start(bf16[2,2,2,2,2,1,32,512]{7,6,5,4,3,2,1,0:T(8,128)(2,1)} %maximum_select_fusion.1), channel_id=1, source_target_pairs={{0,4},{4,0},{8,12},{12,8},{16,20},{20,16},{24,28},{28,24},{32,36},... | collective-permute-start | bytes 3145736 | tf_op jit(solution)/shard_map/ppermute | solution.py:119
  208.6 5.2 %collective-permute-done.13 = f32[258,128]{1,0:T(8,128)S(1)} collective-permute-done((f32[258,128]{1,0:T(8,128)S(1)}, f32[258,128]{1,0:T(8,128)S(1)}, u32[]{:S(2)}, u32[]{:S(2)}) %collective-permute-start.13) | collective-permute-done | bytes 132128 | tf_op jit(solution)/shard_map/ppermute | solution.py:119
  227.9 3.8 %reshape.1076 = f32[16,32,64,8]{1,0,3,2:T(8,128)} reshape(f32[512,512]{0,1:T(8,128)} %convolution_bitcast_fusion.2) | data formatting | bytes 2097152 | tf_op jit(solution)/shard_map/reshape | solution.py:370
  231.6 3.8 %fusion.11 = f32[64,1,32,8]{2,1,3,0:T(1,128)S(1)} fusion(f32[16,32,64,8]{1,0,3,2:T(8,128)} %reshape.1076, pred[64,16,1,1]{1,0,2,3:T(32,128)(4,1)S(1)} %fusion.17), kind=kOutput, calls=%fused_computation.58 | convolution fusion | flops 3145728 | bytes 1115136 | tf_op jit(solution)/shard_map/gxaz,ag->azx/dot_general | solution.py:371
  235.5 4.7 %convolution_subtract_fusion = f32[8,32,2048]{2,1,0:T(8,128)} fusion(f32[8,32,2048]{2,1,0:T(8,128)} %param.22, f32[64,2048,1]{1,0,2:T(8,128)S(1)} %convolution_bitcast_fusion.1, f32[64,1,32,8]{0,2,3,1:T(8,128)S(1)} %copy.76), kind=kOutput, calls=%fused_computation.5 | convolution fusion | flops 403177472 | bytes 4784128 | tf_op jit(solution)/shard_map/azx,ay->zxy/dot_general | solution.py:372
  (149 shorter events, 114.3 us)
Async XLA Ops:
  23.3 12.6 %collective-permute-start.15 = (f32[2,2,2,2,2,1,32,512]{7,6,5,4,3,2,1,0:T(8,128)}, f32[2,2,2,2,2,1,32,512]{7,6,5,4,3,2,1,0:T(8,128)}, u32[]{:S(2)}, u32[]{:S(2)}) collective-permute-start(f32[2,2,2,2,2,1,32,512]{7,6,5,4,3,2,1,0:T(8,128)} %constant_dynamic-slice_fusion.5), channel_id=1, source_target_pairs={{0,4},{4,0},{8,12},{12,8},{16,20},{20,16},{24,28},{28,24},{32,36},... | collective-permute-start | bytes 6291464 | tf_op jit(solution)/shard_map/ppermute | solution.py:119
  27.5 14.3 %collective-permute-start = (f32[2,384,128]{2,1,0:T(8,128)}, f32[2,384,128]{2,1,0:T(8,128)S(1)}, u32[]{:S(2)}, u32[]{:S(2)}) collective-permute-start(f32[2,384,128]{2,1,0:T(8,128)} %get-tuple-element.35), channel_id=1, source_target_pairs={{0,64},{64,128},{128,192},{1,65},{65,129},{129,193},{2,66},{66,130... | collective-permute-start | bytes 1179656 | tf_op jit(solution)/shard_map/ppermute | solution.py:19
  29.0 12.8 %collective-permute-start.1 = (f32[2,384,128]{2,1,0:T(8,128)}, f32[2,384,128]{2,1,0:T(8,128)S(1)}, u32[]{:S(2)}, u32[]{:S(2)}) collective-permute-start(f32[2,384,128]{2,1,0:T(8,128)} %get-tuple-element.36), channel_id=1, source_target_pairs={{64,0},{128,64},{192,128},{65,1},{129,65},{193,129},{66,2},{130,66... | collective-permute-start | bytes 1179656 | tf_op jit(solution)/shard_map/ppermute | solution.py:19
  39.7 34.0 %collective-permute-start.16 = (f32[2,1,2,2,2,1,32,512]{7,6,5,4,3,2,1,0:T(8,128)}, f32[2,1,2,2,2,1,32,512]{7,6,5,4,3,2,1,0:T(8,128)}, u32[]{:S(2)}, u32[]{:S(2)}) collective-permute-start(f32[2,1,2,2,2,1,32,512]{7,6,5,4,3,2,1,0:T(8,128)} %constant_dynamic-slice_fusion.4), channel_id=1, source_target_pairs={{0,64},{64,0},{128,192},{192,128},{1,65},{65,1},{129,193},{193,129... | collective-permute-start | bytes 3145736 | tf_op jit(solution)/shard_map/ppermute | solution.py:119
  57.8 14.7 %collective-permute-start.2 = (f32[2,384,128]{2,1,0:T(8,128)}, f32[2,384,128]{2,1,0:T(8,128)}, u32[]{:S(2)}, u32[]{:S(2)}) collective-permute-start(f32[2,384,128]{2,1,0:T(8,128)} %get-tuple-element.34), channel_id=1, source_target_pairs={{0,64},{64,128},{128,192},{1,65},{65,129},{129,193},{2,66},{66,130... | collective-permute-start | bytes 1179656 | tf_op jit(solution)/shard_map/ppermute | solution.py:19
  66.7 11.6 %collective-permute-start.3 = (f32[2,384,128]{2,1,0:T(8,128)S(1)}, f32[2,384,128]{2,1,0:T(8,128)S(1)}, u32[]{:S(2)}, u32[]{:S(2)}) collective-permute-start(f32[2,384,128]{2,1,0:T(8,128)S(1)} %get-tuple-element.33), channel_id=1, source_target_pairs={{64,0},{128,64},{192,128},{65,1},{129,65},{193,129},{66,2},{130,66... | collective-permute-start | bytes 1179656 | tf_op jit(solution)/shard_map/ppermute | solution.py:19
  75.3 12.1 %collective-permute-start.17 = (f32[2,1,2,1,2,1,32,512]{7,6,5,4,3,2,1,0:T(8,128)S(1)}, f32[2,1,2,1,2,1,32,512]{7,6,5,4,3,2,1,0:T(8,128)S(1)}, u32[]{:S(2)}, u32[]{:S(2)}) collective-permute-start(f32[2,1,2,1,2,1,32,512]{7,6,5,4,3,2,1,0:T(8,128)S(1)} %constant_dynamic-slice_fusion.3), channel_id=1, source_target_pairs={{0,16},{4,20},{8,24},{12,28},{16,0},{20,4},{24,8},{28,12},{32,48},... | collective-permute-start | bytes 1572872 | tf_op jit(solution)/shard_map/ppermute | solution.py:119
  89.0 32.5 %collective-permute-start.18 = (f32[1,1,2,1,2,1,32,512]{7,6,5,4,3,2,1,0:T(8,128)}, f32[1,1,2,1,2,1,32,512]{7,6,5,4,3,2,1,0:T(8,128)}, u32[]{:S(2)}, u32[]{:S(2)}) collective-permute-start(f32[1,1,2,1,2,1,32,512]{7,6,5,4,3,2,1,0:T(8,128)} %constant_dynamic-slice_fusion.2), channel_id=1, source_target_pairs={{0,128},{64,192},{128,0},{192,64},{1,129},{65,193},{129,1},{193,65... | collective-permute-start | bytes 786440 | tf_op jit(solution)/shard_map/ppermute | solution.py:119
  96.1 23.3 %all-to-all-start = ((f32[16,1,1024]{2,1,0:T(1,128)}), f32[16,1,1024]{2,1,0:T(1,128)S(1)}, u32[]{:S(2)}, u32[]{:S(2)}) async-start(f32[16,1,1024]{2,1,0:T(1,128)} %reshape.1080), calls=%async_computation | async-start | bytes 131072 | tf_op jit(solution)/shard_map/all_to_all | solution.py:329
  123.2 6.2 %collective-permute-start.19 = (f32[1,1,1,1,2,1,32,512]{7,6,5,4,3,2,1,0:T(8,128)S(1)}, f32[1,1,1,1,2,1,32,512]{7,6,5,4,3,2,1,0:T(8,128)}, u32[]{:S(2)}, u32[]{:S(2)}) collective-permute-start(f32[1,1,1,1,2,1,32,512]{7,6,5,4,3,2,1,0:T(8,128)S(1)} %constant_dynamic-slice_fusion.1), channel_id=1, source_target_pairs={{0,32},{4,36},{8,40},{12,44},{16,48},{20,52},{24,56},{28,60},{32,0... | collective-permute-start | bytes 393224 | tf_op jit(solution)/shard_map/ppermute | solution.py:119
  125.9 11.0 %all-to-all-start.1 = ((f32[4,1,4096]{2,1,0:T(1,128)}), f32[4,1,4096]{2,1,0:T(1,128)S(1)}, u32[]{:S(2)}, u32[]{:S(2)}) async-start(f32[4,1,4096]{2,1,0:T(1,128)} %reshape.1082), calls=%async_computation.1 | async-start | bytes 131072 | tf_op jit(solution)/shard_map/all_to_all | solution.py:328
  131.1 10.0 %collective-permute-start.20 = (f32[1,1,1,1,1,1,32,512]{7,6,5,4,3,2,1,0:T(8,128)}, f32[1,1,1,1,1,1,32,512]{7,6,5,4,3,2,1,0:T(8,128)}, u32[]{:S(2)}, u32[]{:S(2)}) collective-permute-start(f32[1,1,1,1,1,1,32,512]{7,6,5,4,3,2,1,0:T(8,128)} %constant_dynamic-slice_fusion), channel_id=1, source_target_pairs={{0,8},{4,12},{8,0},{12,4},{16,24},{20,28},{24,16},{28,20},{32,40},... | collective-permute-start | bytes 196616 | tf_op jit(solution)/shard_map/ppermute | solution.py:119
  136.0 8.9 %collective-permute-start.4 = (f32[516,128]{1,0:T(8,128)}, f32[516,128]{1,0:T(8,128)}, u32[]{:S(2)}, u32[]{:S(2)}) collective-permute-start(f32[516,128]{1,0:T(8,128)} %constant_dynamic-slice_fusion.8), channel_id=1, source_target_pairs={{0,4},{4,0},{8,12},{12,8},{16,20},{20,16},{24,28},{28,24},{32,36},... | collective-permute-start | bytes 792584 | tf_op jit(solution)/shard_map/ppermute | solution.py:119
  142.0 6.8 %collective-permute-start.21 = (bf16[1,1,1,1,1,1,32,512]{7,6,5,4,3,2,1,0:T(8,128)(2,1)S(1)}, bf16[1,1,1,1,1,1,32,512]{7,6,5,4,3,2,1,0:T(8,128)(2,1)S(1)}, u32[]{:S(2)}, u32[]{:S(2)}) collective-permute-start(bf16[1,1,1,1,1,1,32,512]{7,6,5,4,3,2,1,0:T(8,128)(2,1)S(1)} %subtract_convert_fusion), channel_id=1, source_target_pairs={{0,8},{4,12},{8,0},{12,4},{16,24},{20,28},{24,16},{28,20},{32,40},... | collective-permute-start | bytes 98312 | tf_op jit(solution)/shard_map/ppermute | solution.py:119
  153.5 5.4 %collective-permute-start.23 = (bf16[1,1,2,1,2,1,32,512]{7,6,5,4,3,2,1,0:T(8,128)(2,1)S(1)}, bf16[1,1,2,1,2,1,32,512]{7,6,5,4,3,2,1,0:T(8,128)(2,1)S(1)}, u32[]{:S(2)}, u32[]{:S(2)}) collective-permute-start(bf16[1,1,2,1,2,1,32,512]{7,6,5,4,3,2,1,0:T(8,128)(2,1)S(1)} %fusion.9), channel_id=1, source_target_pairs={{0,128},{64,192},{128,0},{192,64},{1,129},{65,193},{129,1},{193,65... | collective-permute-start | bytes 393224 | tf_op jit(solution)/shard_map/ppermute | solution.py:119
  154.0 6.0 %collective-permute-start.5 = (f32[258,128]{1,0:T(8,128)S(1)}, f32[258,128]{1,0:T(8,128)S(1)}, u32[]{:S(2)}, u32[]{:S(2)}) collective-permute-start(f32[258,128]{1,0:T(8,128)S(1)} %constant_dynamic-slice_fusion.7), channel_id=1, source_target_pairs={{0,64},{64,0},{128,192},{192,128},{1,65},{65,1},{129,193},{193,129... | collective-permute-start | bytes 396296 | tf_op jit(solution)/shard_map/ppermute | solution.py:119
  159.0 5.3 %collective-permute-start.24 = (bf16[2,1,2,1,2,1,32,512]{7,6,5,4,3,2,1,0:T(8,128)(2,1)S(1)}, bf16[2,1,2,1,2,1,32,512]{7,6,5,4,3,2,1,0:T(8,128)(2,1)S(1)}, u32[]{:S(2)}, u32[]{:S(2)}) collective-permute-start(bf16[2,1,2,1,2,1,32,512]{7,6,5,4,3,2,1,0:T(8,128)(2,1)S(1)} %fusion.5), channel_id=1, source_target_pairs={{0,16},{4,20},{8,24},{12,28},{16,0},{20,4},{24,8},{28,12},{32,48},... | collective-permute-start | bytes 786440 | tf_op jit(solution)/shard_map/ppermute | solution.py:119
  160.0 6.7 %collective-permute-start.6 = (f32[129,128]{1,0:T(8,128)S(1)}, f32[129,128]{1,0:T(8,128)S(1)}, u32[]{:S(2)}, u32[]{:S(2)}) collective-permute-start(f32[129,128]{1,0:T(8,128)S(1)} %constant_dynamic-slice_fusion.6), channel_id=1, source_target_pairs={{0,1},{1,0},{2,3},{3,2},{4,5},{5,4},{6,7},{7,6},{8,9},{9,8},{10,11... | collective-permute-start | bytes 198152 | tf_op jit(solution)/shard_map/ppermute | solution.py:119
  165.1 31.0 %collective-permute-start.25 = (bf16[2,1,2,2,2,1,32,512]{7,6,5,4,3,2,1,0:T(8,128)(2,1)}, bf16[2,1,2,2,2,1,32,512]{7,6,5,4,3,2,1,0:T(8,128)(2,1)}, u32[]{:S(2)}, u32[]{:S(2)}) collective-permute-start(bf16[2,1,2,2,2,1,32,512]{7,6,5,4,3,2,1,0:T(8,128)(2,1)} %maximum_select_fusion.4), channel_id=1, source_target_pairs={{0,64},{64,0},{128,192},{192,128},{1,65},{65,1},{129,193},{193,129... | collective-permute-start | bytes 1572872 | tf_op jit(solution)/shard_map/ppermute | solution.py:119
  170.0 6.4 %collective-permute-start.8 = (f32[129,128]{1,0:T(8,128)S(1)}, f32[129,128]{1,0:T(8,128)S(1)}, u32[]{:S(2)}, u32[]{:S(2)}) collective-permute-start(f32[129,128]{1,0:T(8,128)S(1)} %add.191), channel_id=1, source_target_pairs={{0,128},{64,192},{128,0},{192,64},{1,129},{65,193},{129,1},{193,65... | collective-permute-start | bytes 198152 | tf_op jit(solution)/shard_map/ppermute | solution.py:119
  176.4 5.5 %collective-permute-start.9 = (f32[129,128]{1,0:T(8,128)S(1)}, f32[129,128]{1,0:T(8,128)S(1)}, u32[]{:S(2)}, u32[]{:S(2)}) collective-permute-start(f32[129,128]{1,0:T(8,128)S(1)} %add.192), channel_id=1, source_target_pairs={{0,2},{1,3},{2,0},{3,1},{4,6},{5,7},{6,4},{7,5},{8,10},{9,11},{10,... | collective-permute-start | bytes 198152 | tf_op jit(solution)/shard_map/ppermute | solution.py:119
  186.6 7.2 %collective-permute-start.11 = (f32[129,128]{1,0:T(8,128)S(1)}, f32[129,128]{1,0:T(8,128)S(1)}, u32[]{:S(2)}, u32[]{:S(2)}) collective-permute-start(f32[129,128]{1,0:T(8,128)S(1)} %add.194), channel_id=1, source_target_pairs={{0,8},{4,12},{8,0},{12,4},{16,24},{20,28},{24,16},{28,20},{32,40},... | collective-permute-start | bytes 198152 | tf_op jit(solution)/shard_map/ppermute | solution.py:119
  193.9 14.6 %collective-permute-start.12 = (f32[129,128]{1,0:T(8,128)S(1)}, f32[129,128]{1,0:T(8,128)S(1)}, u32[]{:S(2)}, u32[]{:S(2)}) collective-permute-start(f32[129,128]{1,0:T(8,128)S(1)} %add.195), channel_id=1, source_target_pairs={{0,1},{1,0},{2,3},{3,2},{4,5},{5,4},{6,7},{7,6},{8,9},{9,8},{10,11... | collective-permute-start | bytes 198152 | tf_op jit(solution)/shard_map/ppermute | solution.py:119
  198.4 24.6 %collective-permute-start.26 = (bf16[2,2,2,2,2,1,32,512]{7,6,5,4,3,2,1,0:T(8,128)(2,1)}, bf16[2,2,2,2,2,1,32,512]{7,6,5,4,3,2,1,0:T(8,128)(2,1)}, u32[]{:S(2)}, u32[]{:S(2)}) collective-permute-start(bf16[2,2,2,2,2,1,32,512]{7,6,5,4,3,2,1,0:T(8,128)(2,1)} %maximum_select_fusion.1), channel_id=1, source_target_pairs={{0,4},{4,0},{8,12},{12,8},{16,20},{20,16},{24,28},{28,24},{32,36},... | collective-permute-start | bytes 3145736 | tf_op jit(solution)/shard_map/ppermute | solution.py:119
  (19 other events, 156.1 us)

commit v4 on v3

--- a/solution.py
+++ b/solution.py
@@ -368,7 +368,7 @@
     residue = ordered_gather(own_residue, volume_steps, volume_order)
     backproj = matmul(weight_flat, residue)
     backproj = backproj.reshape(angle_count, x_share, projections, slab_dev)
-    back_sums = jnp.einsum("gxaz,ag->azx", backproj, onehot, precision=lax.Precision.HIGHEST)
+    back_sums = jnp.sum(backproj * onehot.T[:, None, :, None], axis=0).transpose(1, 2, 0)
     gradient = jnp.einsum("azx,ay->zxy", back_sums, ray_table, precision=lax.Precision.HIGHEST)
     new_volume = volume - tomo_step * gradient
     return (new_object, new_probe, new_volume)

time: 242 us -> 240 us (level)
  matrix products: 18.7 us -> 13.5 us
  other arithmetic: 35.9 us -> 39.9 us
  Pallas kernels: 12.3 us -> 9.82 us
    dot_general x1 -> x0, matrix products: 3.76 us -> none  [on_device(): jnp.einsum('gxaz,ag->azx', backproj, onehot, precision=lax.Precision.HIGH...]
    reduce_sum x0 -> x1, other arithmetic: none -> 3.3 us  [on_device(): jnp.sum(backproj * onehot.T[:, None, :, None], axis=0).transpose(1, 2, 0)]
    pallas_call x1, Pallas kernels: 12.3 us -> 9.82 us  [patch_terms_all(): pl.pallas_call(patch_kernel, grid_spec=grid_spec, out_shape=[jax.ShapeDty...]
    unnamed x34 -> x36, local copies, waits for them, and re-layouts: 6.94 us -> 6.99 us
  transfers between devices with their start and end apart: 29 -> 29, of which waited for: 17 -> 16; matrix products, arithmetic and copies ran while one was open for 23% -> 23% of each run, Pallas kernels for 5% -> 4%
where the time goes in v4:
time: 240 us; the launch traced here: 239 us
  starting transfers between devices  75.7 us (32%)
  waiting for transfers between devices  54 us (22%)
  local copies, waits for them, and re-layouts  43.1 us (18%)
  other arithmetic  39.9 us (17%)
  matrix products  13.5 us (6%)
  Pallas kernels  9.82 us (4%)
  between operations  3.01 us (1%)
    ppermute x23, starting transfers between devices, exchange(): lax.ppermute(values, axis, [(source, source ^ 1 << bit) for source in ran...  48.2 us
    ppermute x23, waiting for transfers between devices, exchange(): lax.ppermute(values, axis, [(source, source ^ 1 << bit) for source in ran...  44.2 us
    all_to_all x1, starting transfers between devices, on_device(): lax.all_to_all(slab_values, 'proj', split_axis=2, concat_axis=0, tiled=True)  13.6 us
    ppermute x4, starting transfers between devices, shifted(): lax.ppermute(value, axis, [(source, source + steps) for source in range(l...  10.7 us
    pallas_call x1, Pallas kernels, patch_terms_all(): pl.pallas_call(patch_kernel, grid_spec=grid_spec, out_shape=[jax.ShapeDty...  9.82 us
    unnamed x36, local copies, waits for them, and re-layouts  6.99 us
    add x5, other arithmetic, ordered_scatter(): values = keep + exchange(send, axis, bit)  6.39 us
    ppermute x4, waiting for transfers between devices, shifted(): lax.ppermute(value, axis, [(source, source + steps) for source in range(l...  6.19 us
  transfers between devices with their start and end apart: 29, of which 16 were waited for; matrix products, arithmetic and copies ran while one was open for 23% of the time, Pallas kernels for 4%

profile of v4, /device:TPU:1, one launch (start us, length us, event | category | flops | bytes accessed | tf_op | source)
XLA Modules:
  0.0 239.1 jit_solution(7466573596245600191)
XLA Ops:
  3.5 3.4 %fusion = bf16[32,64,8]{1,0,2:T(8,128)(2,1)S(1)} fusion(f32[64,2048,1]{1,0,2:T(8,128)S(1)} %convolution_bitcast_fusion.1, f32[8,32,2048]{2,1,0:T(8,128)} %param.22), kind=kOutput, calls=%fused_computation.13 | convolution fusion | flops 402669568 | bytes 2654208 | tf_op jit(solution)/shard_map/zxy,ay->azx/dot_general | solution.py:355
  8.6 3.4 %mul.249 = bf16[512,512]{0,1:T(8,128)(2,1)S(1)} reshape(bf16[16,32,64,8]{1,0,3,2:T(8,128)(2,1)} %broadcast_multiply_fusion) | data formatting | bytes 1048576 | tf_op jit(solution)/shard_map/mul | solution.py:358
  12.0 3.3 %convolution_bitcast_fusion = f32[2048,512]{0,1:T(8,128)} fusion(bf16[512,512]{0,1:T(8,128)(2,1)S(1)} %mul.249, bf16[512,2048]{1,0:T(8,128)(2,1)S(1)} %bitcast.97), kind=kOutput, calls=%fused_computation.1 | convolution fusion | flops 1073741824 | bytes 6815744 | tf_op jit(solution)/shard_map/dot_general | solution.py:361
  15.3 5.4 %copy.60 = f32[2048,512]{1,0:T(8,128)} copy(f32[2048,512]{0,1:T(8,128)} %convolution_bitcast_fusion) | data formatting | bytes 8388608 | tf_op jit(solution)/shard_map/dot_general | solution.py:361
  20.6 3.3 %constant_dynamic-slice_fusion.5 = f32[2,2,2,2,2,1,32,512]{7,6,5,4,3,2,1,0:T(8,128)} fusion(f32[2,2,2,2,2,2,32,512]{7,6,5,4,3,2,1,0:T(8,128)} %bitcast.99, s32[]{:T(128)S(6)} %select_n.344), kind=kLoop, calls=%fused_computation.78 | loop fusion | bytes 4194308 | tf_op jit(solution)/shard_map/dynamic_slice | solution.py:98
  24.0 3.2 %collective-permute-start.15 = (f32[2,2,2,2,2,1,32,512]{7,6,5,4,3,2,1,0:T(8,128)}, f32[2,2,2,2,2,1,32,512]{7,6,5,4,3,2,1,0:T(8,128)}, u32[]{:S(2)}, u32[]{:S(2)}) collective-permute-start(f32[2,2,2,2,2,1,32,512]{7,6,5,4,3,2,1,0:T(8,128)} %constant_dynamic-slice_fusion.5), channel_id=1, source_target_pairs={{0,4},{4,0},{8,12},{12,8},{16,20},{20,16},{24,28},{28,24},{32,36},... | collective-permute-start | bytes 6291464 | tf_op jit(solution)/shard_map/ppermute | solution.py:119
  44.1 9.8 %shard_map.130 = (f32[2,392,896]{2,1,0:T(8,128)}, f32[2,256,256]{2,1,0:T(8,128)}, f32[8,128]{1,0:T(8,128)}) custom-call(s32[13]{0:T(128)} %pad_add_fusion.meta_ref, f32[2,392,896]{2,1,0:T(8,128)} %select_maximum_fusion.window_ref, bf16[6,256,256]{2,1,0:T(8,128)(2,1)} %bitcast.112, f32[2,256,256]{2,1,0:T(8,128)} %probe_ref.1, ...), custom_call_target="tpu_custom_call" | custom-call | tf_op jit(solution)/shard_map/pallas_call | solution.py:251
  55.9 6.7 %collective-permute-start.2 = (f32[2,384,128]{2,1,0:T(8,128)}, f32[2,384,128]{2,1,0:T(8,128)}, u32[]{:S(2)}, u32[]{:S(2)}) collective-permute-start(f32[2,384,128]{2,1,0:T(8,128)} %get-tuple-element.34), channel_id=1, source_target_pairs={{0,64},{64,128},{128,192},{1,65},{65,129},{129,193},{2,66},{66,130... | collective-permute-start | bytes 1179656 | tf_op jit(solution)/shard_map/ppermute | solution.py:19
  66.9 6.2 %collective-permute-done.2 = f32[2,384,128]{2,1,0:T(8,128)} collective-permute-done((f32[2,384,128]{2,1,0:T(8,128)}, f32[2,384,128]{2,1,0:T(8,128)}, u32[]{:S(2)}, u32[]{:S(2)}) %collective-permute-start.2) | collective-permute-done | bytes 393248 | tf_op jit(solution)/shard_map/ppermute | solution.py:19
  77.7 10.2 %collective-permute-done.17 = f32[2,1,2,1,2,1,32,512]{7,6,5,4,3,2,1,0:T(8,128)S(1)} collective-permute-done((f32[2,1,2,1,2,1,32,512]{7,6,5,4,3,2,1,0:T(8,128)S(1)}, f32[2,1,2,1,2,1,32,512]{7,6,5,4,3,2,1,0:T(8,128)S(1)}, u32[]{:S(2)}, u32[]{:S(2)}) %collective-permute-start.17) | collective-permute-done | bytes 524320 | tf_op jit(solution)/shard_map/ppermute | solution.py:119
  96.8 13.6 %all-to-all-start = ((f32[16,1,1024]{2,1,0:T(1,128)}), f32[16,1,1024]{2,1,0:T(1,128)S(1)}, u32[]{:S(2)}, u32[]{:S(2)}) async-start(f32[16,1,1024]{2,1,0:T(1,128)} %reshape.1096), calls=%async_computation | async-start | bytes 131072 | tf_op jit(solution)/shard_map/all_to_all | solution.py:329
  116.4 3.6 %all-to-all-done = f32[16,1,1024]{2,1,0:T(1,128)S(1)} async-done(((f32[16,1,1024]{2,1,0:T(1,128)}), f32[16,1,1024]{2,1,0:T(1,128)S(1)}, u32[]{:S(2)}, u32[]{:S(2)}) %all-to-all-start) | async-done | bytes 65568 | tf_op jit(solution)/shard_map/all_to_all | solution.py:329
  126.7 3.3 %all-to-all-start.1 = ((f32[4,1,4096]{2,1,0:T(1,128)}), f32[4,1,4096]{2,1,0:T(1,128)S(1)}, u32[]{:S(2)}, u32[]{:S(2)}) async-start(f32[4,1,4096]{2,1,0:T(1,128)} %reshape.1098), calls=%async_computation.1 | async-start | bytes 131072 | tf_op jit(solution)/shard_map/all_to_all | solution.py:328
  131.8 3.2 %collective-permute-start.20 = (f32[1,1,1,1,1,1,32,512]{7,6,5,4,3,2,1,0:T(8,128)}, f32[1,1,1,1,1,1,32,512]{7,6,5,4,3,2,1,0:T(8,128)}, u32[]{:S(2)}, u32[]{:S(2)}) collective-permute-start(f32[1,1,1,1,1,1,32,512]{7,6,5,4,3,2,1,0:T(8,128)} %constant_dynamic-slice_fusion), channel_id=1, source_target_pairs={{0,8},{4,12},{8,0},{12,4},{16,24},{20,28},{24,16},{28,20},{32,40},... | collective-permute-start | bytes 196616 | tf_op jit(solution)/shard_map/ppermute | solution.py:119
  142.8 2.9 %collective-permute-start.21 = (bf16[1,1,1,1,1,1,32,512]{7,6,5,4,3,2,1,0:T(8,128)(2,1)S(1)}, bf16[1,1,1,1,1,1,32,512]{7,6,5,4,3,2,1,0:T(8,128)(2,1)S(1)}, u32[]{:S(2)}, u32[]{:S(2)}) collective-permute-start(bf16[1,1,1,1,1,1,32,512]{7,6,5,4,3,2,1,0:T(8,128)(2,1)S(1)} %subtract_convert_fusion), channel_id=1, source_target_pairs={{0,8},{4,12},{8,0},{12,4},{16,24},{20,28},{24,16},{28,20},{32,40},... | collective-permute-start | bytes 98312 | tf_op jit(solution)/shard_map/ppermute | solution.py:119
  167.9 2.9 %collective-permute-done.7 = f32[129,128]{1,0:T(8,128)S(1)} collective-permute-done((f32[129,128]{1,0:T(8,128)S(1)}, f32[129,128]{1,0:T(8,128)S(1)}, u32[]{:S(2)}, u32[]{:S(2)}) %collective-permute-start.7) | collective-permute-done | bytes 66080 | tf_op jit(solution)/shard_map/ppermute | solution.py:119
  172.7 4.5 %collective-permute-done.8 = f32[129,128]{1,0:T(8,128)S(1)} collective-permute-done((f32[129,128]{1,0:T(8,128)S(1)}, f32[129,128]{1,0:T(8,128)S(1)}, u32[]{:S(2)}, u32[]{:S(2)}) %collective-permute-start.8) | collective-permute-done | bytes 66080 | tf_op jit(solution)/shard_map/ppermute | solution.py:119
  177.2 3.5 %collective-permute-start.9 = (f32[129,128]{1,0:T(8,128)S(1)}, f32[129,128]{1,0:T(8,128)S(1)}, u32[]{:S(2)}, u32[]{:S(2)}) collective-permute-start(f32[129,128]{1,0:T(8,128)S(1)} %add.192), channel_id=1, source_target_pairs={{0,2},{1,3},{2,0},{3,1},{4,6},{5,7},{6,4},{7,5},{8,10},{9,11},{10,... | collective-permute-start | bytes 198152 | tf_op jit(solution)/shard_map/ppermute | solution.py:119
  189.8 4.9 %collective-permute-done.11 = f32[129,128]{1,0:T(8,128)S(1)} collective-permute-done((f32[129,128]{1,0:T(8,128)S(1)}, f32[129,128]{1,0:T(8,128)S(1)}, u32[]{:S(2)}, u32[]{:S(2)}) %collective-permute-start.11) | collective-permute-done | bytes 66080 | tf_op jit(solution)/shard_map/ppermute | solution.py:119
  199.4 10.0 %collective-permute-start.26 = (bf16[2,2,2,2,2,1,32,512]{7,6,5,4,3,2,1,0:T(8,128)(2,1)}, bf16[2,2,2,2,2,1,32,512]{7,6,5,4,3,2,1,0:T(8,128)(2,1)}, u32[]{:S(2)}, u32[]{:S(2)}) collective-permute-start(bf16[2,2,2,2,2,1,32,512]{7,6,5,4,3,2,1,0:T(8,128)(2,1)} %maximum_select_fusion.1), channel_id=1, source_target_pairs={{0,4},{4,0},{8,12},{12,8},{16,20},{20,16},{24,28},{28,24},{32,36},... | collective-permute-start | bytes 3145736 | tf_op jit(solution)/shard_map/ppermute | solution.py:119
  209.5 5.2 %collective-permute-done.13 = f32[258,128]{1,0:T(8,128)S(1)} collective-permute-done((f32[258,128]{1,0:T(8,128)S(1)}, f32[258,128]{1,0:T(8,128)S(1)}, u32[]{:S(2)}, u32[]{:S(2)}) %collective-permute-start.13) | collective-permute-done | bytes 132128 | tf_op jit(solution)/shard_map/ppermute | solution.py:119
  228.7 3.8 %reshape.1094 = f32[16,32,64,8]{1,0,3,2:T(8,128)} reshape(f32[512,512]{0,1:T(8,128)} %convolution_bitcast_fusion.2) | data formatting | bytes 2097152 | tf_op jit(solution)/shard_map/reshape | solution.py:370
  232.5 3.3 %multiply_reduce_fusion = f32[32,64,8]{0,2,1:T(8,128)S(1)} fusion(f32[16,32,64,8]{1,0,3,2:T(8,128)} %reshape.1094, f32[16,64]{0,1:T(8,128)S(1)} %copy-done.11), kind=kLoop, calls=%fused_computation | loop fusion | flops 507904 | bytes 1118208 | tf_op jit(solution)/shard_map/reduce_sum | solution.py:371
  235.9 3.2 %convolution_subtract_fusion = f32[8,32,2048]{2,1,0:T(8,128)} fusion(f32[8,32,2048]{2,1,0:T(8,128)S(1)} %copy-done.6, f32[64,2048,1]{1,0,2:T(8,128)S(1)} %convolution_bitcast_fusion.1, f32[64,8,32]{2,1,0:T(8,128)S(1)} %bitcast.106), kind=kOutput, calls=%fused_computation.6 | convolution fusion | flops 403177472 | bytes 4784128 | tf_op jit(solution)/shard_map/azx,ay->zxy/dot_general | solution.py:372
  (149 shorter events, 113.5 us)
Async XLA Ops:
  24.0 12.5 %collective-permute-start.15 = (f32[2,2,2,2,2,1,32,512]{7,6,5,4,3,2,1,0:T(8,128)}, f32[2,2,2,2,2,1,32,512]{7,6,5,4,3,2,1,0:T(8,128)}, u32[]{:S(2)}, u32[]{:S(2)}) collective-permute-start(f32[2,2,2,2,2,1,32,512]{7,6,5,4,3,2,1,0:T(8,128)} %constant_dynamic-slice_fusion.5), channel_id=1, source_target_pairs={{0,4},{4,0},{8,12},{12,8},{16,20},{20,16},{24,28},{28,24},{32,36},... | collective-permute-start | bytes 6291464 | tf_op jit(solution)/shard_map/ppermute | solution.py:119
  28.1 14.2 %collective-permute-start = (f32[2,384,128]{2,1,0:T(8,128)}, f32[2,384,128]{2,1,0:T(8,128)S(1)}, u32[]{:S(2)}, u32[]{:S(2)}) collective-permute-start(f32[2,384,128]{2,1,0:T(8,128)} %get-tuple-element.35), channel_id=1, source_target_pairs={{0,64},{64,128},{128,192},{1,65},{65,129},{129,193},{2,66},{66,130... | collective-permute-start | bytes 1179656 | tf_op jit(solution)/shard_map/ppermute | solution.py:19
  29.6 12.8 %collective-permute-start.1 = (f32[2,384,128]{2,1,0:T(8,128)}, f32[2,384,128]{2,1,0:T(8,128)S(1)}, u32[]{:S(2)}, u32[]{:S(2)}) collective-permute-start(f32[2,384,128]{2,1,0:T(8,128)} %get-tuple-element.36), channel_id=1, source_target_pairs={{64,0},{128,64},{192,128},{65,1},{129,65},{193,129},{66,2},{130,66... | collective-permute-start | bytes 1179656 | tf_op jit(solution)/shard_map/ppermute | solution.py:19
  40.3 34.0 %collective-permute-start.16 = (f32[2,1,2,2,2,1,32,512]{7,6,5,4,3,2,1,0:T(8,128)}, f32[2,1,2,2,2,1,32,512]{7,6,5,4,3,2,1,0:T(8,128)}, u32[]{:S(2)}, u32[]{:S(2)}) collective-permute-start(f32[2,1,2,2,2,1,32,512]{7,6,5,4,3,2,1,0:T(8,128)} %constant_dynamic-slice_fusion.4), channel_id=1, source_target_pairs={{0,64},{64,0},{128,192},{192,128},{1,65},{65,1},{129,193},{193,129... | collective-permute-start | bytes 3145736 | tf_op jit(solution)/shard_map/ppermute | solution.py:119
  55.9 17.2 %collective-permute-start.2 = (f32[2,384,128]{2,1,0:T(8,128)}, f32[2,384,128]{2,1,0:T(8,128)}, u32[]{:S(2)}, u32[]{:S(2)}) collective-permute-start(f32[2,384,128]{2,1,0:T(8,128)} %get-tuple-element.34), channel_id=1, source_target_pairs={{0,64},{64,128},{128,192},{1,65},{65,129},{129,193},{2,66},{66,130... | collective-permute-start | bytes 1179656 | tf_op jit(solution)/shard_map/ppermute | solution.py:19
  65.6 11.6 %collective-permute-start.3 = (f32[2,384,128]{2,1,0:T(8,128)S(1)}, f32[2,384,128]{2,1,0:T(8,128)S(1)}, u32[]{:S(2)}, u32[]{:S(2)}) collective-permute-start(f32[2,384,128]{2,1,0:T(8,128)S(1)} %get-tuple-element.33), channel_id=1, source_target_pairs={{64,0},{128,64},{192,128},{65,1},{129,65},{193,129},{66,2},{130,66... | collective-permute-start | bytes 1179656 | tf_op jit(solution)/shard_map/ppermute | solution.py:19
  75.9 12.1 %collective-permute-start.17 = (f32[2,1,2,1,2,1,32,512]{7,6,5,4,3,2,1,0:T(8,128)S(1)}, f32[2,1,2,1,2,1,32,512]{7,6,5,4,3,2,1,0:T(8,128)S(1)}, u32[]{:S(2)}, u32[]{:S(2)}) collective-permute-start(f32[2,1,2,1,2,1,32,512]{7,6,5,4,3,2,1,0:T(8,128)S(1)} %constant_dynamic-slice_fusion.3), channel_id=1, source_target_pairs={{0,16},{4,20},{8,24},{12,28},{16,0},{20,4},{24,8},{28,12},{32,48},... | collective-permute-start | bytes 1572872 | tf_op jit(solution)/shard_map/ppermute | solution.py:119
  89.5 32.6 %collective-permute-start.18 = (f32[1,1,2,1,2,1,32,512]{7,6,5,4,3,2,1,0:T(8,128)}, f32[1,1,2,1,2,1,32,512]{7,6,5,4,3,2,1,0:T(8,128)}, u32[]{:S(2)}, u32[]{:S(2)}) collective-permute-start(f32[1,1,2,1,2,1,32,512]{7,6,5,4,3,2,1,0:T(8,128)} %constant_dynamic-slice_fusion.2), channel_id=1, source_target_pairs={{0,128},{64,192},{128,0},{192,64},{1,129},{65,193},{129,1},{193,65... | collective-permute-start | bytes 786440 | tf_op jit(solution)/shard_map/ppermute | solution.py:119
  96.8 23.3 %all-to-all-start = ((f32[16,1,1024]{2,1,0:T(1,128)}), f32[16,1,1024]{2,1,0:T(1,128)S(1)}, u32[]{:S(2)}, u32[]{:S(2)}) async-start(f32[16,1,1024]{2,1,0:T(1,128)} %reshape.1096), calls=%async_computation | async-start | bytes 131072 | tf_op jit(solution)/shard_map/all_to_all | solution.py:329
  124.0 6.2 %collective-permute-start.19 = (f32[1,1,1,1,2,1,32,512]{7,6,5,4,3,2,1,0:T(8,128)S(1)}, f32[1,1,1,1,2,1,32,512]{7,6,5,4,3,2,1,0:T(8,128)}, u32[]{:S(2)}, u32[]{:S(2)}) collective-permute-start(f32[1,1,1,1,2,1,32,512]{7,6,5,4,3,2,1,0:T(8,128)S(1)} %constant_dynamic-slice_fusion.1), channel_id=1, source_target_pairs={{0,32},{4,36},{8,40},{12,44},{16,48},{20,52},{24,56},{28,60},{32,0... | collective-permute-start | bytes 393224 | tf_op jit(solution)/shard_map/ppermute | solution.py:119
  126.7 11.0 %all-to-all-start.1 = ((f32[4,1,4096]{2,1,0:T(1,128)}), f32[4,1,4096]{2,1,0:T(1,128)S(1)}, u32[]{:S(2)}, u32[]{:S(2)}) async-start(f32[4,1,4096]{2,1,0:T(1,128)} %reshape.1098), calls=%async_computation.1 | async-start | bytes 131072 | tf_op jit(solution)/shard_map/all_to_all | solution.py:328
  131.8 10.1 %collective-permute-start.20 = (f32[1,1,1,1,1,1,32,512]{7,6,5,4,3,2,1,0:T(8,128)}, f32[1,1,1,1,1,1,32,512]{7,6,5,4,3,2,1,0:T(8,128)}, u32[]{:S(2)}, u32[]{:S(2)}) collective-permute-start(f32[1,1,1,1,1,1,32,512]{7,6,5,4,3,2,1,0:T(8,128)} %constant_dynamic-slice_fusion), channel_id=1, source_target_pairs={{0,8},{4,12},{8,0},{12,4},{16,24},{20,28},{24,16},{28,20},{32,40},... | collective-permute-start | bytes 196616 | tf_op jit(solution)/shard_map/ppermute | solution.py:119
  136.7 9.0 %collective-permute-start.4 = (f32[516,128]{1,0:T(8,128)}, f32[516,128]{1,0:T(8,128)}, u32[]{:S(2)}, u32[]{:S(2)}) collective-permute-start(f32[516,128]{1,0:T(8,128)} %constant_dynamic-slice_fusion.8), channel_id=1, source_target_pairs={{0,4},{4,0},{8,12},{12,8},{16,20},{20,16},{24,28},{28,24},{32,36},... | collective-permute-start | bytes 792584 | tf_op jit(solution)/shard_map/ppermute | solution.py:119
  142.8 6.8 %collective-permute-start.21 = (bf16[1,1,1,1,1,1,32,512]{7,6,5,4,3,2,1,0:T(8,128)(2,1)S(1)}, bf16[1,1,1,1,1,1,32,512]{7,6,5,4,3,2,1,0:T(8,128)(2,1)S(1)}, u32[]{:S(2)}, u32[]{:S(2)}) collective-permute-start(bf16[1,1,1,1,1,1,32,512]{7,6,5,4,3,2,1,0:T(8,128)(2,1)S(1)} %subtract_convert_fusion), channel_id=1, source_target_pairs={{0,8},{4,12},{8,0},{12,4},{16,24},{20,28},{24,16},{28,20},{32,40},... | collective-permute-start | bytes 98312 | tf_op jit(solution)/shard_map/ppermute | solution.py:119
  154.3 5.4 %collective-permute-start.23 = (bf16[1,1,2,1,2,1,32,512]{7,6,5,4,3,2,1,0:T(8,128)(2,1)S(1)}, bf16[1,1,2,1,2,1,32,512]{7,6,5,4,3,2,1,0:T(8,128)(2,1)S(1)}, u32[]{:S(2)}, u32[]{:S(2)}) collective-permute-start(bf16[1,1,2,1,2,1,32,512]{7,6,5,4,3,2,1,0:T(8,128)(2,1)S(1)} %fusion.10), channel_id=1, source_target_pairs={{0,128},{64,192},{128,0},{192,64},{1,129},{65,193},{129,1},{193,65... | collective-permute-start | bytes 393224 | tf_op jit(solution)/shard_map/ppermute | solution.py:119
  154.8 6.0 %collective-permute-start.5 = (f32[258,128]{1,0:T(8,128)S(1)}, f32[258,128]{1,0:T(8,128)S(1)}, u32[]{:S(2)}, u32[]{:S(2)}) collective-permute-start(f32[258,128]{1,0:T(8,128)S(1)} %constant_dynamic-slice_fusion.7), channel_id=1, source_target_pairs={{0,64},{64,0},{128,192},{192,128},{1,65},{65,1},{129,193},{193,129... | collective-permute-start | bytes 396296 | tf_op jit(solution)/shard_map/ppermute | solution.py:119
  159.8 5.3 %collective-permute-start.24 = (bf16[2,1,2,1,2,1,32,512]{7,6,5,4,3,2,1,0:T(8,128)(2,1)S(1)}, bf16[2,1,2,1,2,1,32,512]{7,6,5,4,3,2,1,0:T(8,128)(2,1)S(1)}, u32[]{:S(2)}, u32[]{:S(2)}) collective-permute-start(bf16[2,1,2,1,2,1,32,512]{7,6,5,4,3,2,1,0:T(8,128)(2,1)S(1)} %fusion.5), channel_id=1, source_target_pairs={{0,16},{4,20},{8,24},{12,28},{16,0},{20,4},{24,8},{28,12},{32,48},... | collective-permute-start | bytes 786440 | tf_op jit(solution)/shard_map/ppermute | solution.py:119
  160.8 6.7 %collective-permute-start.6 = (f32[129,128]{1,0:T(8,128)S(1)}, f32[129,128]{1,0:T(8,128)S(1)}, u32[]{:S(2)}, u32[]{:S(2)}) collective-permute-start(f32[129,128]{1,0:T(8,128)S(1)} %constant_dynamic-slice_fusion.6), channel_id=1, source_target_pairs={{0,1},{1,0},{2,3},{3,2},{4,5},{5,4},{6,7},{7,6},{8,9},{9,8},{10,11... | collective-permute-start | bytes 198152 | tf_op jit(solution)/shard_map/ppermute | solution.py:119
  165.9 31.1 %collective-permute-start.25 = (bf16[2,1,2,2,2,1,32,512]{7,6,5,4,3,2,1,0:T(8,128)(2,1)}, bf16[2,1,2,2,2,1,32,512]{7,6,5,4,3,2,1,0:T(8,128)(2,1)}, u32[]{:S(2)}, u32[]{:S(2)}) collective-permute-start(bf16[2,1,2,2,2,1,32,512]{7,6,5,4,3,2,1,0:T(8,128)(2,1)} %maximum_select_fusion.4), channel_id=1, source_target_pairs={{0,64},{64,0},{128,192},{192,128},{1,65},{65,1},{129,193},{193,129... | collective-permute-start | bytes 1572872 | tf_op jit(solution)/shard_map/ppermute | solution.py:119
  170.8 6.4 %collective-permute-start.8 = (f32[129,128]{1,0:T(8,128)S(1)}, f32[129,128]{1,0:T(8,128)S(1)}, u32[]{:S(2)}, u32[]{:S(2)}) collective-permute-start(f32[129,128]{1,0:T(8,128)S(1)} %add.191), channel_id=1, source_target_pairs={{0,128},{64,192},{128,0},{192,64},{1,129},{65,193},{129,1},{193,65... | collective-permute-start | bytes 198152 | tf_op jit(solution)/shard_map/ppermute | solution.py:119
  177.2 5.5 %collective-permute-start.9 = (f32[129,128]{1,0:T(8,128)S(1)}, f32[129,128]{1,0:T(8,128)S(1)}, u32[]{:S(2)}, u32[]{:S(2)}) collective-permute-start(f32[129,128]{1,0:T(8,128)S(1)} %add.192), channel_id=1, source_target_pairs={{0,2},{1,3},{2,0},{3,1},{4,6},{5,7},{6,4},{7,5},{8,10},{9,11},{10,... | collective-permute-start | bytes 198152 | tf_op jit(solution)/shard_map/ppermute | solution.py:119
  187.4 7.2 %collective-permute-start.11 = (f32[129,128]{1,0:T(8,128)S(1)}, f32[129,128]{1,0:T(8,128)S(1)}, u32[]{:S(2)}, u32[]{:S(2)}) collective-permute-start(f32[129,128]{1,0:T(8,128)S(1)} %add.194), channel_id=1, source_target_pairs={{0,8},{4,12},{8,0},{12,4},{16,24},{20,28},{24,16},{28,20},{32,40},... | collective-permute-start | bytes 198152 | tf_op jit(solution)/shard_map/ppermute | solution.py:119
  194.7 14.7 %collective-permute-start.12 = (f32[129,128]{1,0:T(8,128)S(1)}, f32[129,128]{1,0:T(8,128)S(1)}, u32[]{:S(2)}, u32[]{:S(2)}) collective-permute-start(f32[129,128]{1,0:T(8,128)S(1)} %add.195), channel_id=1, source_target_pairs={{0,1},{1,0},{2,3},{3,2},{4,5},{5,4},{6,7},{7,6},{8,9},{9,8},{10,11... | collective-permute-start | bytes 198152 | tf_op jit(solution)/shard_map/ppermute | solution.py:119
  199.4 24.5 %collective-permute-start.26 = (bf16[2,2,2,2,2,1,32,512]{7,6,5,4,3,2,1,0:T(8,128)(2,1)}, bf16[2,2,2,2,2,1,32,512]{7,6,5,4,3,2,1,0:T(8,128)(2,1)}, u32[]{:S(2)}, u32[]{:S(2)}) collective-permute-start(bf16[2,2,2,2,2,1,32,512]{7,6,5,4,3,2,1,0:T(8,128)(2,1)} %maximum_select_fusion.1), channel_id=1, source_target_pairs={{0,4},{4,0},{8,12},{12,8},{16,20},{20,16},{24,28},{28,24},{32,36},... | collective-permute-start | bytes 3145736 | tf_op jit(solution)/shard_map/ppermute | solution.py:119
  (20 other events, 137.4 us)

commit v5 on v4

--- a/solution.py
+++ b/solution.py
@@ -325,24 +325,18 @@
     slab_total = admm_dual.shape[1]
     first_row = (own_object.shape[1] - slab_total) // 2
     slab_values = new_object[:, 1, first_row : first_row + slab_total, :] + admm_dual
-    arrived = lax.all_to_all(
-        lax.all_to_all(slab_values, "proj", split_axis=2, concat_axis=0, tiled=True),
-        "cuts",
-        split_axis=1,
-        concat_axis=0,
-        tiled=True,
-    )
     proj_count = lax.axis_size("proj")
     cuts_count = lax.axis_size("cuts")
-    slab_dev = arrived.shape[1]
-    u_share = arrived.shape[2]
+    slab_dev = slab_total // cuts_count
+    u_share = slab_values.shape[2] // proj_count
     projections = proj_count * cuts_count
-    arrived = arrived.reshape(cuts_count, proj_count, slab_dev, u_share).transpose(1, 0, 2, 3)
-    target = (
-        arrived.reshape(projections, slab_dev, u_share)
-        .transpose(2, 0, 1)
-        .reshape(u_share, projections * slab_dev)
-    )
+    pieces = (
+        slab_values.reshape(cuts_count, slab_dev, proj_count, u_share)
+        .transpose(2, 0, 1, 3)
+        .reshape(projections, slab_dev, u_share)
+    )
+    arrived = lax.all_to_all(pieces, ("proj", "cuts"), 0, 0, tiled=True)
+    target = arrived.transpose(2, 0, 1).reshape(u_share, projections * slab_dev)
     angle_count = ray_weights.shape[0]
     x_share = volume.shape[1]
     width = volume.shape[2]

time: 240 us -> 227 us (0.946)
  waiting for transfers between devices: 54 us -> 43.2 us
  starting transfers between devices: 75.7 us -> 72.2 us
    ppermute x4, waiting for transfers between devices: 6.19 us -> 0.01 us  [shifted(): lax.ppermute(value, axis, [(source, source + steps) for source in range(l...]
    ppermute x23, starting transfers between devices: 48.2 us -> 53.4 us  [exchange(): lax.ppermute(values, axis, [(source, source ^ 1 << bit) for source in ran...]
    all_to_all x2 -> x1, starting transfers between devices: 16.8 us -> 12.4 us  [on_device(): arrived = lax.all_to_all(pieces, ('proj', 'cuts'), 0, 0, tiled=True)]
    ppermute x4, starting transfers between devices: 10.7 us -> 6.41 us  [shifted(): lax.ppermute(value, axis, [(source, source + steps) for source in range(l...]
    all_to_all x2 -> x1, waiting for transfers between devices: 3.61 us -> 0.53 us  [on_device(): arrived = lax.all_to_all(pieces, ('proj', 'cuts'), 0, 0, tiled=True)]
    unnamed x36 -> x32, local copies, waits for them, and re-layouts: 6.99 us -> 5.02 us
  transfers between devices with their start and end apart: 29 -> 28, of which waited for: 16 -> 14; matrix products, arithmetic and copies ran while one was open for 23% -> 24% of each run, Pallas kernels for 4% -> 5%
where the time goes in v5:
time: 227 us
  starting transfers between devices  72.2 us (32%)
  waiting for transfers between devices  43.2 us (19%)
  local copies, waits for them, and re-layouts  42.3 us (19%)
  other arithmetic  41 us (18%)
  matrix products  13.5 us (6%)
  Pallas kernels  12.2 us (5%)
  between operations  2.98 us (1%)
    ppermute x23, starting transfers between devices, exchange(): lax.ppermute(values, axis, [(source, source ^ 1 << bit) for source in ran...  53.4 us
    ppermute x23, waiting for transfers between devices, exchange(): lax.ppermute(values, axis, [(source, source ^ 1 << bit) for source in ran...  42.7 us
    all_to_all x1, starting transfers between devices, on_device(): arrived = lax.all_to_all(pieces, ('proj', 'cuts'), 0, 0, tiled=True)  12.4 us
    pallas_call x1, Pallas kernels, patch_terms_all(): pl.pallas_call(patch_kernel, grid_spec=grid_spec, out_shape=[jax.ShapeDty...  12.2 us
    add x5, other arithmetic, ordered_scatter(): values = keep + exchange(send, axis, bit)  6.91 us
    dynamic_slice x6, local copies, waits for them, and re-layouts, ordered_scatter(): send = lax.dynamic_slice_in_dim(values, 1 - mine, 1, place)  6.55 us
    ppermute x4, starting transfers between devices, shifted(): lax.ppermute(value, axis, [(source, source + steps) for source in range(l...  6.41 us
    select_n x6, other arithmetic, ordered_gather(): jnp.where(mine == 0, jnp.concatenate([values, other], axis=place), jnp.co...  5.84 us
  transfers between devices with their start and end apart: 28, of which 14 were waited for; matrix products, arithmetic and copies ran while one was open for 24% of the time, Pallas kernels for 5%

profile of v5, /device:TPU:1, one launch (start us, length us, event | category | flops | bytes accessed | tf_op | source)
XLA Modules:
  0.0 227.3 jit_solution(1799316972728209557)
XLA Ops:
  3.5 3.4 %fusion = bf16[32,64,8]{1,0,2:T(8,128)(2,1)S(1)} fusion(f32[64,2048,1]{1,0,2:T(8,128)S(1)} %convolution_bitcast_fusion.1, f32[8,32,2048]{2,1,0:T(8,128)} %param.22), kind=kOutput, calls=%fused_computation.13 | convolution fusion | flops 402669568 | bytes 2654208 | tf_op jit(solution)/shard_map/zxy,ay->azx/dot_general | solution.py:349
  8.6 3.4 %mul.249 = bf16[512,512]{0,1:T(8,128)(2,1)S(1)} reshape(bf16[16,32,64,8]{1,0,3,2:T(8,128)(2,1)} %broadcast_multiply_fusion) | data formatting | bytes 1048576 | tf_op jit(solution)/shard_map/mul | solution.py:352
  12.0 3.3 %convolution_bitcast_fusion = f32[2048,512]{0,1:T(8,128)} fusion(bf16[512,512]{0,1:T(8,128)(2,1)S(1)} %mul.249, bf16[512,2048]{1,0:T(8,128)(2,1)S(1)} %bitcast.88), kind=kOutput, calls=%fused_computation.1 | convolution fusion | flops 1073741824 | bytes 6815744 | tf_op jit(solution)/shard_map/dot_general | solution.py:355
  15.2 5.3 %copy.60 = f32[2048,512]{1,0:T(8,128)} copy(f32[2048,512]{0,1:T(8,128)} %convolution_bitcast_fusion) | data formatting | bytes 8388608 | tf_op jit(solution)/shard_map/dot_general | solution.py:355
  20.6 3.3 %constant_dynamic-slice_fusion.5 = f32[2,2,2,2,2,1,32,512]{7,6,5,4,3,2,1,0:T(8,128)} fusion(f32[2,2,2,2,2,2,32,512]{7,6,5,4,3,2,1,0:T(8,128)} %bitcast.90, s32[]{:T(128)S(6)} %select_n.344), kind=kLoop, calls=%fused_computation.78 | loop fusion | bytes 4194308 | tf_op jit(solution)/shard_map/dynamic_slice | solution.py:98
  23.9 3.2 %collective-permute-start.15 = (f32[2,2,2,2,2,1,32,512]{7,6,5,4,3,2,1,0:T(8,128)}, f32[2,2,2,2,2,1,32,512]{7,6,5,4,3,2,1,0:T(8,128)}, u32[]{:S(2)}, u32[]{:S(2)}) collective-permute-start(f32[2,2,2,2,2,1,32,512]{7,6,5,4,3,2,1,0:T(8,128)} %constant_dynamic-slice_fusion.5), channel_id=1, source_target_pairs={{0,4},{4,0},{8,12},{12,8},{16,20},{20,16},{24,28},{28,24},{32,36},... | collective-permute-start | bytes 6291464 | tf_op jit(solution)/shard_map/ppermute | solution.py:119
  46.2 12.2 %shard_map.130 = (f32[2,392,896]{2,1,0:T(8,128)}, f32[2,256,256]{2,1,0:T(8,128)}, f32[8,128]{1,0:T(8,128)}) custom-call(s32[13]{0:T(128)} %pad_add_fusion.meta_ref, f32[2,392,896]{2,1,0:T(8,128)} %select_maximum_fusion.window_ref, bf16[6,256,256]{2,1,0:T(8,128)(2,1)} %bitcast.101, f32[2,256,256]{2,1,0:T(8,128)} %probe_ref.1, ...), custom_call_target="tpu_custom_call" | custom-call | tf_op jit(solution)/shard_map/pallas_call | solution.py:251
  68.3 2.9 %collective-permute-start.17 = (f32[2,1,2,1,2,1,32,512]{7,6,5,4,3,2,1,0:T(8,128)}, f32[2,1,2,1,2,1,32,512]{7,6,5,4,3,2,1,0:T(8,128)}, u32[]{:S(2)}, u32[]{:S(2)}) collective-permute-start(f32[2,1,2,1,2,1,32,512]{7,6,5,4,3,2,1,0:T(8,128)} %constant_dynamic-slice_fusion.3), channel_id=1, source_target_pairs={{0,16},{4,20},{8,24},{12,28},{16,0},{20,4},{24,8},{28,12},{32,48},... | collective-permute-start | bytes 1572872 | tf_op jit(solution)/shard_map/ppermute | solution.py:119
  86.7 4.7 %collective-permute-start.18 = (f32[1,1,2,1,2,1,32,512]{7,6,5,4,3,2,1,0:T(8,128)S(1)}, f32[1,1,2,1,2,1,32,512]{7,6,5,4,3,2,1,0:T(8,128)S(1)}, u32[]{:S(2)}, u32[]{:S(2)}) collective-permute-start(f32[1,1,2,1,2,1,32,512]{7,6,5,4,3,2,1,0:T(8,128)S(1)} %constant_dynamic-slice_fusion.2), channel_id=1, source_target_pairs={{0,128},{64,192},{128,0},{192,64},{1,129},{65,193},{129,1},{193,65... | collective-permute-start | bytes 786440 | tf_op jit(solution)/shard_map/ppermute | solution.py:119
  91.9 4.5 %collective-permute-done.18 = f32[1,1,2,1,2,1,32,512]{7,6,5,4,3,2,1,0:T(8,128)S(1)} collective-permute-done((f32[1,1,2,1,2,1,32,512]{7,6,5,4,3,2,1,0:T(8,128)S(1)}, f32[1,1,2,1,2,1,32,512]{7,6,5,4,3,2,1,0:T(8,128)S(1)}, u32[]{:S(2)}, u32[]{:S(2)}) %collective-permute-start.18) | collective-permute-done | bytes 262176 | tf_op jit(solution)/shard_map/ppermute | solution.py:119
  97.2 4.1 %collective-permute-start.19 = (f32[1,1,1,1,2,1,32,512]{7,6,5,4,3,2,1,0:T(8,128)}, f32[1,1,1,1,2,1,32,512]{7,6,5,4,3,2,1,0:T(8,128)}, u32[]{:S(2)}, u32[]{:S(2)}) collective-permute-start(f32[1,1,1,1,2,1,32,512]{7,6,5,4,3,2,1,0:T(8,128)} %constant_dynamic-slice_fusion.1), channel_id=1, source_target_pairs={{0,32},{4,36},{8,40},{12,44},{16,48},{20,52},{24,56},{28,60},{32,0... | collective-permute-start | bytes 393224 | tf_op jit(solution)/shard_map/ppermute | solution.py:119
  103.9 12.4 %all-to-all-start = ((f32[64,1,256]{2,1,0:T(1,128)}), f32[64,1,256]{2,1,0:T(1,128)S(1)}, u32[]{:S(2)}, u32[]{:S(2)}) async-start(f32[64,1,256]{2,1,0:T(1,128)} %reshape.1097), calls=%async_computation | async-start | bytes 131072 | tf_op jit(solution)/shard_map/all_to_all | solution.py:338
  117.9 5.3 %collective-permute-start.20 = (f32[1,1,1,1,1,1,32,512]{7,6,5,4,3,2,1,0:T(8,128)}, f32[1,1,1,1,1,1,32,512]{7,6,5,4,3,2,1,0:T(8,128)}, u32[]{:S(2)}, u32[]{:S(2)}) collective-permute-start(f32[1,1,1,1,1,1,32,512]{7,6,5,4,3,2,1,0:T(8,128)} %constant_dynamic-slice_fusion), channel_id=1, source_target_pairs={{0,8},{4,12},{8,0},{12,4},{16,24},{20,28},{24,16},{28,20},{32,40},... | collective-permute-start | bytes 196616 | tf_op jit(solution)/shard_map/ppermute | solution.py:119
  133.3 4.2 %collective-permute-done.21 = bf16[1,1,1,1,1,1,32,512]{7,6,5,4,3,2,1,0:T(8,128)(2,1)S(1)} collective-permute-done((bf16[1,1,1,1,1,1,32,512]{7,6,5,4,3,2,1,0:T(8,128)(2,1)S(1)}, bf16[1,1,1,1,1,1,32,512]{7,6,5,4,3,2,1,0:T(8,128)(2,1)S(1)}, u32[]{:S(2)}, u32[]{:S(2)}) %collective-permute-start.21) | collective-permute-done | bytes 32800 | tf_op jit(solution)/shard_map/ppermute | solution.py:119
  137.5 3.2 %collective-permute-start.22 = (bf16[1,1,1,1,2,1,32,512]{7,6,5,4,3,2,1,0:T(8,128)(2,1)S(1)}, bf16[1,1,1,1,2,1,32,512]{7,6,5,4,3,2,1,0:T(8,128)(2,1)S(1)}, u32[]{:S(2)}, u32[]{:S(2)}) collective-permute-start(bf16[1,1,1,1,2,1,32,512]{7,6,5,4,3,2,1,0:T(8,128)(2,1)S(1)} %maximum_select_fusion.10), channel_id=1, source_target_pairs={{0,32},{4,36},{8,40},{12,44},{16,48},{20,52},{24,56},{28,60},{32,0... | collective-permute-start | bytes 196616 | tf_op jit(solution)/shard_map/ppermute | solution.py:119
  160.4 5.0 %collective-permute-done.8 = f32[129,128]{1,0:T(8,128)S(1)} collective-permute-done((f32[129,128]{1,0:T(8,128)S(1)}, f32[129,128]{1,0:T(8,128)S(1)}, u32[]{:S(2)}, u32[]{:S(2)}) %collective-permute-start.8) | collective-permute-done | bytes 66080 | tf_op jit(solution)/shard_map/ppermute | solution.py:119
  165.8 4.4 %collective-permute-done.9 = f32[129,128]{1,0:T(8,128)S(1)} collective-permute-done((f32[129,128]{1,0:T(8,128)S(1)}, f32[129,128]{1,0:T(8,128)S(1)}, u32[]{:S(2)}, u32[]{:S(2)}) %collective-permute-start.9) | collective-permute-done | bytes 66080 | tf_op jit(solution)/shard_map/ppermute | solution.py:119
  170.2 3.0 %collective-permute-start.10 = (f32[129,128]{1,0:T(8,128)S(1)}, f32[129,128]{1,0:T(8,128)S(1)}, u32[]{:S(2)}, u32[]{:S(2)}) collective-permute-start(f32[129,128]{1,0:T(8,128)S(1)} %add.193), channel_id=1, source_target_pairs={{0,32},{4,36},{8,40},{12,44},{16,48},{20,52},{24,56},{28,60},{32,0... | collective-permute-start | bytes 198152 | tf_op jit(solution)/shard_map/ppermute | solution.py:119
  175.6 6.9 %collective-permute-done.11 = f32[129,128]{1,0:T(8,128)S(1)} collective-permute-done((f32[129,128]{1,0:T(8,128)S(1)}, f32[129,128]{1,0:T(8,128)S(1)}, u32[]{:S(2)}, u32[]{:S(2)}) %collective-permute-start.11) | collective-permute-done | bytes 66080 | tf_op jit(solution)/shard_map/ppermute | solution.py:119
  186.8 10.8 %collective-permute-start.26 = (bf16[2,2,2,2,2,1,32,512]{7,6,5,4,3,2,1,0:T(8,128)(2,1)}, bf16[2,2,2,2,2,1,32,512]{7,6,5,4,3,2,1,0:T(8,128)(2,1)}, u32[]{:S(2)}, u32[]{:S(2)}) collective-permute-start(bf16[2,2,2,2,2,1,32,512]{7,6,5,4,3,2,1,0:T(8,128)(2,1)} %maximum_select_fusion.1), channel_id=1, source_target_pairs={{0,4},{4,0},{8,12},{12,8},{16,20},{20,16},{24,28},{28,24},{32,36},... | collective-permute-start | bytes 3145736 | tf_op jit(solution)/shard_map/ppermute | solution.py:119
  197.8 4.6 %collective-permute-done.13 = f32[258,128]{1,0:T(8,128)S(1)} collective-permute-done((f32[258,128]{1,0:T(8,128)S(1)}, f32[258,128]{1,0:T(8,128)S(1)}, u32[]{:S(2)}, u32[]{:S(2)}) %collective-permute-start.13) | collective-permute-done | bytes 132128 | tf_op jit(solution)/shard_map/ppermute | solution.py:119
  217.0 3.8 %reshape.1095 = f32[16,32,64,8]{1,0,3,2:T(8,128)} reshape(f32[512,512]{0,1:T(8,128)} %convolution_bitcast_fusion.2) | data formatting | bytes 2097152 | tf_op jit(solution)/shard_map/reshape | solution.py:364
  220.7 3.3 %multiply_reduce_fusion = f32[32,64,8]{0,2,1:T(8,128)S(1)} fusion(f32[16,32,64,8]{1,0,3,2:T(8,128)} %reshape.1095, f32[16,64]{0,1:T(8,128)S(1)} %copy-done.11), kind=kLoop, calls=%fused_computation | loop fusion | flops 507904 | bytes 1118208 | tf_op jit(solution)/shard_map/reduce_sum | solution.py:365
  224.1 3.2 %convolution_subtract_fusion = f32[8,32,2048]{2,1,0:T(8,128)} fusion(f32[8,32,2048]{2,1,0:T(8,128)S(1)} %copy-done.5, f32[64,2048,1]{1,0,2:T(8,128)S(1)} %convolution_bitcast_fusion.1, f32[64,8,32]{2,1,0:T(8,128)S(1)} %bitcast.97), kind=kOutput, calls=%fused_computation.6 | convolution fusion | flops 403177472 | bytes 4784128 | tf_op jit(solution)/shard_map/azx,ay->zxy/dot_general | solution.py:366
  (141 shorter events, 103.8 us)
Async XLA Ops:
  23.9 8.7 %collective-permute-start.15 = (f32[2,2,2,2,2,1,32,512]{7,6,5,4,3,2,1,0:T(8,128)}, f32[2,2,2,2,2,1,32,512]{7,6,5,4,3,2,1,0:T(8,128)}, u32[]{:S(2)}, u32[]{:S(2)}) collective-permute-start(f32[2,2,2,2,2,1,32,512]{7,6,5,4,3,2,1,0:T(8,128)} %constant_dynamic-slice_fusion.5), channel_id=1, source_target_pairs={{0,4},{4,0},{8,12},{12,8},{16,20},{20,16},{24,28},{28,24},{32,36},... | collective-permute-start | bytes 6291464 | tf_op jit(solution)/shard_map/ppermute | solution.py:119
  28.1 15.4 %collective-permute-start = (f32[2,384,128]{2,1,0:T(8,128)}, f32[2,384,128]{2,1,0:T(8,128)S(1)}, u32[]{:S(2)}, u32[]{:S(2)}) collective-permute-start(f32[2,384,128]{2,1,0:T(8,128)} %get-tuple-element.35), channel_id=1, source_target_pairs={{0,64},{64,128},{128,192},{1,65},{65,129},{129,193},{2,66},{66,130... | collective-permute-start | bytes 1179656 | tf_op jit(solution)/shard_map/ppermute | solution.py:19
  29.6 13.9 %collective-permute-start.1 = (f32[2,384,128]{2,1,0:T(8,128)}, f32[2,384,128]{2,1,0:T(8,128)}, u32[]{:S(2)}, u32[]{:S(2)}) collective-permute-start(f32[2,384,128]{2,1,0:T(8,128)} %get-tuple-element.36), channel_id=1, source_target_pairs={{64,0},{128,64},{192,128},{65,1},{129,65},{193,129},{66,2},{130,66... | collective-permute-start | bytes 1179656 | tf_op jit(solution)/shard_map/ppermute | solution.py:19
  37.7 26.9 %collective-permute-start.16 = (f32[2,1,2,2,2,1,32,512]{7,6,5,4,3,2,1,0:T(8,128)}, f32[2,1,2,2,2,1,32,512]{7,6,5,4,3,2,1,0:T(8,128)}, u32[]{:S(2)}, u32[]{:S(2)}) collective-permute-start(f32[2,1,2,2,2,1,32,512]{7,6,5,4,3,2,1,0:T(8,128)} %constant_dynamic-slice_fusion.4), channel_id=1, source_target_pairs={{0,64},{64,0},{128,192},{192,128},{1,65},{65,1},{129,193},{193,129... | collective-permute-start | bytes 3145736 | tf_op jit(solution)/shard_map/ppermute | solution.py:119
  60.3 21.0 %collective-permute-start.2 = (f32[2,384,128]{2,1,0:T(8,128)}, f32[2,384,128]{2,1,0:T(8,128)}, u32[]{:S(2)}, u32[]{:S(2)}) collective-permute-start(f32[2,384,128]{2,1,0:T(8,128)} %get-tuple-element.34), channel_id=1, source_target_pairs={{0,64},{64,128},{128,192},{1,65},{65,129},{129,193},{2,66},{66,130... | collective-permute-start | bytes 1179656 | tf_op jit(solution)/shard_map/ppermute | solution.py:19
  62.4 21.0 %collective-permute-start.3 = (f32[2,384,128]{2,1,0:T(8,128)S(1)}, f32[2,384,128]{2,1,0:T(8,128)}, u32[]{:S(2)}, u32[]{:S(2)}) collective-permute-start(f32[2,384,128]{2,1,0:T(8,128)S(1)} %get-tuple-element.33), channel_id=1, source_target_pairs={{64,0},{128,64},{192,128},{65,1},{129,65},{193,129},{66,2},{130,66... | collective-permute-start | bytes 1179656 | tf_op jit(solution)/shard_map/ppermute | solution.py:19
  68.3 17.0 %collective-permute-start.17 = (f32[2,1,2,1,2,1,32,512]{7,6,5,4,3,2,1,0:T(8,128)}, f32[2,1,2,1,2,1,32,512]{7,6,5,4,3,2,1,0:T(8,128)}, u32[]{:S(2)}, u32[]{:S(2)}) collective-permute-start(f32[2,1,2,1,2,1,32,512]{7,6,5,4,3,2,1,0:T(8,128)} %constant_dynamic-slice_fusion.3), channel_id=1, source_target_pairs={{0,16},{4,20},{8,24},{12,28},{16,0},{20,4},{24,8},{28,12},{32,48},... | collective-permute-start | bytes 1572872 | tf_op jit(solution)/shard_map/ppermute | solution.py:119
  86.7 9.7 %collective-permute-start.18 = (f32[1,1,2,1,2,1,32,512]{7,6,5,4,3,2,1,0:T(8,128)S(1)}, f32[1,1,2,1,2,1,32,512]{7,6,5,4,3,2,1,0:T(8,128)S(1)}, u32[]{:S(2)}, u32[]{:S(2)}) collective-permute-start(f32[1,1,2,1,2,1,32,512]{7,6,5,4,3,2,1,0:T(8,128)S(1)} %constant_dynamic-slice_fusion.2), channel_id=1, source_target_pairs={{0,128},{64,192},{128,0},{192,64},{1,129},{65,193},{129,1},{193,65... | collective-permute-start | bytes 786440 | tf_op jit(solution)/shard_map/ppermute | solution.py:119
  97.2 19.1 %collective-permute-start.19 = (f32[1,1,1,1,2,1,32,512]{7,6,5,4,3,2,1,0:T(8,128)}, f32[1,1,1,1,2,1,32,512]{7,6,5,4,3,2,1,0:T(8,128)}, u32[]{:S(2)}, u32[]{:S(2)}) collective-permute-start(f32[1,1,1,1,2,1,32,512]{7,6,5,4,3,2,1,0:T(8,128)} %constant_dynamic-slice_fusion.1), channel_id=1, source_target_pairs={{0,32},{4,36},{8,40},{12,44},{16,48},{20,52},{24,56},{28,60},{32,0... | collective-permute-start | bytes 393224 | tf_op jit(solution)/shard_map/ppermute | solution.py:119
  103.9 22.2 %all-to-all-start = ((f32[64,1,256]{2,1,0:T(1,128)}), f32[64,1,256]{2,1,0:T(1,128)S(1)}, u32[]{:S(2)}, u32[]{:S(2)}) async-start(f32[64,1,256]{2,1,0:T(1,128)} %reshape.1097), calls=%async_computation | async-start | bytes 131072 | tf_op jit(solution)/shard_map/all_to_all | solution.py:338
  117.9 11.9 %collective-permute-start.20 = (f32[1,1,1,1,1,1,32,512]{7,6,5,4,3,2,1,0:T(8,128)}, f32[1,1,1,1,1,1,32,512]{7,6,5,4,3,2,1,0:T(8,128)}, u32[]{:S(2)}, u32[]{:S(2)}) collective-permute-start(f32[1,1,1,1,1,1,32,512]{7,6,5,4,3,2,1,0:T(8,128)} %constant_dynamic-slice_fusion), channel_id=1, source_target_pairs={{0,8},{4,12},{8,0},{12,4},{16,24},{20,28},{24,16},{28,20},{32,40},... | collective-permute-start | bytes 196616 | tf_op jit(solution)/shard_map/ppermute | solution.py:119
  124.9 7.3 %collective-permute-start.4 = (f32[516,128]{1,0:T(8,128)}, f32[516,128]{1,0:T(8,128)}, u32[]{:S(2)}, u32[]{:S(2)}) collective-permute-start(f32[516,128]{1,0:T(8,128)} %constant_dynamic-slice_fusion.8), channel_id=1, source_target_pairs={{0,4},{4,0},{8,12},{12,8},{16,20},{20,16},{24,28},{28,24},{32,36},... | collective-permute-start | bytes 792584 | tf_op jit(solution)/shard_map/ppermute | solution.py:119
  130.7 6.8 %collective-permute-start.21 = (bf16[1,1,1,1,1,1,32,512]{7,6,5,4,3,2,1,0:T(8,128)(2,1)S(1)}, bf16[1,1,1,1,1,1,32,512]{7,6,5,4,3,2,1,0:T(8,128)(2,1)S(1)}, u32[]{:S(2)}, u32[]{:S(2)}) collective-permute-start(bf16[1,1,1,1,1,1,32,512]{7,6,5,4,3,2,1,0:T(8,128)(2,1)S(1)} %subtract_convert_fusion), channel_id=1, source_target_pairs={{0,8},{4,12},{8,0},{12,4},{16,24},{20,28},{24,16},{28,20},{32,40},... | collective-permute-start | bytes 98312 | tf_op jit(solution)/shard_map/ppermute | solution.py:119
  142.4 5.4 %collective-permute-start.23 = (bf16[1,1,2,1,2,1,32,512]{7,6,5,4,3,2,1,0:T(8,128)(2,1)S(1)}, bf16[1,1,2,1,2,1,32,512]{7,6,5,4,3,2,1,0:T(8,128)(2,1)S(1)}, u32[]{:S(2)}, u32[]{:S(2)}) collective-permute-start(bf16[1,1,2,1,2,1,32,512]{7,6,5,4,3,2,1,0:T(8,128)(2,1)S(1)} %fusion.10), channel_id=1, source_target_pairs={{0,128},{64,192},{128,0},{192,64},{1,129},{65,193},{129,1},{193,65... | collective-permute-start | bytes 393224 | tf_op jit(solution)/shard_map/ppermute | solution.py:119
  142.7 6.6 %collective-permute-start.5 = (f32[258,128]{1,0:T(8,128)S(1)}, f32[258,128]{1,0:T(8,128)S(1)}, u32[]{:S(2)}, u32[]{:S(2)}) collective-permute-start(f32[258,128]{1,0:T(8,128)S(1)} %constant_dynamic-slice_fusion.7), channel_id=1, source_target_pairs={{0,64},{64,0},{128,192},{192,128},{1,65},{65,1},{129,193},{193,129... | collective-permute-start | bytes 396296 | tf_op jit(solution)/shard_map/ppermute | solution.py:119
  147.9 5.3 %collective-permute-start.24 = (bf16[2,1,2,1,2,1,32,512]{7,6,5,4,3,2,1,0:T(8,128)(2,1)S(1)}, bf16[2,1,2,1,2,1,32,512]{7,6,5,4,3,2,1,0:T(8,128)(2,1)S(1)}, u32[]{:S(2)}, u32[]{:S(2)}) collective-permute-start(bf16[2,1,2,1,2,1,32,512]{7,6,5,4,3,2,1,0:T(8,128)(2,1)S(1)} %fusion.5), channel_id=1, source_target_pairs={{0,16},{4,20},{8,24},{12,28},{16,0},{20,4},{24,8},{28,12},{32,48},... | collective-permute-start | bytes 786440 | tf_op jit(solution)/shard_map/ppermute | solution.py:119
  149.4 7.0 %collective-permute-start.6 = (f32[129,128]{1,0:T(8,128)S(1)}, f32[129,128]{1,0:T(8,128)S(1)}, u32[]{:S(2)}, u32[]{:S(2)}) collective-permute-start(f32[129,128]{1,0:T(8,128)S(1)} %constant_dynamic-slice_fusion.6), channel_id=1, source_target_pairs={{0,1},{1,0},{2,3},{3,2},{4,5},{5,4},{6,7},{7,6},{8,9},{9,8},{10,11... | collective-permute-start | bytes 198152 | tf_op jit(solution)/shard_map/ppermute | solution.py:119
  154.0 30.4 %collective-permute-start.25 = (bf16[2,1,2,2,2,1,32,512]{7,6,5,4,3,2,1,0:T(8,128)(2,1)}, bf16[2,1,2,2,2,1,32,512]{7,6,5,4,3,2,1,0:T(8,128)(2,1)}, u32[]{:S(2)}, u32[]{:S(2)}) collective-permute-start(bf16[2,1,2,2,2,1,32,512]{7,6,5,4,3,2,1,0:T(8,128)(2,1)} %maximum_select_fusion.4), channel_id=1, source_target_pairs={{0,64},{64,0},{128,192},{192,128},{1,65},{65,1},{129,193},{193,129... | collective-permute-start | bytes 1572872 | tf_op jit(solution)/shard_map/ppermute | solution.py:119
  159.7 5.7 %collective-permute-start.8 = (f32[129,128]{1,0:T(8,128)S(1)}, f32[129,128]{1,0:T(8,128)S(1)}, u32[]{:S(2)}, u32[]{:S(2)}) collective-permute-start(f32[129,128]{1,0:T(8,128)S(1)} %add.191), channel_id=1, source_target_pairs={{0,128},{64,192},{128,0},{192,64},{1,129},{65,193},{129,1},{193,65... | collective-permute-start | bytes 198152 | tf_op jit(solution)/shard_map/ppermute | solution.py:119
  165.3 4.9 %collective-permute-start.9 = (f32[129,128]{1,0:T(8,128)S(1)}, f32[129,128]{1,0:T(8,128)S(1)}, u32[]{:S(2)}, u32[]{:S(2)}) collective-permute-start(f32[129,128]{1,0:T(8,128)S(1)} %add.192), channel_id=1, source_target_pairs={{0,2},{1,3},{2,0},{3,1},{4,6},{5,7},{6,4},{7,5},{8,10},{9,11},{10,... | collective-permute-start | bytes 198152 | tf_op jit(solution)/shard_map/ppermute | solution.py:119
  170.2 5.0 %collective-permute-start.10 = (f32[129,128]{1,0:T(8,128)S(1)}, f32[129,128]{1,0:T(8,128)S(1)}, u32[]{:S(2)}, u32[]{:S(2)}) collective-permute-start(f32[129,128]{1,0:T(8,128)S(1)} %add.193), channel_id=1, source_target_pairs={{0,32},{4,36},{8,40},{12,44},{16,48},{20,52},{24,56},{28,60},{32,0... | collective-permute-start | bytes 198152 | tf_op jit(solution)/shard_map/ppermute | solution.py:119
  175.2 7.2 %collective-permute-start.11 = (f32[129,128]{1,0:T(8,128)S(1)}, f32[129,128]{1,0:T(8,128)S(1)}, u32[]{:S(2)}, u32[]{:S(2)}) collective-permute-start(f32[129,128]{1,0:T(8,128)S(1)} %add.194), channel_id=1, source_target_pairs={{0,8},{4,12},{8,0},{12,4},{16,24},{20,28},{24,16},{28,20},{32,40},... | collective-permute-start | bytes 198152 | tf_op jit(solution)/shard_map/ppermute | solution.py:119
  182.5 15.1 %collective-permute-start.12 = (f32[129,128]{1,0:T(8,128)S(1)}, f32[129,128]{1,0:T(8,128)S(1)}, u32[]{:S(2)}, u32[]{:S(2)}) collective-permute-start(f32[129,128]{1,0:T(8,128)S(1)} %add.195), channel_id=1, source_target_pairs={{0,1},{1,0},{2,3},{3,2},{4,5},{5,4},{6,7},{7,6},{8,9},{9,8},{10,11... | collective-permute-start | bytes 198152 | tf_op jit(solution)/shard_map/ppermute | solution.py:119
  186.8 25.3 %collective-permute-start.26 = (bf16[2,2,2,2,2,1,32,512]{7,6,5,4,3,2,1,0:T(8,128)(2,1)}, bf16[2,2,2,2,2,1,32,512]{7,6,5,4,3,2,1,0:T(8,128)(2,1)}, u32[]{:S(2)}, u32[]{:S(2)}) collective-permute-start(bf16[2,2,2,2,2,1,32,512]{7,6,5,4,3,2,1,0:T(8,128)(2,1)} %maximum_select_fusion.1), channel_id=1, source_target_pairs={{0,4},{4,0},{8,12},{12,8},{16,20},{20,16},{24,28},{28,24},{32,36},... | collective-permute-start | bytes 3145736 | tf_op jit(solution)/shard_map/ppermute | solution.py:119
  (19 other events, 106.1 us)

commit v6 on v5

--- a/solution.py
+++ b/solution.py
@@ -359,7 +359,10 @@
     volume_order = link_order(volume_steps)
     own_rows = ordered_scatter(partial_term, volume_steps, volume_order)
     own_residue = (own_rows - target).astype(jnp.bfloat16)
-    residue = ordered_gather(own_residue, volume_steps, volume_order)
+    spread_count = lax.axis_size("tile") * lax.axis_size("proj")
+    copies = jnp.broadcast_to(own_residue[None], (spread_count,) + own_residue.shape)
+    residue = lax.all_to_all(copies, ("tile", "proj"), 0, 0, tiled=True)
+    residue = residue.reshape((-1,) + own_residue.shape[1:])
     backproj = matmul(weight_flat, residue)
     backproj = backproj.reshape(angle_count, x_share, projections, slab_dev)
     back_sums = jnp.sum(backproj * onehot.T[:, None, :, None], axis=0).transpose(1, 2, 0)

time: 227 us -> 253 us (1.11)
  waiting for transfers between devices: 43.2 us -> 68.8 us
  other arithmetic: 41 us -> 33.4 us
  starting transfers between devices: 72.2 us -> 79.5 us
    ppermute x23 -> x17, waiting for transfers between devices: 42.7 us -> 63.5 us  [exchange(): lax.ppermute(values, axis, [(source, source ^ 1 << bit) for source in ran...]
    all_to_all x0 -> x1, starting transfers between devices: none -> 9.8 us  [on_device(): residue = lax.all_to_all(copies, ('tile', 'proj'), 0, 0, tiled=True)]
    select_n x6 -> x0, other arithmetic: 5.84 us -> none  [ordered_gather(): jnp.where(mine == 0, jnp.concatenate([values, other], axis=place), jnp.co...]
    ppermute x23 -> x17, starting transfers between devices: 53.4 us -> 49.7 us  [exchange(): lax.ppermute(values, axis, [(source, source ^ 1 << bit) for source in ran...]
  transfers between devices with their start and end apart: 28 -> 23, of which waited for: 14 -> 16; matrix products, arithmetic and copies ran while one was open for 24% -> 18% of each run, Pallas kernels for 5% -> 4%
where the time goes in v6:
time: 253 us; the launch traced here: 252 us
  starting transfers between devices  79.5 us (31%)
  waiting for transfers between devices  68.8 us (27%)
  local copies, waits for them, and re-layouts  42.2 us (17%)
  other arithmetic  33.4 us (13%)
  matrix products  15 us (6%)
  Pallas kernels  9.68 us (4%)
  between operations  2.95 us (1%)
    ppermute x17, waiting for transfers between devices, exchange(): lax.ppermute(values, axis, [(source, source ^ 1 << bit) for source in ran...  63.5 us
    ppermute x17, starting transfers between devices, exchange(): lax.ppermute(values, axis, [(source, source ^ 1 << bit) for source in ran...  49.7 us
    all_to_all x1, starting transfers between devices, on_device(): arrived = lax.all_to_all(pieces, ('proj', 'cuts'), 0, 0, tiled=True)  13 us
    all_to_all x1, starting transfers between devices, on_device(): residue = lax.all_to_all(copies, ('tile', 'proj'), 0, 0, tiled=True)  9.8 us
    pallas_call x1, Pallas kernels, patch_terms_all(): pl.pallas_call(patch_kernel, grid_spec=grid_spec, out_shape=[jax.ShapeDty...  9.68 us
    ppermute x4, starting transfers between devices, shifted(): lax.ppermute(value, axis, [(source, source + steps) for source in range(l...  7.02 us
    add x5, other arithmetic, ordered_scatter(): values = keep + exchange(send, axis, bit)  6.64 us
    dynamic_slice x6, local copies, waits for them, and re-layouts, ordered_scatter(): send = lax.dynamic_slice_in_dim(values, 1 - mine, 1, place)  6.57 us
  transfers between devices with their start and end apart: 23, of which 16 were waited for; matrix products, arithmetic and copies ran while one was open for 18% of the time, Pallas kernels for 4%

profile of v6, /device:TPU:1, one launch (start us, length us, event | category | flops | bytes accessed | tf_op | source)
XLA Modules:
  0.0 251.5 jit_solution(14721426001168375732)
XLA Ops:
  3.5 3.4 %fusion = bf16[32,64,8]{1,0,2:T(8,128)(2,1)S(1)} fusion(f32[64,2048,1]{1,0,2:T(8,128)S(1)} %convolution_bitcast_fusion.1, f32[8,32,2048]{2,1,0:T(8,128)} %param.22), kind=kOutput, calls=%fused_computation.12 | convolution fusion | flops 402669568 | bytes 2654208 | tf_op jit(solution)/shard_map/zxy,ay->azx/dot_general | solution.py:349
  8.6 3.4 %mul.249 = bf16[512,512]{0,1:T(8,128)(2,1)S(1)} reshape(bf16[16,32,64,8]{1,0,3,2:T(8,128)(2,1)} %broadcast_multiply_fusion) | data formatting | bytes 1048576 | tf_op jit(solution)/shard_map/mul | solution.py:352
  12.0 3.3 %convolution_bitcast_fusion = f32[2048,512]{0,1:T(8,128)} fusion(bf16[512,512]{0,1:T(8,128)(2,1)S(1)} %mul.249, bf16[512,2048]{1,0:T(8,128)(2,1)S(1)} %bitcast.51), kind=kOutput, calls=%fused_computation.1 | convolution fusion | flops 1073741824 | bytes 6815744 | tf_op jit(solution)/shard_map/dot_general | solution.py:355
  15.2 5.3 %copy.26 = f32[2048,512]{1,0:T(8,128)} copy(f32[2048,512]{0,1:T(8,128)} %convolution_bitcast_fusion) | data formatting | bytes 8388608 | tf_op jit(solution)/shard_map/dot_general | solution.py:355
  20.6 3.3 %constant_dynamic-slice_fusion.5 = f32[2,2,2,2,2,1,32,512]{7,6,5,4,3,2,1,0:T(8,128)} fusion(f32[2,2,2,2,2,2,32,512]{7,6,5,4,3,2,1,0:T(8,128)} %bitcast.53, s32[]{:T(128)S(6)} %select_n.129), kind=kLoop, calls=%fused_computation.64 | loop fusion | bytes 4194308 | tf_op jit(solution)/shard_map/dynamic_slice | solution.py:98
  23.9 3.2 %collective-permute-start.15 = (f32[2,2,2,2,2,1,32,512]{7,6,5,4,3,2,1,0:T(8,128)}, f32[2,2,2,2,2,1,32,512]{7,6,5,4,3,2,1,0:T(8,128)}, u32[]{:S(2)}, u32[]{:S(2)}) collective-permute-start(f32[2,2,2,2,2,1,32,512]{7,6,5,4,3,2,1,0:T(8,128)} %constant_dynamic-slice_fusion.5), channel_id=1, source_target_pairs={{0,4},{4,0},{8,12},{12,8},{16,20},{20,16},{24,28},{28,24},{32,36},... | collective-permute-start | bytes 6291464 | tf_op jit(solution)/shard_map/ppermute | solution.py:119
  46.3 9.7 %shard_map.130 = (f32[2,392,896]{2,1,0:T(8,128)}, f32[2,256,256]{2,1,0:T(8,128)}, f32[8,128]{1,0:T(8,128)}) custom-call(s32[13]{0:T(128)} %pad_add_fusion.meta_ref, f32[2,392,896]{2,1,0:T(8,128)} %select_maximum_fusion.window_ref, bf16[6,256,256]{2,1,0:T(8,128)(2,1)} %bitcast.60, f32[2,256,256]{2,1,0:T(8,128)} %probe_ref.1, ...), custom_call_target="tpu_custom_call" | custom-call | tf_op jit(solution)/shard_map/pallas_call | solution.py:251
  68.3 3.0 %collective-permute-start.17 = (f32[2,1,2,1,2,1,32,512]{7,6,5,4,3,2,1,0:T(8,128)}, f32[2,1,2,1,2,1,32,512]{7,6,5,4,3,2,1,0:T(8,128)}, u32[]{:S(2)}, u32[]{:S(2)}) collective-permute-start(f32[2,1,2,1,2,1,32,512]{7,6,5,4,3,2,1,0:T(8,128)} %constant_dynamic-slice_fusion.3), channel_id=1, source_target_pairs={{0,16},{4,20},{8,24},{12,28},{16,0},{20,4},{24,8},{28,12},{32,48},... | collective-permute-start | bytes 1572872 | tf_op jit(solution)/shard_map/ppermute | solution.py:119
  83.2 5.8 %collective-permute-start.18 = (f32[1,1,2,1,2,1,32,512]{7,6,5,4,3,2,1,0:T(8,128)S(1)}, f32[1,1,2,1,2,1,32,512]{7,6,5,4,3,2,1,0:T(8,128)S(1)}, u32[]{:S(2)}, u32[]{:S(2)}) collective-permute-start(f32[1,1,2,1,2,1,32,512]{7,6,5,4,3,2,1,0:T(8,128)S(1)} %constant_dynamic-slice_fusion.2), channel_id=1, source_target_pairs={{0,128},{64,192},{128,0},{192,64},{1,129},{65,193},{129,1},{193,65... | collective-permute-start | bytes 786440 | tf_op jit(solution)/shard_map/ppermute | solution.py:119
  89.4 4.4 %collective-permute-done.18 = f32[1,1,2,1,2,1,32,512]{7,6,5,4,3,2,1,0:T(8,128)S(1)} collective-permute-done((f32[1,1,2,1,2,1,32,512]{7,6,5,4,3,2,1,0:T(8,128)S(1)}, f32[1,1,2,1,2,1,32,512]{7,6,5,4,3,2,1,0:T(8,128)S(1)}, u32[]{:S(2)}, u32[]{:S(2)}) %collective-permute-start.18) | collective-permute-done | bytes 262176 | tf_op jit(solution)/shard_map/ppermute | solution.py:119
  99.5 13.0 %all-to-all-start = ((f32[64,1,256]{2,1,0:T(1,128)}), f32[64,1,256]{2,1,0:T(1,128)S(1)}, u32[]{:S(2)}, u32[]{:S(2)}) async-start(f32[64,1,256]{2,1,0:T(1,128)} %reshape.175), calls=%async_computation | async-start | bytes 131072 | tf_op jit(solution)/shard_map/all_to_all | solution.py:338
  114.1 5.3 %collective-permute-start.20 = (f32[1,1,1,1,1,1,32,512]{7,6,5,4,3,2,1,0:T(8,128)}, f32[1,1,1,1,1,1,32,512]{7,6,5,4,3,2,1,0:T(8,128)}, u32[]{:S(2)}, u32[]{:S(2)}) collective-permute-start(f32[1,1,1,1,1,1,32,512]{7,6,5,4,3,2,1,0:T(8,128)} %constant_dynamic-slice_fusion), channel_id=1, source_target_pairs={{0,8},{4,12},{8,0},{12,4},{16,24},{20,28},{24,16},{28,20},{32,40},... | collective-permute-start | bytes 196616 | tf_op jit(solution)/shard_map/ppermute | solution.py:119
  128.5 9.8 %all-to-all-start.1 = ((bf16[64,32,512]{2,1,0:T(8,128)(2,1)}), bf16[64,32,512]{2,1,0:T(8,128)(2,1)}, u32[]{:S(2)}, u32[]{:S(2)}) async-start(bf16[64,32,512]{2,1,0:T(8,128)(2,1)} %broadcast_in_dim.11), calls=%async_computation.1 | async-start | bytes 4194304 | tf_op jit(solution)/shard_map/all_to_all | solution.py:364
  149.7 9.8 %collective-permute-done.5 = f32[258,128]{1,0:T(8,128)} collective-permute-done((f32[258,128]{1,0:T(8,128)S(1)}, f32[258,128]{1,0:T(8,128)}, u32[]{:S(2)}, u32[]{:S(2)}) %collective-permute-start.5) | collective-permute-done | bytes 132128 | tf_op jit(solution)/shard_map/ppermute | solution.py:119
  160.6 25.7 %collective-permute-done.6 = f32[129,128]{1,0:T(8,128)S(1)} collective-permute-done((f32[129,128]{1,0:T(8,128)S(1)}, f32[129,128]{1,0:T(8,128)S(1)}, u32[]{:S(2)}, u32[]{:S(2)}) %collective-permute-start.6) | collective-permute-done | bytes 66080 | tf_op jit(solution)/shard_map/ppermute | solution.py:119
  189.6 2.9 %collective-permute-start.8 = (f32[129,128]{1,0:T(8,128)S(1)}, f32[129,128]{1,0:T(8,128)S(1)}, u32[]{:S(2)}, u32[]{:S(2)}) collective-permute-start(f32[129,128]{1,0:T(8,128)S(1)} %add.191), channel_id=1, source_target_pairs={{0,128},{64,192},{128,0},{192,64},{1,129},{65,193},{129,1},{193,65... | collective-permute-start | bytes 198152 | tf_op jit(solution)/shard_map/ppermute | solution.py:119
  194.6 3.9 %collective-permute-done.9 = f32[129,128]{1,0:T(8,128)S(1)} collective-permute-done((f32[129,128]{1,0:T(8,128)S(1)}, f32[129,128]{1,0:T(8,128)S(1)}, u32[]{:S(2)}, u32[]{:S(2)}) %collective-permute-start.9) | collective-permute-done | bytes 66080 | tf_op jit(solution)/shard_map/ppermute | solution.py:119
  198.5 3.3 %collective-permute-start.10 = (f32[129,128]{1,0:T(8,128)S(1)}, f32[129,128]{1,0:T(8,128)S(1)}, u32[]{:S(2)}, u32[]{:S(2)}) collective-permute-start(f32[129,128]{1,0:T(8,128)S(1)} %add.193), channel_id=1, source_target_pairs={{0,32},{4,36},{8,40},{12,44},{16,48},{20,52},{24,56},{28,60},{32,0... | collective-permute-start | bytes 198152 | tf_op jit(solution)/shard_map/ppermute | solution.py:119
  203.5 5.0 %collective-permute-start.11 = (f32[129,128]{1,0:T(8,128)S(1)}, f32[129,128]{1,0:T(8,128)S(1)}, u32[]{:S(2)}, u32[]{:S(2)}) collective-permute-start(f32[129,128]{1,0:T(8,128)S(1)} %add.194), channel_id=1, source_target_pairs={{0,8},{4,12},{8,0},{12,4},{16,24},{20,28},{24,16},{28,20},{32,40},... | collective-permute-start | bytes 198152 | tf_op jit(solution)/shard_map/ppermute | solution.py:119
  219.5 9.5 %collective-permute-start.14 = (f32[516,128]{1,0:T(8,128)S(1)}, f32[516,128]{1,0:T(8,128)}, u32[]{:S(2)}, u32[]{:S(2)}) collective-permute-start(f32[516,128]{1,0:T(8,128)S(1)} %maximum_select_fusion.1), channel_id=1, source_target_pairs={{0,4},{4,0},{8,12},{12,8},{16,20},{20,16},{24,28},{28,24},{32,36},... | collective-permute-start | bytes 792584 | tf_op jit(solution)/shard_map/ppermute | solution.py:119
  237.3 3.9 %convolution_bitcast_fusion.2 = f32[512,512]{0,1:T(8,128)} fusion(bf16[2048,512]{1,0:T(8,128)(2,1)} %bitcast.19, bf16[512,2048]{1,0:T(8,128)(2,1)S(1)} %bitcast.52), kind=kOutput, calls=%fused_computation.10 | convolution fusion | flops 1073741824 | bytes 5242880 | tf_op jit(solution)/shard_map/dot_general | solution.py:34
  241.2 3.8 %reshape.173 = f32[16,32,64,8]{1,0,3,2:T(8,128)} reshape(f32[512,512]{0,1:T(8,128)} %convolution_bitcast_fusion.2) | data formatting | bytes 2097152 | tf_op jit(solution)/shard_map/reshape | solution.py:367
  245.0 3.3 %multiply_reduce_fusion = f32[32,64,8]{0,2,1:T(8,128)S(1)} fusion(f32[16,32,64,8]{1,0,3,2:T(8,128)} %reshape.173, f32[16,64]{0,1:T(8,128)S(1)} %copy-done.11), kind=kLoop, calls=%fused_computation | loop fusion | flops 507904 | bytes 1118208 | tf_op jit(solution)/shard_map/reduce_sum | solution.py:368
  248.3 3.2 %convolution_subtract_fusion = f32[8,32,2048]{2,1,0:T(8,128)} fusion(f32[8,32,2048]{2,1,0:T(8,128)S(1)} %copy-done.5, f32[64,2048,1]{1,0,2:T(8,128)S(1)} %convolution_bitcast_fusion.1, f32[64,8,32]{2,1,0:T(8,128)S(1)} %bitcast.57), kind=kOutput, calls=%fused_computation.6 | convolution fusion | flops 403177472 | bytes 4784128 | tf_op jit(solution)/shard_map/azx,ay->zxy/dot_general | solution.py:369
  (122 shorter events, 101.4 us)
Async XLA Ops:
  23.9 8.7 %collective-permute-start.15 = (f32[2,2,2,2,2,1,32,512]{7,6,5,4,3,2,1,0:T(8,128)}, f32[2,2,2,2,2,1,32,512]{7,6,5,4,3,2,1,0:T(8,128)}, u32[]{:S(2)}, u32[]{:S(2)}) collective-permute-start(f32[2,2,2,2,2,1,32,512]{7,6,5,4,3,2,1,0:T(8,128)} %constant_dynamic-slice_fusion.5), channel_id=1, source_target_pairs={{0,4},{4,0},{8,12},{12,8},{16,20},{20,16},{24,28},{28,24},{32,36},... | collective-permute-start | bytes 6291464 | tf_op jit(solution)/shard_map/ppermute | solution.py:119
  28.1 15.5 %collective-permute-start = (f32[2,384,128]{2,1,0:T(8,128)}, f32[2,384,128]{2,1,0:T(8,128)S(1)}, u32[]{:S(2)}, u32[]{:S(2)}) collective-permute-start(f32[2,384,128]{2,1,0:T(8,128)} %get-tuple-element.35), channel_id=1, source_target_pairs={{0,64},{64,128},{128,192},{1,65},{65,129},{129,193},{2,66},{66,130... | collective-permute-start | bytes 1179656 | tf_op jit(solution)/shard_map/ppermute | solution.py:19
  29.6 14.0 %collective-permute-start.1 = (f32[2,384,128]{2,1,0:T(8,128)}, f32[2,384,128]{2,1,0:T(8,128)}, u32[]{:S(2)}, u32[]{:S(2)}) collective-permute-start(f32[2,384,128]{2,1,0:T(8,128)} %get-tuple-element.36), channel_id=1, source_target_pairs={{64,0},{128,64},{192,128},{65,1},{129,65},{193,129},{66,2},{130,66... | collective-permute-start | bytes 1179656 | tf_op jit(solution)/shard_map/ppermute | solution.py:19
  37.7 26.9 %collective-permute-start.16 = (f32[2,1,2,2,2,1,32,512]{7,6,5,4,3,2,1,0:T(8,128)}, f32[2,1,2,2,2,1,32,512]{7,6,5,4,3,2,1,0:T(8,128)}, u32[]{:S(2)}, u32[]{:S(2)}) collective-permute-start(f32[2,1,2,2,2,1,32,512]{7,6,5,4,3,2,1,0:T(8,128)} %constant_dynamic-slice_fusion.4), channel_id=1, source_target_pairs={{0,64},{64,0},{128,192},{192,128},{1,65},{65,1},{129,193},{193,129... | collective-permute-start | bytes 3145736 | tf_op jit(solution)/shard_map/ppermute | solution.py:119
  58.0 16.3 %collective-permute-start.2 = (f32[2,384,128]{2,1,0:T(8,128)}, f32[2,384,128]{2,1,0:T(8,128)}, u32[]{:S(2)}, u32[]{:S(2)}) collective-permute-start(f32[2,384,128]{2,1,0:T(8,128)} %get-tuple-element.34), channel_id=1, source_target_pairs={{0,64},{64,128},{128,192},{1,65},{65,129},{129,193},{2,66},{66,130... | collective-permute-start | bytes 1179656 | tf_op jit(solution)/shard_map/ppermute | solution.py:19
  60.6 17.4 %collective-permute-start.3 = (f32[2,384,128]{2,1,0:T(8,128)S(1)}, f32[2,384,128]{2,1,0:T(8,128)}, u32[]{:S(2)}, u32[]{:S(2)}) collective-permute-start(f32[2,384,128]{2,1,0:T(8,128)S(1)} %get-tuple-element.33), channel_id=1, source_target_pairs={{64,0},{128,64},{192,128},{65,1},{129,65},{193,129},{66,2},{130,66... | collective-permute-start | bytes 1179656 | tf_op jit(solution)/shard_map/ppermute | solution.py:19
  68.3 13.7 %collective-permute-start.17 = (f32[2,1,2,1,2,1,32,512]{7,6,5,4,3,2,1,0:T(8,128)}, f32[2,1,2,1,2,1,32,512]{7,6,5,4,3,2,1,0:T(8,128)}, u32[]{:S(2)}, u32[]{:S(2)}) collective-permute-start(f32[2,1,2,1,2,1,32,512]{7,6,5,4,3,2,1,0:T(8,128)} %constant_dynamic-slice_fusion.3), channel_id=1, source_target_pairs={{0,16},{4,20},{8,24},{12,28},{16,0},{20,4},{24,8},{28,12},{32,48},... | collective-permute-start | bytes 1572872 | tf_op jit(solution)/shard_map/ppermute | solution.py:119
  74.3 14.7 %copy-start.3 = (f32[1,2,384,512]{3,2,1,0:T(8,128)S(1)}, f32[1,2,384,512]{3,2,1,0:T(8,128)}, u32[]{:S(2)}) copy-start(f32[1,2,384,512]{3,2,1,0:T(8,128)} %param.15) | copy-start | bytes 4718596
  83.2 10.6 %collective-permute-start.18 = (f32[1,1,2,1,2,1,32,512]{7,6,5,4,3,2,1,0:T(8,128)S(1)}, f32[1,1,2,1,2,1,32,512]{7,6,5,4,3,2,1,0:T(8,128)S(1)}, u32[]{:S(2)}, u32[]{:S(2)}) collective-permute-start(f32[1,1,2,1,2,1,32,512]{7,6,5,4,3,2,1,0:T(8,128)S(1)} %constant_dynamic-slice_fusion.2), channel_id=1, source_target_pairs={{0,128},{64,192},{128,0},{192,64},{1,129},{65,193},{129,1},{193,65... | collective-permute-start | bytes 786440 | tf_op jit(solution)/shard_map/ppermute | solution.py:119
  94.6 17.9 %collective-permute-start.19 = (f32[1,1,1,1,2,1,32,512]{7,6,5,4,3,2,1,0:T(8,128)}, f32[1,1,1,1,2,1,32,512]{7,6,5,4,3,2,1,0:T(8,128)}, u32[]{:S(2)}, u32[]{:S(2)}) collective-permute-start(f32[1,1,1,1,2,1,32,512]{7,6,5,4,3,2,1,0:T(8,128)} %constant_dynamic-slice_fusion.1), channel_id=1, source_target_pairs={{0,32},{4,36},{8,40},{12,44},{16,48},{20,52},{24,56},{28,60},{32,0... | collective-permute-start | bytes 393224 | tf_op jit(solution)/shard_map/ppermute | solution.py:119
  99.5 22.8 %all-to-all-start = ((f32[64,1,256]{2,1,0:T(1,128)}), f32[64,1,256]{2,1,0:T(1,128)S(1)}, u32[]{:S(2)}, u32[]{:S(2)}) async-start(f32[64,1,256]{2,1,0:T(1,128)} %reshape.175), calls=%async_computation | async-start | bytes 131072 | tf_op jit(solution)/shard_map/all_to_all | solution.py:338
  114.1 11.9 %collective-permute-start.20 = (f32[1,1,1,1,1,1,32,512]{7,6,5,4,3,2,1,0:T(8,128)}, f32[1,1,1,1,1,1,32,512]{7,6,5,4,3,2,1,0:T(8,128)}, u32[]{:S(2)}, u32[]{:S(2)}) collective-permute-start(f32[1,1,1,1,1,1,32,512]{7,6,5,4,3,2,1,0:T(8,128)} %constant_dynamic-slice_fusion), channel_id=1, source_target_pairs={{0,8},{4,12},{8,0},{12,4},{16,24},{20,28},{24,16},{28,20},{32,40},... | collective-permute-start | bytes 196616 | tf_op jit(solution)/shard_map/ppermute | solution.py:119
  128.5 108.8 %all-to-all-start.1 = ((bf16[64,32,512]{2,1,0:T(8,128)(2,1)}), bf16[64,32,512]{2,1,0:T(8,128)(2,1)}, u32[]{:S(2)}, u32[]{:S(2)}) async-start(bf16[64,32,512]{2,1,0:T(8,128)(2,1)} %broadcast_in_dim.11), calls=%async_computation.1 | async-start | bytes 4194304 | tf_op jit(solution)/shard_map/all_to_all | solution.py:364
  145.4 1.9 collective-permute-start.4
  148.4 11.2 %collective-permute-start.5 = (f32[258,128]{1,0:T(8,128)S(1)}, f32[258,128]{1,0:T(8,128)}, u32[]{:S(2)}, u32[]{:S(2)}) collective-permute-start(f32[258,128]{1,0:T(8,128)S(1)} %constant_dynamic-slice_fusion.7), channel_id=1, source_target_pairs={{0,64},{64,0},{128,192},{192,128},{1,65},{65,1},{129,193},{193,129... | collective-permute-start | bytes 396296 | tf_op jit(solution)/shard_map/ppermute | solution.py:119
  160.5 25.8 %collective-permute-start.6 = (f32[129,128]{1,0:T(8,128)S(1)}, f32[129,128]{1,0:T(8,128)S(1)}, u32[]{:S(2)}, u32[]{:S(2)}) collective-permute-start(f32[129,128]{1,0:T(8,128)S(1)} %constant_dynamic-slice_fusion.6), channel_id=1, source_target_pairs={{0,1},{1,0},{2,3},{3,2},{4,5},{5,4},{6,7},{7,6},{8,9},{9,8},{10,11... | collective-permute-start | bytes 198152 | tf_op jit(solution)/shard_map/ppermute | solution.py:119
  186.3 3.2 %collective-permute-start.7 = (f32[129,128]{1,0:T(8,128)S(1)}, f32[129,128]{1,0:T(8,128)S(1)}, u32[]{:S(2)}, u32[]{:S(2)}) collective-permute-start(f32[129,128]{1,0:T(8,128)S(1)} %dynamic-slice_add_fusion.7), channel_id=1, source_target_pairs={{0,16},{4,20},{8,24},{12,28},{16,0},{20,4},{24,8},{28,12},{32,48},... | collective-permute-start | bytes 198152 | tf_op jit(solution)/shard_map/ppermute | solution.py:119
  189.6 4.8 %collective-permute-start.8 = (f32[129,128]{1,0:T(8,128)S(1)}, f32[129,128]{1,0:T(8,128)S(1)}, u32[]{:S(2)}, u32[]{:S(2)}) collective-permute-start(f32[129,128]{1,0:T(8,128)S(1)} %add.191), channel_id=1, source_target_pairs={{0,128},{64,192},{128,0},{192,64},{1,129},{65,193},{129,1},{193,65... | collective-permute-start | bytes 198152 | tf_op jit(solution)/shard_map/ppermute | solution.py:119
  194.3 4.1 %collective-permute-start.9 = (f32[129,128]{1,0:T(8,128)S(1)}, f32[129,128]{1,0:T(8,128)S(1)}, u32[]{:S(2)}, u32[]{:S(2)}) collective-permute-start(f32[129,128]{1,0:T(8,128)S(1)} %add.192), channel_id=1, source_target_pairs={{0,2},{1,3},{2,0},{3,1},{4,6},{5,7},{6,4},{7,5},{8,10},{9,11},{10,... | collective-permute-start | bytes 198152 | tf_op jit(solution)/shard_map/ppermute | solution.py:119
  198.5 5.0 %collective-permute-start.10 = (f32[129,128]{1,0:T(8,128)S(1)}, f32[129,128]{1,0:T(8,128)S(1)}, u32[]{:S(2)}, u32[]{:S(2)}) collective-permute-start(f32[129,128]{1,0:T(8,128)S(1)} %add.193), channel_id=1, source_target_pairs={{0,32},{4,36},{8,40},{12,44},{16,48},{20,52},{24,56},{28,60},{32,0... | collective-permute-start | bytes 198152 | tf_op jit(solution)/shard_map/ppermute | solution.py:119
  203.5 7.2 %collective-permute-start.11 = (f32[129,128]{1,0:T(8,128)S(1)}, f32[129,128]{1,0:T(8,128)S(1)}, u32[]{:S(2)}, u32[]{:S(2)}) collective-permute-start(f32[129,128]{1,0:T(8,128)S(1)} %add.194), channel_id=1, source_target_pairs={{0,8},{4,12},{8,0},{12,4},{16,24},{20,28},{24,16},{28,20},{32,40},... | collective-permute-start | bytes 198152 | tf_op jit(solution)/shard_map/ppermute | solution.py:119
  210.6 3.5 %collective-permute-start.12 = (f32[129,128]{1,0:T(8,128)S(1)}, f32[129,128]{1,0:T(8,128)S(1)}, u32[]{:S(2)}, u32[]{:S(2)}) collective-permute-start(f32[129,128]{1,0:T(8,128)S(1)} %add.195), channel_id=1, source_target_pairs={{0,1},{1,0},{2,3},{3,2},{4,5},{5,4},{6,7},{7,6},{8,9},{9,8},{10,11... | collective-permute-start | bytes 198152 | tf_op jit(solution)/shard_map/ppermute | solution.py:119
  214.2 4.3 %collective-permute-start.13 = (f32[258,128]{1,0:T(8,128)S(1)}, f32[258,128]{1,0:T(8,128)}, u32[]{:S(2)}, u32[]{:S(2)}) collective-permute-start(f32[258,128]{1,0:T(8,128)S(1)} %maximum_select_fusion.2), channel_id=1, source_target_pairs={{0,64},{64,0},{128,192},{192,128},{1,65},{65,1},{129,193},{193,129... | collective-permute-start | bytes 396296 | tf_op jit(solution)/shard_map/ppermute | solution.py:119
  219.5 10.8 %collective-permute-start.14 = (f32[516,128]{1,0:T(8,128)S(1)}, f32[516,128]{1,0:T(8,128)}, u32[]{:S(2)}, u32[]{:S(2)}) collective-permute-start(f32[516,128]{1,0:T(8,128)S(1)} %maximum_select_fusion.1), channel_id=1, source_target_pairs={{0,4},{4,0},{8,12},{12,8},{16,20},{20,16},{24,28},{28,24},{32,36},... | collective-permute-start | bytes 792584 | tf_op jit(solution)/shard_map/ppermute | solution.py:119
  (14 other events, 80.9 us)

commit v7 on v5

--- a/solution.py
+++ b/solution.py
@@ -343,9 +343,7 @@
     onehot = (angle_ids[:, None] == jnp.arange(angle_count, dtype=jnp.int32)[None, :]).astype(
         jnp.float32
     )
-    ray_table = jnp.dot(
-        onehot, ray_weights, precision=lax.Precision.HIGHEST, preferred_element_type=jnp.float32
-    )
+    ray_table = jnp.take(ray_weights, angle_ids, axis=0)
     ray_sums = jnp.einsum("zxy,ay->azx", volume, ray_table, precision=lax.Precision.HIGHEST).astype(
         jnp.bfloat16
     )

time: 227 us -> 230 us (1.013)
  starting transfers between devices: 72.2 us -> 77.1 us
  waiting for transfers between devices: 43.2 us -> 40.7 us
    all_to_all x1, starting transfers between devices: 12.4 us -> 16.8 us  [on_device(): arrived = lax.all_to_all(pieces, ('proj', 'cuts'), 0, 0, tiled=True)]
    ppermute x23, waiting for transfers between devices: 42.7 us -> 40.1 us  [exchange(): lax.ppermute(values, axis, [(source, source ^ 1 << bit) for source in ran...]
  transfers between devices with their start and end apart: 28 -> 28, of which waited for: 14 -> 15; matrix products, arithmetic and copies ran while one was open for 24% -> 23% of each run, Pallas kernels for 5% -> 5%
where the time goes in v7:
time: 230 us; the launch traced here: 232 us
  starting transfers between devices  77.1 us (34%)
  local copies, waits for them, and re-layouts  44.2 us (19%)
  other arithmetic  42.3 us (18%)
  waiting for transfers between devices  40.7 us (18%)
  matrix products  12.2 us (5%)
  Pallas kernels  12.2 us (5%)
  between operations  2.99 us (1%)
    ppermute x23, starting transfers between devices, exchange(): lax.ppermute(values, axis, [(source, source ^ 1 << bit) for source in ran...  54 us
    ppermute x23, waiting for transfers between devices, exchange(): lax.ppermute(values, axis, [(source, source ^ 1 << bit) for source in ran...  40.1 us
    all_to_all x1, starting transfers between devices, on_device(): arrived = lax.all_to_all(pieces, ('proj', 'cuts'), 0, 0, tiled=True)  16.8 us
    pallas_call x1, Pallas kernels, patch_terms_all(): pl.pallas_call(patch_kernel, grid_spec=grid_spec, out_shape=[jax.ShapeDty...  12.2 us
    add x5, other arithmetic, ordered_scatter(): values = keep + exchange(send, axis, bit)  6.91 us
    dynamic_slice x6, local copies, waits for them, and re-layouts, ordered_scatter(): send = lax.dynamic_slice_in_dim(values, 1 - mine, 1, place)  6.55 us
    ppermute x4, starting transfers between devices, shifted(): lax.ppermute(value, axis, [(source, source + steps) for source in range(l...  6.23 us
    select_n x6, other arithmetic, ordered_gather(): jnp.where(mine == 0, jnp.concatenate([values, other], axis=place), jnp.co...  5.84 us
  transfers between devices with their start and end apart: 28, of which 15 were waited for; matrix products, arithmetic and copies ran while one was open for 23% of the time, Pallas kernels for 5%

profile of v7, /device:TPU:1, one launch (start us, length us, event | category | flops | bytes accessed | tf_op | source)
XLA Modules:
  0.0 231.6 jit_solution(5718250243493648541)
XLA Ops:
  5.4 3.4 %fusion = bf16[32,64,8]{1,0,2:T(8,128)(2,1)S(1)} fusion(f32[8,32,2048]{2,1,0:T(8,128)} %param.22, f32[64,2048]{1,0:T(8,128)S(1)} %gather_fusion, pred[64]{0:T(512)(128)(4,1)S(1)} %compare_and_fusion), kind=kOutput, calls=%fused_computation.13 | convolution fusion | flops 402800640 | bytes 2654272 | tf_op jit(solution)/shard_map/zxy,ay->azx/dot_general | solution.py:347
  10.5 3.4 %mul.249 = bf16[512,512]{0,1:T(8,128)(2,1)S(1)} reshape(bf16[16,32,64,8]{1,0,3,2:T(8,128)(2,1)} %broadcast_multiply_fusion) | data formatting | bytes 1048576 | tf_op jit(solution)/shard_map/mul | solution.py:350
  13.9 3.3 %convolution_bitcast_fusion = f32[2048,512]{0,1:T(8,128)} fusion(bf16[512,512]{0,1:T(8,128)(2,1)S(1)} %mul.249, bf16[512,2048]{1,0:T(8,128)(2,1)S(1)} %bitcast.88), kind=kOutput, calls=%fused_computation.2 | convolution fusion | flops 1073741824 | bytes 6815744 | tf_op jit(solution)/shard_map/dot_general | solution.py:353
  17.2 5.3 %copy.60 = f32[2048,512]{1,0:T(8,128)} copy(f32[2048,512]{0,1:T(8,128)} %convolution_bitcast_fusion) | data formatting | bytes 8388608 | tf_op jit(solution)/shard_map/dot_general | solution.py:353
  22.5 3.3 %constant_dynamic-slice_fusion.5 = f32[2,2,2,2,2,1,32,512]{7,6,5,4,3,2,1,0:T(8,128)} fusion(f32[2,2,2,2,2,2,32,512]{7,6,5,4,3,2,1,0:T(8,128)} %bitcast.90, s32[]{:T(128)S(6)} %select_n.355), kind=kLoop, calls=%fused_computation.84 | loop fusion | bytes 4194308 | tf_op jit(solution)/shard_map/dynamic_slice | solution.py:98
  25.9 3.2 %collective-permute-start.15 = (f32[2,2,2,2,2,1,32,512]{7,6,5,4,3,2,1,0:T(8,128)}, f32[2,2,2,2,2,1,32,512]{7,6,5,4,3,2,1,0:T(8,128)}, u32[]{:S(2)}, u32[]{:S(2)}) collective-permute-start(f32[2,2,2,2,2,1,32,512]{7,6,5,4,3,2,1,0:T(8,128)} %constant_dynamic-slice_fusion.5), channel_id=1, source_target_pairs={{0,4},{4,0},{8,12},{12,8},{16,20},{20,16},{24,28},{28,24},{32,36},... | collective-permute-start | bytes 6291464 | tf_op jit(solution)/shard_map/ppermute | solution.py:119
  48.2 12.2 %shard_map.130 = (f32[2,392,896]{2,1,0:T(8,128)}, f32[2,256,256]{2,1,0:T(8,128)}, f32[8,128]{1,0:T(8,128)}) custom-call(s32[13]{0:T(128)} %pad_add_fusion.meta_ref, f32[2,392,896]{2,1,0:T(8,128)} %select_maximum_fusion.window_ref, bf16[6,256,256]{2,1,0:T(8,128)(2,1)} %bitcast.101, f32[2,256,256]{2,1,0:T(8,128)} %probe_ref.1, ...), custom_call_target="tpu_custom_call" | custom-call | tf_op jit(solution)/shard_map/pallas_call | solution.py:251
  88.5 3.0 %collective-permute-start.18 = (f32[1,1,2,1,2,1,32,512]{7,6,5,4,3,2,1,0:T(8,128)S(1)}, f32[1,1,2,1,2,1,32,512]{7,6,5,4,3,2,1,0:T(8,128)S(1)}, u32[]{:S(2)}, u32[]{:S(2)}) collective-permute-start(f32[1,1,2,1,2,1,32,512]{7,6,5,4,3,2,1,0:T(8,128)S(1)} %constant_dynamic-slice_fusion.2), channel_id=1, source_target_pairs={{0,128},{64,192},{128,0},{192,64},{1,129},{65,193},{129,1},{193,65... | collective-permute-start | bytes 786440 | tf_op jit(solution)/shard_map/ppermute | solution.py:119
  91.9 3.4 %collective-permute-done.18 = f32[1,1,2,1,2,1,32,512]{7,6,5,4,3,2,1,0:T(8,128)S(1)} collective-permute-done((f32[1,1,2,1,2,1,32,512]{7,6,5,4,3,2,1,0:T(8,128)S(1)}, f32[1,1,2,1,2,1,32,512]{7,6,5,4,3,2,1,0:T(8,128)S(1)}, u32[]{:S(2)}, u32[]{:S(2)}) %collective-permute-start.18) | collective-permute-done | bytes 262176 | tf_op jit(solution)/shard_map/ppermute | solution.py:119
  96.1 5.3 %collective-permute-start.19 = (f32[1,1,1,1,2,1,32,512]{7,6,5,4,3,2,1,0:T(8,128)}, f32[1,1,1,1,2,1,32,512]{7,6,5,4,3,2,1,0:T(8,128)}, u32[]{:S(2)}, u32[]{:S(2)}) collective-permute-start(f32[1,1,1,1,2,1,32,512]{7,6,5,4,3,2,1,0:T(8,128)} %constant_dynamic-slice_fusion.1), channel_id=1, source_target_pairs={{0,32},{4,36},{8,40},{12,44},{16,48},{20,52},{24,56},{28,60},{32,0... | collective-permute-start | bytes 393224 | tf_op jit(solution)/shard_map/ppermute | solution.py:119
  104.1 16.8 %all-to-all-start = ((f32[64,1,256]{2,1,0:T(1,128)}), f32[64,1,256]{2,1,0:T(1,128)S(1)}, u32[]{:S(2)}, u32[]{:S(2)}) async-start(f32[64,1,256]{2,1,0:T(1,128)} %reshape.1111), calls=%async_computation | async-start | bytes 131072 | tf_op jit(solution)/shard_map/all_to_all | solution.py:338
  122.5 5.3 %collective-permute-start.20 = (f32[1,1,1,1,1,1,32,512]{7,6,5,4,3,2,1,0:T(8,128)}, f32[1,1,1,1,1,1,32,512]{7,6,5,4,3,2,1,0:T(8,128)}, u32[]{:S(2)}, u32[]{:S(2)}) collective-permute-start(f32[1,1,1,1,1,1,32,512]{7,6,5,4,3,2,1,0:T(8,128)} %constant_dynamic-slice_fusion), channel_id=1, source_target_pairs={{0,8},{4,12},{8,0},{12,4},{16,24},{20,28},{24,16},{28,20},{32,40},... | collective-permute-start | bytes 196616 | tf_op jit(solution)/shard_map/ppermute | solution.py:119
  137.8 4.2 %collective-permute-done.21 = bf16[1,1,1,1,1,1,32,512]{7,6,5,4,3,2,1,0:T(8,128)(2,1)S(1)} collective-permute-done((bf16[1,1,1,1,1,1,32,512]{7,6,5,4,3,2,1,0:T(8,128)(2,1)S(1)}, bf16[1,1,1,1,1,1,32,512]{7,6,5,4,3,2,1,0:T(8,128)(2,1)S(1)}, u32[]{:S(2)}, u32[]{:S(2)}) %collective-permute-start.21) | collective-permute-done | bytes 32800 | tf_op jit(solution)/shard_map/ppermute | solution.py:119
  142.1 3.2 %collective-permute-start.22 = (bf16[1,1,1,1,2,1,32,512]{7,6,5,4,3,2,1,0:T(8,128)(2,1)S(1)}, bf16[1,1,1,1,2,1,32,512]{7,6,5,4,3,2,1,0:T(8,128)(2,1)S(1)}, u32[]{:S(2)}, u32[]{:S(2)}) collective-permute-start(bf16[1,1,1,1,2,1,32,512]{7,6,5,4,3,2,1,0:T(8,128)(2,1)S(1)} %maximum_select_fusion.10), channel_id=1, source_target_pairs={{0,32},{4,36},{8,40},{12,44},{16,48},{20,52},{24,56},{28,60},{32,0... | collective-permute-start | bytes 196616 | tf_op jit(solution)/shard_map/ppermute | solution.py:119
  147.0 3.3 %collective-permute-start.23 = (bf16[1,1,2,1,2,1,32,512]{7,6,5,4,3,2,1,0:T(8,128)(2,1)S(1)}, bf16[1,1,2,1,2,1,32,512]{7,6,5,4,3,2,1,0:T(8,128)(2,1)S(1)}, u32[]{:S(2)}, u32[]{:S(2)}) collective-permute-start(bf16[1,1,2,1,2,1,32,512]{7,6,5,4,3,2,1,0:T(8,128)(2,1)S(1)} %fusion.18), channel_id=1, source_target_pairs={{0,128},{64,192},{128,0},{192,64},{1,129},{65,193},{129,1},{193,65... | collective-permute-start | bytes 393224 | tf_op jit(solution)/shard_map/ppermute | solution.py:119
  166.0 4.3 %collective-permute-done.8 = f32[129,128]{1,0:T(8,128)S(1)} collective-permute-done((f32[129,128]{1,0:T(8,128)S(1)}, f32[129,128]{1,0:T(8,128)S(1)}, u32[]{:S(2)}, u32[]{:S(2)}) %collective-permute-start.8) | collective-permute-done | bytes 66080 | tf_op jit(solution)/shard_map/ppermute | solution.py:119
  170.8 4.4 %collective-permute-done.9 = f32[129,128]{1,0:T(8,128)S(1)} collective-permute-done((f32[129,128]{1,0:T(8,128)S(1)}, f32[129,128]{1,0:T(8,128)S(1)}, u32[]{:S(2)}, u32[]{:S(2)}) %collective-permute-start.9) | collective-permute-done | bytes 66080 | tf_op jit(solution)/shard_map/ppermute | solution.py:119
  175.2 3.1 %collective-permute-start.10 = (f32[129,128]{1,0:T(8,128)S(1)}, f32[129,128]{1,0:T(8,128)S(1)}, u32[]{:S(2)}, u32[]{:S(2)}) collective-permute-start(f32[129,128]{1,0:T(8,128)S(1)} %add.201), channel_id=1, source_target_pairs={{0,32},{4,36},{8,40},{12,44},{16,48},{20,52},{24,56},{28,60},{32,0... | collective-permute-start | bytes 198152 | tf_op jit(solution)/shard_map/ppermute | solution.py:119
  180.1 7.4 %collective-permute-done.11 = f32[129,128]{1,0:T(8,128)S(1)} collective-permute-done((f32[129,128]{1,0:T(8,128)S(1)}, f32[129,128]{1,0:T(8,128)S(1)}, u32[]{:S(2)}, u32[]{:S(2)}) %collective-permute-start.11) | collective-permute-done | bytes 66080 | tf_op jit(solution)/shard_map/ppermute | solution.py:119
  191.2 10.5 %collective-permute-start.26 = (bf16[2,2,2,2,2,1,32,512]{7,6,5,4,3,2,1,0:T(8,128)(2,1)}, bf16[2,2,2,2,2,1,32,512]{7,6,5,4,3,2,1,0:T(8,128)(2,1)}, u32[]{:S(2)}, u32[]{:S(2)}) collective-permute-start(bf16[2,2,2,2,2,1,32,512]{7,6,5,4,3,2,1,0:T(8,128)(2,1)} %maximum_select_fusion.1), channel_id=1, source_target_pairs={{0,4},{4,0},{8,12},{12,8},{16,20},{20,16},{24,28},{28,24},{32,36},... | collective-permute-start | bytes 3145736 | tf_op jit(solution)/shard_map/ppermute | solution.py:119
  202.2 4.6 %collective-permute-done.13 = f32[258,128]{1,0:T(8,128)S(1)} collective-permute-done((f32[258,128]{1,0:T(8,128)S(1)}, f32[258,128]{1,0:T(8,128)S(1)}, u32[]{:S(2)}, u32[]{:S(2)}) %collective-permute-start.13) | collective-permute-done | bytes 132128 | tf_op jit(solution)/shard_map/ppermute | solution.py:119
  221.3 3.8 %reshape.1100 = f32[16,32,64,8]{1,0,3,2:T(8,128)} reshape(f32[512,512]{0,1:T(8,128)} %convolution_bitcast_fusion.1) | data formatting | bytes 2097152 | tf_op jit(solution)/shard_map/reshape | solution.py:362
  225.1 3.3 %multiply_reduce_fusion = f32[32,64,8]{0,2,1:T(8,128)S(1)} fusion(f32[16,32,64,8]{1,0,3,2:T(8,128)} %reshape.1100, f32[16,64]{0,1:T(8,128)S(1)} %copy-done.11), kind=kLoop, calls=%fused_computation.1 | loop fusion | flops 507904 | bytes 1118208 | tf_op jit(solution)/shard_map/reduce_sum | solution.py:363
  228.4 3.2 %convolution_subtract_fusion = f32[8,32,2048]{2,1,0:T(8,128)} fusion(f32[8,32,2048]{2,1,0:T(8,128)S(1)} %copy-done.5, f32[64,2048]{1,0:T(8,128)S(1)} %gather_fusion, f32[64,8,32]{2,1,0:T(8,128)S(1)} %bitcast.97, pred[64]{0:T(512)(128)(4,1)S(1)} %compare_and_fusion), kind=kOutput, calls=%fused_computation.7 | convolution fusion | flops 403308544 | bytes 4784192 | tf_op jit(solution)/shard_map/azx,ay->zxy/dot_general | solution.py:364
  (144 shorter events, 105.3 us)
Async XLA Ops:
  25.9 8.7 %collective-permute-start.15 = (f32[2,2,2,2,2,1,32,512]{7,6,5,4,3,2,1,0:T(8,128)}, f32[2,2,2,2,2,1,32,512]{7,6,5,4,3,2,1,0:T(8,128)}, u32[]{:S(2)}, u32[]{:S(2)}) collective-permute-start(f32[2,2,2,2,2,1,32,512]{7,6,5,4,3,2,1,0:T(8,128)} %constant_dynamic-slice_fusion.5), channel_id=1, source_target_pairs={{0,4},{4,0},{8,12},{12,8},{16,20},{20,16},{24,28},{28,24},{32,36},... | collective-permute-start | bytes 6291464 | tf_op jit(solution)/shard_map/ppermute | solution.py:119
  30.0 15.4 %collective-permute-start = (f32[2,384,128]{2,1,0:T(8,128)}, f32[2,384,128]{2,1,0:T(8,128)S(1)}, u32[]{:S(2)}, u32[]{:S(2)}) collective-permute-start(f32[2,384,128]{2,1,0:T(8,128)} %get-tuple-element.35), channel_id=1, source_target_pairs={{0,64},{64,128},{128,192},{1,65},{65,129},{129,193},{2,66},{66,130... | collective-permute-start | bytes 1179656 | tf_op jit(solution)/shard_map/ppermute | solution.py:19
  31.5 13.9 %collective-permute-start.1 = (f32[2,384,128]{2,1,0:T(8,128)}, f32[2,384,128]{2,1,0:T(8,128)}, u32[]{:S(2)}, u32[]{:S(2)}) collective-permute-start(f32[2,384,128]{2,1,0:T(8,128)} %get-tuple-element.36), channel_id=1, source_target_pairs={{64,0},{128,64},{192,128},{65,1},{129,65},{193,129},{66,2},{130,66... | collective-permute-start | bytes 1179656 | tf_op jit(solution)/shard_map/ppermute | solution.py:19
  39.7 26.9 %collective-permute-start.16 = (f32[2,1,2,2,2,1,32,512]{7,6,5,4,3,2,1,0:T(8,128)}, f32[2,1,2,2,2,1,32,512]{7,6,5,4,3,2,1,0:T(8,128)}, u32[]{:S(2)}, u32[]{:S(2)}) collective-permute-start(f32[2,1,2,2,2,1,32,512]{7,6,5,4,3,2,1,0:T(8,128)} %constant_dynamic-slice_fusion.4), channel_id=1, source_target_pairs={{0,64},{64,0},{128,192},{192,128},{1,65},{65,1},{129,193},{193,129... | collective-permute-start | bytes 3145736 | tf_op jit(solution)/shard_map/ppermute | solution.py:119
  62.3 20.8 %collective-permute-start.2 = (f32[2,384,128]{2,1,0:T(8,128)}, f32[2,384,128]{2,1,0:T(8,128)}, u32[]{:S(2)}, u32[]{:S(2)}) collective-permute-start(f32[2,384,128]{2,1,0:T(8,128)} %get-tuple-element.34), channel_id=1, source_target_pairs={{0,64},{64,128},{128,192},{1,65},{65,129},{129,193},{2,66},{66,130... | collective-permute-start | bytes 1179656 | tf_op jit(solution)/shard_map/ppermute | solution.py:19
  64.4 20.7 %collective-permute-start.3 = (f32[2,384,128]{2,1,0:T(8,128)S(1)}, f32[2,384,128]{2,1,0:T(8,128)}, u32[]{:S(2)}, u32[]{:S(2)}) collective-permute-start(f32[2,384,128]{2,1,0:T(8,128)S(1)} %get-tuple-element.33), channel_id=1, source_target_pairs={{64,0},{128,64},{192,128},{65,1},{129,65},{193,129},{66,2},{130,66... | collective-permute-start | bytes 1179656 | tf_op jit(solution)/shard_map/ppermute | solution.py:19
  70.2 16.8 %collective-permute-start.17 = (f32[2,1,2,1,2,1,32,512]{7,6,5,4,3,2,1,0:T(8,128)}, f32[2,1,2,1,2,1,32,512]{7,6,5,4,3,2,1,0:T(8,128)}, u32[]{:S(2)}, u32[]{:S(2)}) collective-permute-start(f32[2,1,2,1,2,1,32,512]{7,6,5,4,3,2,1,0:T(8,128)} %constant_dynamic-slice_fusion.3), channel_id=1, source_target_pairs={{0,16},{4,20},{8,24},{12,28},{16,0},{20,4},{24,8},{28,12},{32,48},... | collective-permute-start | bytes 1572872 | tf_op jit(solution)/shard_map/ppermute | solution.py:119
  88.5 6.8 %collective-permute-start.18 = (f32[1,1,2,1,2,1,32,512]{7,6,5,4,3,2,1,0:T(8,128)S(1)}, f32[1,1,2,1,2,1,32,512]{7,6,5,4,3,2,1,0:T(8,128)S(1)}, u32[]{:S(2)}, u32[]{:S(2)}) collective-permute-start(f32[1,1,2,1,2,1,32,512]{7,6,5,4,3,2,1,0:T(8,128)S(1)} %constant_dynamic-slice_fusion.2), channel_id=1, source_target_pairs={{0,128},{64,192},{128,0},{192,64},{1,129},{65,193},{129,1},{193,65... | collective-permute-start | bytes 786440 | tf_op jit(solution)/shard_map/ppermute | solution.py:119
  96.1 24.8 %collective-permute-start.19 = (f32[1,1,1,1,2,1,32,512]{7,6,5,4,3,2,1,0:T(8,128)}, f32[1,1,1,1,2,1,32,512]{7,6,5,4,3,2,1,0:T(8,128)}, u32[]{:S(2)}, u32[]{:S(2)}) collective-permute-start(f32[1,1,1,1,2,1,32,512]{7,6,5,4,3,2,1,0:T(8,128)} %constant_dynamic-slice_fusion.1), channel_id=1, source_target_pairs={{0,32},{4,36},{8,40},{12,44},{16,48},{20,52},{24,56},{28,60},{32,0... | collective-permute-start | bytes 393224 | tf_op jit(solution)/shard_map/ppermute | solution.py:119
  104.1 26.6 %all-to-all-start = ((f32[64,1,256]{2,1,0:T(1,128)}), f32[64,1,256]{2,1,0:T(1,128)S(1)}, u32[]{:S(2)}, u32[]{:S(2)}) async-start(f32[64,1,256]{2,1,0:T(1,128)} %reshape.1111), calls=%async_computation | async-start | bytes 131072 | tf_op jit(solution)/shard_map/all_to_all | solution.py:338
  122.5 11.9 %collective-permute-start.20 = (f32[1,1,1,1,1,1,32,512]{7,6,5,4,3,2,1,0:T(8,128)}, f32[1,1,1,1,1,1,32,512]{7,6,5,4,3,2,1,0:T(8,128)}, u32[]{:S(2)}, u32[]{:S(2)}) collective-permute-start(f32[1,1,1,1,1,1,32,512]{7,6,5,4,3,2,1,0:T(8,128)} %constant_dynamic-slice_fusion), channel_id=1, source_target_pairs={{0,8},{4,12},{8,0},{12,4},{16,24},{20,28},{24,16},{28,20},{32,40},... | collective-permute-start | bytes 196616 | tf_op jit(solution)/shard_map/ppermute | solution.py:119
  129.5 7.3 %collective-permute-start.4 = (f32[516,128]{1,0:T(8,128)}, f32[516,128]{1,0:T(8,128)}, u32[]{:S(2)}, u32[]{:S(2)}) collective-permute-start(f32[516,128]{1,0:T(8,128)} %constant_dynamic-slice_fusion.8), channel_id=1, source_target_pairs={{0,4},{4,0},{8,12},{12,8},{16,20},{20,16},{24,28},{28,24},{32,36},... | collective-permute-start | bytes 792584 | tf_op jit(solution)/shard_map/ppermute | solution.py:119
  135.3 6.8 %collective-permute-start.21 = (bf16[1,1,1,1,1,1,32,512]{7,6,5,4,3,2,1,0:T(8,128)(2,1)S(1)}, bf16[1,1,1,1,1,1,32,512]{7,6,5,4,3,2,1,0:T(8,128)(2,1)S(1)}, u32[]{:S(2)}, u32[]{:S(2)}) collective-permute-start(bf16[1,1,1,1,1,1,32,512]{7,6,5,4,3,2,1,0:T(8,128)(2,1)S(1)} %subtract_convert_fusion), channel_id=1, source_target_pairs={{0,8},{4,12},{8,0},{12,4},{16,24},{20,28},{24,16},{28,20},{32,40},... | collective-permute-start | bytes 98312 | tf_op jit(solution)/shard_map/ppermute | solution.py:119
  142.1 4.9 %collective-permute-start.22 = (bf16[1,1,1,1,2,1,32,512]{7,6,5,4,3,2,1,0:T(8,128)(2,1)S(1)}, bf16[1,1,1,1,2,1,32,512]{7,6,5,4,3,2,1,0:T(8,128)(2,1)S(1)}, u32[]{:S(2)}, u32[]{:S(2)}) collective-permute-start(bf16[1,1,1,1,2,1,32,512]{7,6,5,4,3,2,1,0:T(8,128)(2,1)S(1)} %maximum_select_fusion.10), channel_id=1, source_target_pairs={{0,32},{4,36},{8,40},{12,44},{16,48},{20,52},{24,56},{28,60},{32,0... | collective-permute-start | bytes 196616 | tf_op jit(solution)/shard_map/ppermute | solution.py:119
  147.0 5.7 %collective-permute-start.23 = (bf16[1,1,2,1,2,1,32,512]{7,6,5,4,3,2,1,0:T(8,128)(2,1)S(1)}, bf16[1,1,2,1,2,1,32,512]{7,6,5,4,3,2,1,0:T(8,128)(2,1)S(1)}, u32[]{:S(2)}, u32[]{:S(2)}) collective-permute-start(bf16[1,1,2,1,2,1,32,512]{7,6,5,4,3,2,1,0:T(8,128)(2,1)S(1)} %fusion.18), channel_id=1, source_target_pairs={{0,128},{64,192},{128,0},{192,64},{1,129},{65,193},{129,1},{193,65... | collective-permute-start | bytes 393224 | tf_op jit(solution)/shard_map/ppermute | solution.py:119
  150.3 4.8 %collective-permute-start.5 = (f32[258,128]{1,0:T(8,128)S(1)}, f32[258,128]{1,0:T(8,128)S(1)}, u32[]{:S(2)}, u32[]{:S(2)}) collective-permute-start(f32[258,128]{1,0:T(8,128)S(1)} %constant_dynamic-slice_fusion.7), channel_id=1, source_target_pairs={{0,64},{64,0},{128,192},{192,128},{1,65},{65,1},{129,193},{193,129... | collective-permute-start | bytes 396296 | tf_op jit(solution)/shard_map/ppermute | solution.py:119
  152.7 5.4 %collective-permute-start.24 = (bf16[2,1,2,1,2,1,32,512]{7,6,5,4,3,2,1,0:T(8,128)(2,1)S(1)}, bf16[2,1,2,1,2,1,32,512]{7,6,5,4,3,2,1,0:T(8,128)(2,1)S(1)}, u32[]{:S(2)}, u32[]{:S(2)}) collective-permute-start(bf16[2,1,2,1,2,1,32,512]{7,6,5,4,3,2,1,0:T(8,128)(2,1)S(1)} %fusion.9), channel_id=1, source_target_pairs={{0,16},{4,20},{8,24},{12,28},{16,0},{20,4},{24,8},{28,12},{32,48},... | collective-permute-start | bytes 786440 | tf_op jit(solution)/shard_map/ppermute | solution.py:119
  158.9 29.9 %collective-permute-start.25 = (bf16[2,1,2,2,2,1,32,512]{7,6,5,4,3,2,1,0:T(8,128)(2,1)}, bf16[2,1,2,2,2,1,32,512]{7,6,5,4,3,2,1,0:T(8,128)(2,1)}, u32[]{:S(2)}, u32[]{:S(2)}) collective-permute-start(bf16[2,1,2,2,2,1,32,512]{7,6,5,4,3,2,1,0:T(8,128)(2,1)} %maximum_select_fusion.4), channel_id=1, source_target_pairs={{0,64},{64,0},{128,192},{192,128},{1,65},{65,1},{129,193},{193,129... | collective-permute-start | bytes 1572872 | tf_op jit(solution)/shard_map/ppermute | solution.py:119
  163.2 7.1 %collective-permute-start.8 = (f32[129,128]{1,0:T(8,128)S(1)}, f32[129,128]{1,0:T(8,128)S(1)}, u32[]{:S(2)}, u32[]{:S(2)}) collective-permute-start(f32[129,128]{1,0:T(8,128)S(1)} %add.199), channel_id=1, source_target_pairs={{0,128},{64,192},{128,0},{192,64},{1,129},{65,193},{129,1},{193,65... | collective-permute-start | bytes 198152 | tf_op jit(solution)/shard_map/ppermute | solution.py:119
  170.3 4.9 %collective-permute-start.9 = (f32[129,128]{1,0:T(8,128)S(1)}, f32[129,128]{1,0:T(8,128)S(1)}, u32[]{:S(2)}, u32[]{:S(2)}) collective-permute-start(f32[129,128]{1,0:T(8,128)S(1)} %add.200), channel_id=1, source_target_pairs={{0,2},{1,3},{2,0},{3,1},{4,6},{5,7},{6,4},{7,5},{8,10},{9,11},{10,... | collective-permute-start | bytes 198152 | tf_op jit(solution)/shard_map/ppermute | solution.py:119
  180.0 7.5 %collective-permute-start.11 = (f32[129,128]{1,0:T(8,128)S(1)}, f32[129,128]{1,0:T(8,128)S(1)}, u32[]{:S(2)}, u32[]{:S(2)}) collective-permute-start(f32[129,128]{1,0:T(8,128)S(1)} %add.202), channel_id=1, source_target_pairs={{0,8},{4,12},{8,0},{12,4},{16,24},{20,28},{24,16},{28,20},{32,40},... | collective-permute-start | bytes 198152 | tf_op jit(solution)/shard_map/ppermute | solution.py:119
  187.5 14.2 %collective-permute-start.12 = (f32[129,128]{1,0:T(8,128)S(1)}, f32[129,128]{1,0:T(8,128)S(1)}, u32[]{:S(2)}, u32[]{:S(2)}) collective-permute-start(f32[129,128]{1,0:T(8,128)S(1)} %add.203), channel_id=1, source_target_pairs={{0,1},{1,0},{2,3},{3,2},{4,5},{5,4},{6,7},{7,6},{8,9},{9,8},{10,11... | collective-permute-start | bytes 198152 | tf_op jit(solution)/shard_map/ppermute | solution.py:119
  191.2 25.3 %collective-permute-start.26 = (bf16[2,2,2,2,2,1,32,512]{7,6,5,4,3,2,1,0:T(8,128)(2,1)}, bf16[2,2,2,2,2,1,32,512]{7,6,5,4,3,2,1,0:T(8,128)(2,1)}, u32[]{:S(2)}, u32[]{:S(2)}) collective-permute-start(bf16[2,2,2,2,2,1,32,512]{7,6,5,4,3,2,1,0:T(8,128)(2,1)} %maximum_select_fusion.1), channel_id=1, source_target_pairs={{0,4},{4,0},{8,12},{12,8},{16,20},{20,16},{24,28},{28,24},{32,36},... | collective-permute-start | bytes 3145736 | tf_op jit(solution)/shard_map/ppermute | solution.py:119
  201.7 5.1 %collective-permute-start.13 = (f32[258,128]{1,0:T(8,128)S(1)}, f32[258,128]{1,0:T(8,128)S(1)}, u32[]{:S(2)}, u32[]{:S(2)}) collective-permute-start(f32[258,128]{1,0:T(8,128)S(1)} %maximum_select_fusion.7), channel_id=1, source_target_pairs={{0,64},{64,0},{128,192},{192,128},{1,65},{65,1},{129,193},{193,129... | collective-permute-start | bytes 396296 | tf_op jit(solution)/shard_map/ppermute | solution.py:119
  (19 other events, 103.9 us)
